TPU v7x, 32 devices: a whole 2x2x4 slice. The times are simulated.
32 devices in a mesh: dp: 8 (over y, x, core), seq: 4 (over z).
Axes of the slice: x: 2, y: 2, z: 4, core: 2. Of those that a mesh axis runs over, the one named last changes fastest.
Arguments:
- tokens: bfloat16 [16, 1024, 1024], P('dp', 'seq'), may hold values from -6 to 6
- w_qkv: bfloat16 [1024, 3072], P('dp'), may hold values from -0.1875 to 0.1875
- w_out: bfloat16 [1024, 1024], P('dp'), may hold values from -2 to 2
- w_up: bfloat16 [1024, 4096], P('dp'), may hold values from -0.1875 to 0.1875
- w_down: bfloat16 [4096, 1024], P(None, 'dp'), may hold values from -0.09375 to 0.09375
- b_query: bfloat16 [1024], P('dp'), may hold values from -4 to 4
- b_value: bfloat16 [1024], P('dp'), may hold values from -0.75 to 0.75
- b_out: bfloat16 [1024], P('dp'), may hold values from -4 to 4
- b_up: bfloat16 [4096], P('dp'), may hold values from -4 to 4
- b_down: bfloat16 [1024], P('dp'), may hold values from -4 to 4
- ln1_gain: bfloat16 [1024], P('dp'), may hold values from 0.5 to 1.5
- ln1_bias: bfloat16 [1024], P('dp'), may hold values from -4 to 4
- ln2_gain: bfloat16 [1024], P('dp'), may hold values from 0.5 to 1.5
- ln2_bias: bfloat16 [1024], P('dp'), may hold values from -4 to 4
- cotangent: bfloat16 [16, 1024, 1024], P('dp', 'seq'), may hold values from -6 to 6
Outputs:
- result: bfloat16 [16, 1024, 1024], P('dp', 'seq')
- grad_input: bfloat16 [16, 1024, 1024], P('dp', 'seq')
- grad_w_qkv: float32 [1024, 3072], P('dp')
- grad_w_out: float32 [1024, 1024], P('dp')
- grad_w_up: float32 [1024, 4096], P('dp')
- grad_w_down: float32 [4096, 1024], P(None, 'dp')
- grad_b_query: float32 [1024], P('dp')
- grad_b_value: float32 [1024], P('dp')
- grad_b_out: float32 [1024], P('dp')
- grad_b_up: float32 [4096], P('dp')
- grad_b_down: float32 [1024], P('dp')
- grad_ln1_gain: float32 [1024], P('dp')
- grad_ln1_bias: float32 [1024], P('dp')
- grad_ln2_gain: float32 [1024], P('dp')
- grad_ln2_bias: float32 [1024], P('dp')
All inputs are finite; a program needn't handle non-finite values.
Results may differ from a plain program's by a relative error of at most 0.02.
Values may be sent and summed in bfloat16 or wider, within the bound.
A program may use at most 192 MiB of HBM per device.

v0:
```python
import jax
import jax.numpy as jnp
from jax import lax
from jax.sharding import PartitionSpec as P

H = 16
DH = 64
MICRO = 2
IMG_MB = 1


norm_eps = 1e-06


def normalize(inputs, ln_gain, ln_offset):
    centre = jnp.mean(inputs, axis=-1, keepdims=True)
    spread = jnp.mean(jnp.square(inputs - centre), axis=-1, keepdims=True)
    return (inputs - centre) * lax.rsqrt(spread + norm_eps) * ln_gain + ln_offset


def activate(upward):
    return jax.nn.gelu(upward, approximate=True)


def add_pairs(first_set, second_set):
    return tuple(
        (first_item + second_item for first_item, second_item in zip(first_set, second_set))
    )


def forward_heads(queries, keyed, valued, factor):
    images, length, head_count, head_size = queries.shape
    block_rows = min(512, length)
    blocks = length // block_rows
    query_blocks = queries.reshape(images, blocks, block_rows, head_count, head_size)

    def forward_per_image(element):
        q_image, k_image, v_image = element

        def forward_per_block(q_block):
            scores = (
                jnp.einsum("qhd,khd->hqk", q_block, k_image, preferred_element_type=jnp.float32)
                * factor
            )
            row_max = jnp.max(scores, axis=-1, keepdims=True)
            exponent = jnp.exp(scores - row_max)
            row_total = jnp.sum(exponent, axis=-1, keepdims=True)
            attn_probs = (exponent / row_total).astype(jnp.bfloat16)
            mixture = jnp.einsum(
                "hqk,khd->qhd", attn_probs, v_image, preferred_element_type=jnp.float32
            )
            return (mixture, row_max[..., 0] + jnp.log(row_total[..., 0]))

        return lax.map(forward_per_block, q_image)

    mixture, log_total = lax.map(forward_per_image, (query_blocks, keyed, valued))
    return (mixture.reshape(images, length, head_count * head_size), log_total)


def backward_heads(queries, keyed, valued, grad_mixed, log_total, factor):
    images, length, head_count, head_size = queries.shape
    block_rows = min(512, length)
    blocks = length // block_rows
    query_blocks = queries.reshape(images, blocks, block_rows, head_count, head_size)
    grad_blocks = grad_mixed.reshape(images, blocks, block_rows, head_count, head_size)

    def backward_per_image(element):
        q_image, k_image, v_image, g_image, l_image = element

        def backward_per_block(running, pieces):
            grad_key, grad_value = running
            q_block, g_block, l_block = pieces
            scores = (
                jnp.einsum("qhd,khd->hqk", q_block, k_image, preferred_element_type=jnp.float32)
                * factor
            )
            full_probs = jnp.exp(scores - l_block[..., None])
            grad_probs = jnp.einsum(
                "qhd,khd->hqk", g_block, v_image, preferred_element_type=jnp.float32
            )
            row_inner = jnp.sum(full_probs * grad_probs, axis=-1, keepdims=True)
            grad_scores = (full_probs * (grad_probs - row_inner)).astype(jnp.bfloat16)
            grad_query = (
                jnp.einsum("hqk,khd->qhd", grad_scores, k_image, preferred_element_type=jnp.float32)
                * factor
            )
            grad_key = (
                grad_key
                + jnp.einsum(
                    "hqk,qhd->khd", grad_scores, q_block, preferred_element_type=jnp.float32
                )
                * factor
            )
            grad_value = grad_value + jnp.einsum(
                "hqk,qhd->khd",
                full_probs.astype(jnp.bfloat16),
                g_block,
                preferred_element_type=jnp.float32,
            )
            return ((grad_key, grad_value), grad_query)

        empty_sum = jnp.zeros((length, head_count, head_size), jnp.float32)
        (grad_key, grad_value), grad_query = lax.scan(
            backward_per_block, (empty_sum, empty_sum), (q_image, g_image, l_image)
        )
        return (grad_query.reshape(length, head_count, head_size), grad_key, grad_value)

    return lax.map(backward_per_image, (query_blocks, keyed, valued, grad_blocks, log_total))


def weight_grads(
    normed_one_low,
    grad_projected,
    mixed_tokens,
    grad_attn_low,
    normed_two_low,
    grad_upward_low,
    activated_low,
    grad_branch,
    model_width,
):
    grad_qkv = jnp.einsum(
        "ptd,pte->de", normed_one_low, grad_projected, preferred_element_type=jnp.float32
    )
    grad_bquery = jnp.sum(grad_projected[:, :, :model_width], axis=(0, 1), dtype=jnp.float32)
    grad_bvalue = jnp.sum(grad_projected[:, :, 2 * model_width :], axis=(0, 1), dtype=jnp.float32)
    grad_wout = jnp.einsum(
        "pte,ptd->ed", mixed_tokens, grad_attn_low, preferred_element_type=jnp.float32
    )
    grad_bout = jnp.sum(grad_attn_low, axis=(0, 1), dtype=jnp.float32)
    grad_up = jnp.einsum(
        "ptd,ptf->df", normed_two_low, grad_upward_low, preferred_element_type=jnp.float32
    )
    grad_bup = jnp.sum(grad_upward_low, axis=(0, 1), dtype=jnp.float32)
    grad_down = jnp.einsum(
        "ptf,ptd->fd", activated_low, grad_branch, preferred_element_type=jnp.float32
    )
    grad_bdown = jnp.sum(grad_branch, axis=(0, 1), dtype=jnp.float32)
    return (
        grad_qkv,
        grad_wout,
        grad_up,
        grad_down,
        grad_bquery,
        grad_bvalue,
        grad_bout,
        grad_bup,
        grad_bdown,
    )


def local(
    tokens,
    w_qkv,
    w_out,
    w_up,
    w_down,
    b_query,
    b_value,
    b_out,
    b_up,
    b_down,
    ln1_gain,
    ln1_bias,
    ln2_gain,
    ln2_bias,
    cotangent,
):
    seq_count = lax.axis_size("seq")
    local_patches = tokens.shape[1]
    model_width = tokens.shape[2]
    patches = local_patches * seq_count
    head_local = H // seq_count
    factor = DH ** (-0.5)
    gathered = (
        lax.all_gather(w_qkv, "dp", axis=0, tiled=True),
        lax.all_gather(w_out, "dp", axis=0, tiled=True),
        lax.all_gather(w_up, "dp", axis=0, tiled=True),
        lax.all_gather(w_down, "dp", axis=1, tiled=True),
        lax.all_gather(b_query, "dp", axis=0, tiled=True),
        lax.all_gather(b_value, "dp", axis=0, tiled=True),
        lax.all_gather(b_out, "dp", axis=0, tiled=True),
        lax.all_gather(b_up, "dp", axis=0, tiled=True),
        lax.all_gather(b_down, "dp", axis=0, tiled=True),
        lax.all_gather(ln1_gain, "dp", axis=0, tiled=True),
        lax.all_gather(ln1_bias, "dp", axis=0, tiled=True),
        lax.all_gather(ln2_gain, "dp", axis=0, tiled=True),
        lax.all_gather(ln2_bias, "dp", axis=0, tiled=True),
    )
    outputs = []
    grad_inputs = []
    kept = []
    for micro_idx in range(MICRO):
        w_qkv_full, w_out_full, w_up_full, w_down_full = (
            gathered[0],
            gathered[1],
            gathered[2],
            gathered[3],
        )
        vectors = [piece.astype(jnp.float32) for piece in gathered[4:]]
        (
            bias_query,
            bias_value,
            bias_out,
            bias_up,
            bias_down,
            gain_one,
            offset_one,
            gain_two,
            offset_two,
        ) = vectors
        start = micro_idx * IMG_MB
        inputs = tokens[start : start + IMG_MB].astype(jnp.float32)
        normed_one, norm_one_back = jax.vjp(normalize, inputs, gain_one, offset_one)
        normed_one_low = normed_one.astype(jnp.bfloat16)
        qkv_bias = jnp.concatenate([bias_query, jnp.zeros_like(bias_query), bias_value])
        projected = (
            jnp.einsum(
                "ptd,de->pte", normed_one_low, w_qkv_full, preferred_element_type=jnp.float32
            )
            + qkv_bias
        )
        projected_low = projected.astype(jnp.bfloat16).reshape(
            IMG_MB, local_patches, 3, model_width
        )
        by_heads = lax.all_to_all(projected_low, "seq", split_axis=3, concat_axis=1, tiled=True)
        queries = by_heads[:, :, 0].reshape(IMG_MB, patches, head_local, DH)
        keyed = by_heads[:, :, 1].reshape(IMG_MB, patches, head_local, DH)
        valued = by_heads[:, :, 2].reshape(IMG_MB, patches, head_local, DH)
        attended, log_total = forward_heads(queries, keyed, valued, factor)
        attended_low = attended.astype(jnp.bfloat16)
        mixed_tokens = lax.all_to_all(attended_low, "seq", split_axis=1, concat_axis=2, tiled=True)
        residual = (
            inputs
            + jnp.einsum(
                "pte,ed->ptd", mixed_tokens, w_out_full, preferred_element_type=jnp.float32
            )
            + bias_out
        )
        normed_two, norm_two_back = jax.vjp(normalize, residual, gain_two, offset_two)
        normed_two_low = normed_two.astype(jnp.bfloat16)
        upward = (
            jnp.einsum("ptd,df->ptf", normed_two_low, w_up_full, preferred_element_type=jnp.float32)
            + bias_up
        )
        activated, activate_back = jax.vjp(activate, upward)
        activated_low = activated.astype(jnp.bfloat16)
        layer_out = (
            residual
            + jnp.einsum(
                "ptf,fd->ptd", activated_low, w_down_full, preferred_element_type=jnp.float32
            )
            + bias_down
        )
        outputs.append(layer_out.astype(jnp.bfloat16))
        grad_result = cotangent[start : start + IMG_MB].astype(jnp.float32)
        grad_branch = grad_result.astype(jnp.bfloat16)
        grad_active = jnp.einsum(
            "ptd,fd->ptf", grad_branch, w_down_full, preferred_element_type=jnp.float32
        )
        (grad_upward,) = activate_back(grad_active)
        grad_upward_low = grad_upward.astype(jnp.bfloat16)
        grad_normed_two = jnp.einsum(
            "ptf,df->ptd", grad_upward_low, w_up_full, preferred_element_type=jnp.float32
        )
        grad_from_two, grad_gain2, grad_bias2 = norm_two_back(grad_normed_two)
        grad_residual = grad_result + grad_from_two
        grad_attn_low = grad_residual.astype(jnp.bfloat16)
        grad_mixed = jnp.einsum(
            "ptd,ed->pte", grad_attn_low, w_out_full, preferred_element_type=jnp.float32
        ).astype(jnp.bfloat16)
        grad_heads = lax.all_to_all(grad_mixed, "seq", split_axis=2, concat_axis=1, tiled=True)
        grad_query, grad_key, grad_value = backward_heads(
            queries,
            keyed,
            valued,
            grad_heads.reshape(IMG_MB, patches, head_local, DH),
            log_total,
            factor,
        )
        stacked = (
            jnp.stack([grad_query, grad_key, grad_value], axis=2)
            .reshape(IMG_MB, patches, 3, head_local * DH)
            .astype(jnp.bfloat16)
        )
        grad_parts = lax.all_to_all(stacked, "seq", split_axis=1, concat_axis=3, tiled=True)
        grad_projected = grad_parts.reshape(IMG_MB, local_patches, 3 * model_width)
        grad_normed_one = jnp.einsum(
            "pte,de->ptd", grad_projected, w_qkv_full, preferred_element_type=jnp.float32
        )
        grad_from_one, grad_gain1, grad_bias1 = norm_one_back(grad_normed_one)
        grad_inputs.append((grad_residual + grad_from_one).astype(jnp.bfloat16))
        norm_grads = (grad_gain1, grad_bias1, grad_gain2, grad_bias2)
        norm_total = norm_grads if micro_idx == 0 else add_pairs(norm_total, norm_grads)
        kept.append(
            (
                normed_one_low,
                grad_projected,
                mixed_tokens,
                grad_attn_low,
                normed_two_low,
                grad_upward_low,
                activated_low,
                grad_branch,
            )
        )
    joined = [jnp.concatenate([item[index] for item in kept], axis=0) for index in range(8)]
    big = weight_grads(
        joined[0],
        joined[1],
        joined[2],
        joined[3],
        joined[4],
        joined[5],
        joined[6],
        joined[7],
        model_width,
    )
    owned = (
        lax.psum_scatter(big[0].astype(jnp.bfloat16), "dp", scatter_dimension=0, tiled=True).astype(
            jnp.float32
        ),
        lax.psum_scatter(big[1].astype(jnp.bfloat16), "dp", scatter_dimension=0, tiled=True).astype(
            jnp.float32
        ),
        lax.psum_scatter(big[2].astype(jnp.bfloat16), "dp", scatter_dimension=0, tiled=True).astype(
            jnp.float32
        ),
        lax.psum_scatter(big[3].astype(jnp.bfloat16), "dp", scatter_dimension=1, tiled=True).astype(
            jnp.float32
        ),
        lax.psum_scatter(big[4].astype(jnp.bfloat16), "dp", scatter_dimension=0, tiled=True).astype(
            jnp.float32
        ),
        lax.psum_scatter(big[5].astype(jnp.bfloat16), "dp", scatter_dimension=0, tiled=True).astype(
            jnp.float32
        ),
        lax.psum_scatter(big[6].astype(jnp.bfloat16), "dp", scatter_dimension=0, tiled=True).astype(
            jnp.float32
        ),
        lax.psum_scatter(big[7].astype(jnp.bfloat16), "dp", scatter_dimension=0, tiled=True).astype(
            jnp.float32
        ),
        lax.psum_scatter(big[8].astype(jnp.bfloat16), "dp", scatter_dimension=0, tiled=True).astype(
            jnp.float32
        ),
        lax.psum_scatter(
            norm_total[0].astype(jnp.bfloat16), "dp", scatter_dimension=0, tiled=True
        ).astype(jnp.float32),
        lax.psum_scatter(
            norm_total[1].astype(jnp.bfloat16), "dp", scatter_dimension=0, tiled=True
        ).astype(jnp.float32),
        lax.psum_scatter(
            norm_total[2].astype(jnp.bfloat16), "dp", scatter_dimension=0, tiled=True
        ).astype(jnp.float32),
        lax.psum_scatter(
            norm_total[3].astype(jnp.bfloat16), "dp", scatter_dimension=0, tiled=True
        ).astype(jnp.float32),
    )
    owned = (
        lax.psum(owned[0].astype(jnp.bfloat16), "seq").astype(jnp.float32),
        lax.psum(owned[1].astype(jnp.bfloat16), "seq").astype(jnp.float32),
        lax.psum(owned[2].astype(jnp.bfloat16), "seq").astype(jnp.float32),
        lax.psum(owned[3].astype(jnp.bfloat16), "seq").astype(jnp.float32),
        lax.psum(owned[4].astype(jnp.bfloat16), "seq").astype(jnp.float32),
        lax.psum(owned[5].astype(jnp.bfloat16), "seq").astype(jnp.float32),
        lax.psum(owned[6].astype(jnp.bfloat16), "seq").astype(jnp.float32),
        lax.psum(owned[7].astype(jnp.bfloat16), "seq").astype(jnp.float32),
        lax.psum(owned[8].astype(jnp.bfloat16), "seq").astype(jnp.float32),
        lax.psum(owned[9].astype(jnp.bfloat16), "seq").astype(jnp.float32),
        lax.psum(owned[10].astype(jnp.bfloat16), "seq").astype(jnp.float32),
        lax.psum(owned[11].astype(jnp.bfloat16), "seq").astype(jnp.float32),
        lax.psum(owned[12].astype(jnp.bfloat16), "seq").astype(jnp.float32),
    )
    return (
        jnp.concatenate(outputs, axis=0),
        jnp.concatenate(grad_inputs, axis=0),
        owned[0],
        owned[1],
        owned[2],
        owned[3],
        owned[4],
        owned[5],
        owned[6],
        owned[7],
        owned[8],
        owned[9],
        owned[10],
        owned[11],
        owned[12],
    )


def solution(mesh):
    in_specs = (
        P("dp", "seq", None),
        P("dp", None),
        P("dp", None),
        P("dp", None),
        P(None, "dp"),
        P("dp"),
        P("dp"),
        P("dp"),
        P("dp"),
        P("dp"),
        P("dp"),
        P("dp"),
        P("dp"),
        P("dp"),
        P("dp", "seq", None),
    )
    out_specs = (
        P("dp", "seq", None),
        P("dp", "seq", None),
        P("dp", None),
        P("dp", None),
        P("dp", None),
        P(None, "dp"),
        P("dp"),
        P("dp"),
        P("dp"),
        P("dp"),
        P("dp"),
        P("dp"),
        P("dp"),
        P("dp"),
        P("dp"),
    )
    return jax.shard_map(local, mesh=mesh, in_specs=in_specs, out_specs=out_specs, check_vma=False)
```

profile of v0, /device:TPU:0, one launch (start us, length us, event | category | flops | bytes accessed | tf_op | source)
XLA Modules:
  0.0 808.3 jit_solution(17491299193227380128)
XLA Ops:
  9.4 10.4 %all-gather.2 = bf16[8,1,128]{2,1,0:T(2,128)(2,1)S(1)} all-gather(bf16[1,1,128]{2,1,0:T(2,128)(2,1)} %bitcast.454), channel_id=1, replica_groups=mesh['dp'=8,'seq'=4] {'dp'}, dimensions={0}, use_global_device_ids=true | all-gather | bytes 2304 | tf_op jit(solution)/shard_map/all_gather | solution.py:180
  19.8 8.8 %all-gather.3 = bf16[8,1,128]{2,1,0:T(2,128)(2,1)S(1)} all-gather(bf16[1,1,128]{2,1,0:T(2,128)(2,1)} %bitcast.455), channel_id=1, replica_groups=mesh['dp'=8,'seq'=4] {'dp'}, dimensions={0}, use_global_device_ids=true | all-gather | bytes 2304 | tf_op jit(solution)/shard_map/all_gather | solution.py:181
  28.6 8.1 all-gather
  36.7 8.9 %all-gather.1 = bf16[8,1,128]{2,1,0:T(2,128)(2,1)S(1)} all-gather(bf16[1,1,128]{2,1,0:T(2,128)(2,1)} %bitcast.457), channel_id=1, replica_groups=mesh['dp'=8,'seq'=4] {'dp'}, dimensions={0}, use_global_device_ids=true | all-gather | bytes 2304 | tf_op jit(solution)/shard_map/all_gather | solution.py:186
  50.5 7.6 all-gather.14.cloned.1.call-done
  58.1 4.6 fusion.98
  66.0 4.6 all-to-all-start
  71.2 5.7 fusion.99
  83.6 35.6 %all-to-all-done = bf16[1,256,3,1024]{1,2,0,3:T(4,128)(2,1)S(1)} async-done(((bf16[1,256,3,1024]{1,2,0,3:T(4,128)(2,1)}), bf16[1,256,3,1024]{1,2,0,3:T(4,128)(2,1)S(1)}, u32[]{:S(2)}, u32[]{:S(2)}) %all-to-all-start) | async-done | bytes 1572896 | tf_op jit(solution)/shard_map/all_to_all | solution.py:226
  119.2 4.6 all-to-all-start.2
  128.6 10.7 %while.94 = (s32[]{:T(128)}, bf16[2,512,4,64]{1,3,2,0:T(8,128)(2,1)S(1)}, f32[2,4,512]{2,1,0:T(4,128)S(1)}, bf16[2,512,4,64]{1,3,2,0:T(8,128)(2,1)S(1)}, bf16[10...) while((s32[]{:T(128)}, bf16[2,512,4,64]{1,3,2,0:T(8,128)(2,1)S(1)}, ...), condition=%wide.region_5.6_spmd, body=%wide.region_2.5_spmd.sunk | while | flops 555743232 | bytes 27066464 | solution.py:54
  150.6 21.1 %all-to-all-done.2 = bf16[1,256,3,1024]{1,2,0,3:T(4,128)(2,1)} async-done(((bf16[1,256,3,1024]{1,2,0,3:T(4,128)(2,1)}), bf16[1,256,3,1024]{1,2,0,3:T(4,128)(2,1)}, u32[]{:S(2)}, u32[]{:S(2)}) %all-to-all-start.2) | async-done | bytes 1572896 | tf_op jit(solution)/shard_map/all_to_all | solution.py:226
  182.2 10.8 %while.95 = (s32[]{:T(128)}, bf16[2,512,4,64]{1,3,2,0:T(8,128)(2,1)S(1)}, f32[2,4,512]{2,1,0:T(4,128)S(1)}, bf16[2,512,4,64]{1,3,2,0:T(8,128)(2,1)S(1)}, bf16[10...) while((s32[]{:T(128)}, bf16[2,512,4,64]{1,3,2,0:T(8,128)(2,1)S(1)}, ...), condition=%wide.region_13.14_spmd, body=%wide.region_10.13_spmd.sunk | while | flops 555743232 | bytes 27066464 | solution.py:54
  196.2 4.8 reduce.47
  201.9 5.1 all-to-all-start.3
  207.0 8.8 %all-gather.4 = bf16[8,1,128]{2,1,0:T(2,128)(2,1)S(1)} all-gather(bf16[1,1,128]{2,1,0:T(2,128)(2,1)S(1)} %bitcast.458), channel_id=1, replica_groups=mesh['dp'=8,'seq'=4] {'dp'}, dimensions={0}, use_global_device_ids=true | all-gather | bytes 2304 | tf_op jit(solution)/shard_map/all_gather | solution.py:182
  215.8 7.8 all-gather.5
  223.6 8.8 %all-gather.6 = bf16[8,1,128]{2,1,0:T(2,128)(2,1)S(1)} all-gather(bf16[1,1,128]{2,1,0:T(2,128)(2,1)S(1)} %bitcast.460), channel_id=1, replica_groups=mesh['dp'=8,'seq'=4] {'dp'}, dimensions={0}, use_global_device_ids=true | all-gather | bytes 2304 | tf_op jit(solution)/shard_map/all_gather | solution.py:188
  232.4 8.3 %all-gather.7 = bf16[8,1,512]{2,1,0:T(2,128)(2,1)S(1)} all-gather(bf16[1,1,512]{2,1,0:T(2,128)(2,1)S(1)} %reshape.726), channel_id=1, replica_groups=mesh['dp'=8,'seq'=4] {'dp'}, dimensions={0}, use_global_device_ids=true | all-gather | bytes 9216 | tf_op jit(solution)/shard_map/all_gather | solution.py:183
  261.4 6.1 convolution_add_fusion.1
  274.5 12.1 %fusion.200 = (bf16[4096]{0:T(1024)(128)(2,1)}, bf16[256,4096]{1,0:T(8,128)(2,1)S(1)}) fusion(f32[256,4096]{1,0:T(8,128)} %copy-done.32, bf16[4096,1024]{1,0:T(8,128)(2,1)} %all-gather.20.cloned.1.call-done, bf16[2,256,1024]{2,1,0:T(8,128)(2,1)S(1)} %copy-done.33), kind=kOutput, calls=%fused_computation.275 | convolution fusion | flops 2169499648 | bytes 15212544 | tf_op jit(solution)/shard_map/ptd,fd->ptf/dot_general | solution.py:258
  286.6 5.8 fusion.201
  307.6 4.6 reduce.49
  314.2 5.1 all-to-all-start.6
  325.0 4.6 reduce.50
  331.7 4.8 fusion.187
  336.5 5.1 all-to-all-start.4
  341.6 9.5 %bitcast_convert_fusion = bf16[4096,1024]{1,0:T(8,128)(2,1)} fusion(bf16[2,256,1024]{2,1,0:T(8,128)(2,1)S(1)} %copy-done.34, bf16[1,256,4096]{2,1,0:T(8,128)(2,1)} %fusion.187, bf16[1,256,4096]{2,1,0:T(8,128)(2,1)} %fusion.186), kind=kOutput, calls=%fused_computation.88 | convolution fusion | flops 4301258752 | bytes 13631488 | tf_op jit(solution)/shard_map/ptf,ptd->fd/dot_general | solution.py:135
  351.1 11.3 %copy.233 = bf16[4096,1024]{0,1:T(8,128)(2,1)} copy(bf16[4096,1024]{1,0:T(8,128)(2,1)} %bitcast_convert_fusion) | data formatting | bytes 16777216
  380.1 21.3 %while.96 = (s32[]{:T(128)}, f32[1024,4,64]{0,2,1:T(8,128)S(1)}, f32[1024,4,64]{0,2,1:T(8,128)S(1)}, bf16[2,512,4,64]{1,3,2,0:T(8,128)(2,1)}, bf16[2,512,4,64]{1...) while((s32[]{:T(128)}, f32[1024,4,64]{0,2,1:T(8,128)S(1)}, ...), condition=%wide.region_21.22_spmd.clone, body=%wide.region_19.21_spmd.clone.sunk | while | flops 1368782848 | bytes 78700808 | solution.py:103
  404.8 4.4 copy.210
  409.2 5.1 all-to-all-start.5
  415.2 21.3 %while.97 = (s32[]{:T(128)}, f32[1024,4,64]{0,2,1:T(8,128)S(1)}, f32[1024,4,64]{0,2,1:T(8,128)S(1)}, bf16[2,512,4,64]{1,3,2,0:T(8,128)(2,1)}, bf16[2,512,4,64]{1...) while((s32[]{:T(128)}, f32[1024,4,64]{0,2,1:T(8,128)S(1)}, ...), condition=%wide.region_30.31_spmd.clone, body=%wide.region_28.30_spmd.clone.sunk | while | flops 1368782848 | bytes 78700808 | solution.py:103
  441.4 20.5 %all-to-all-done.5 = bf16[1,1024,3,256]{3,2,0,1:T(4,128)(2,1)} async-done(((bf16[1,1024,3,256]{3,2,0,1:T(4,128)(2,1)}), bf16[1,1024,3,256]{3,2,0,1:T(4,128)(2,1)}, u32[]{:S(2)}, u32[]{:S(2)}) %all-to-all-start.5) | async-done | bytes 1572896 | tf_op jit(solution)/shard_map/all_to_all | solution.py:286
  461.9 4.4 all-to-all-start.7
  477.5 36.6 %all-to-all-done.7 = bf16[1,1024,3,256]{3,2,0,1:T(4,128)(2,1)} async-done(((bf16[1,1024,3,256]{3,2,0,1:T(4,128)(2,1)}), bf16[1,1024,3,256]{3,2,0,1:T(4,128)(2,1)}, u32[]{:S(2)}, u32[]{:S(2)}) %all-to-all-start.7) | async-done | bytes 1572896 | tf_op jit(solution)/shard_map/all_to_all | solution.py:286
  527.2 5.5 bitcast_convert_fusion.2
  534.0 9.0 %bitcast_convert_fusion.1 = bf16[1024,4096]{1,0:T(8,128)(2,1)} fusion(bf16[1,256,4096]{2,1,0:T(8,128)(2,1)} %bitcast.465, bf16[1,256,4096]{2,1,0:T(8,128)(2,1)} %bitcast.464, bf16[1,256,1024]{2,1,0:T(8,128)(2,1)S(1)} %copy-done.53, bf16[1,256,1024]{2,1,0:T(8,128)(2,1)S(1)} %copy-done.51), kind=kOutput, calls=%fused_computation.89 | convolution fusion | flops 4301783040 | bytes 13631488 | tf_op jit(solution)/shard_map/ptd,ptf->df/dot_general | solution.py:131
  547.0 9.1 %all-gather.8 = bf16[8,1,128]{2,1,0:T(2,128)(2,1)S(1)} all-gather(bf16[1,1,128]{2,1,0:T(2,128)(2,1)S(1)} %bitcast.461), channel_id=1, replica_groups=mesh['dp'=8,'seq'=4] {'dp'}, dimensions={0}, use_global_device_ids=true | all-gather | bytes 2304 | tf_op jit(solution)/shard_map/all_gather | solution.py:184
  556.2 7.5 fusion.115
  563.8 6.2 fusion.114
  575.3 5.2 fusion.203
  583.2 9.8 %reduce-scatter.7.cloned.1.call-done = bf16[128,3072]{1,0:T(8,128)(2,1)} async-done(((bf16[1024,3072]{1,0:T(8,128)(2,1)}), bf16[128,3072]{1,0:T(8,128)(2,1)}) %reduce-scatter.7.cloned.1.call-update) | async-done | bytes 786448 | tf_op jit(solution)/shard_map/reduce_scatter | solution.py:320
  593.0 75.0 %reduce-scatter.11.cloned.1.call-done = bf16[128,4096]{1,0:T(8,128)(2,1)} async-done(((bf16[1024,4096]{1,0:T(8,128)(2,1)}), bf16[128,4096]{1,0:T(8,128)(2,1)}) %reduce-scatter.11.cloned.1.call-update) | async-done | bytes 1048592 | tf_op jit(solution)/shard_map/reduce_scatter | solution.py:326
  670.0 5.6 fusion.137
  676.0 24.5 %all-reduce.9 = (bf16[1024]{0:T(1024)(128)(2,1)S(1)}, bf16[1024]{0:T(1024)(128)(2,1)S(1)}, bf16[1024]{0:T(1024)(128)(2,1)S(1)}, bf16[4096]{0:T(1024)(128)(2,1)S(...) all-reduce(bf16[1024]{0:T(1024)(128)(2,1)S(1)} %get-tuple-element.4, ...), channel_id=6, replica_groups=mesh['dp'=8,'seq'=4] {'dp'}, use_global_device_ids=true, to_apply=%region_43.44.clone | all-reduce | flops 12288 | bytes 49152
  701.2 12.7 %all-reduce.10 = (bf16[128]{0:T(256)(128)(2,1)S(1)}, bf16[128]{0:T(256)(128)(2,1)S(1)}, bf16[128]{0:T(256)(128)(2,1)S(1)}, bf16[512]{0:T(512)(128)(2,1)S(1)}, bf...) all-reduce(bf16[128]{0:T(256)(128)(2,1)S(1)} %dynamic-slice.3, ...), channel_id=1, replica_groups=mesh['dp'=8,'seq'=4] {'seq'}, use_global_device_ids=true, to_apply=%region_44.45 | all-reduce | flops 1536 | bytes 6144 | tf_op jit(solution)/shard_map/psum | solution.py:365
  722.4 70.4 %all-reduce.14.cloned.1.call-done = (bf16[128,3072]{1,0:T(8,128)(2,1)}, bf16[128,1024]{1,0:T(8,128)(2,1)}, bf16[128,4096]{1,0:T(8,128)(2,1)}, bf16[4096,128]{1,0:T(8,128)(2,1)}) async-done(((bf16[128,3072]{1,0:T(8,128)(2,1)}, bf16[128,1024]{1,0:T(8,128)(2,1)}, bf16[128,4096]{1,0:T(8,128)(2,1)}, bf16[4096,128]{1,0:T(8,128)(2,1)}), (bf16[128,3072]{1,0:T(8,128)(2,1)}, bf16[128,1024]{1,0:T(8,128)(2,1)}, ...) | async-done | bytes 3145744 | tf_op jit(solution)/shard_map/psum | solution.py:361
  (433 shorter events, 246.6 us)
Async XLA Ops:
  7.2 42.1 %copy-start.10 = (bf16[2,256,1024]{2,1,0:T(8,128)(2,1)S(1)}, bf16[2,256,1024]{2,1,0:T(8,128)(2,1)}, u32[]{:S(2)}) copy-start(bf16[2,256,1024]{2,1,0:T(8,128)(2,1)} %param.23) | copy-start | bytes 3145732
  7.2 50.9 %all-gather.14.cloned.1.call-start = ((), (), s32[]{:S(2)}) async-start(), calls=%async_computation.12 | async-start | bytes 7077888 | tf_op jit(solution)/shard_map/all_gather | solution.py:176
  7.9 248.2 %all-gather.16.cloned.1.call-start = ((), (), s32[]{:S(2)}) async-start(), calls=%async_computation.13 | async-start | bytes 2359296 | tf_op jit(solution)/shard_map/all_gather | solution.py:177
  8.7 252.7 %all-gather.18.cloned.1.call-start = ((), (), s32[]{:S(2)}) async-start(), calls=%async_computation.14 | async-start | bytes 9437184 | tf_op jit(solution)/shard_map/all_gather | solution.py:178
  66.0 53.2 %all-to-all-start = ((bf16[1,256,3,1024]{1,2,0,3:T(4,128)(2,1)}), bf16[1,256,3,1024]{1,2,0,3:T(4,128)(2,1)S(1)}, u32[]{:S(2)}, u32[]{:S(2)}) async-start(bf16[1,256,3,1024]{1,2,0,3:T(4,128)(2,1)} %copy.184), calls=%async_computation | async-start | bytes 4194304 | tf_op jit(solution)/shard_map/all_to_all | solution.py:226
  70.6 203.9 %all-gather.20.cloned.1.call-start = ((), (), s32[]{:S(2)}) async-start(), calls=%async_computation.15 | async-start | bytes 9437184 | tf_op jit(solution)/shard_map/all_gather | solution.py:179
  119.2 52.5 %all-to-all-start.2 = ((bf16[1,256,3,1024]{1,2,0,3:T(4,128)(2,1)}), bf16[1,256,3,1024]{1,2,0,3:T(4,128)(2,1)}, u32[]{:S(2)}, u32[]{:S(2)}) async-start(bf16[1,256,3,1024]{1,2,0,3:T(4,128)(2,1)} %copy.195), calls=%async_computation.2 | async-start | bytes 4194304 | tf_op jit(solution)/shard_map/all_to_all | solution.py:226
  139.4 38.6 %copy-start.2 = (bf16[1024,4,64]{0,2,1:T(8,128)(2,1)}, bf16[1024,4,64]{0,2,1:T(8,128)(2,1)S(1)}, u32[]{:S(2)}) copy-start(bf16[1024,4,64]{0,2,1:T(8,128)(2,1)S(1)} %get-tuple-element.969) | copy-start | bytes 1572868
  139.4 38.6 %copy-start.7 = (bf16[2,512,4,64]{1,3,2,0:T(8,128)(2,1)}, bf16[2,512,4,64]{1,3,2,0:T(8,128)(2,1)S(1)}, u32[]{:S(2)}) copy-start(bf16[2,512,4,64]{1,3,2,0:T(8,128)(2,1)S(1)} %get-tuple-element.971) | copy-start | bytes 1572868
  139.4 38.6 %copy-start.23 = (bf16[1024,4,64]{0,2,1:T(8,128)(2,1)}, bf16[1024,4,64]{0,2,1:T(8,128)(2,1)S(1)}, u32[]{:S(2)}) copy-start(bf16[1024,4,64]{0,2,1:T(8,128)(2,1)S(1)} %get-tuple-element.975) | copy-start | bytes 1572868
  171.7 30.2 %all-to-all-start.1 = ((bf16[4,2,32768]{2,1,0:T(2,128)(2,1)}), bf16[4,2,32768]{2,1,0:T(2,128)(2,1)}, u32[]{:S(2)}, u32[]{:S(2)}) async-start(bf16[4,2,32768]{2,1,0:T(2,128)(2,1)} %reshape.760), calls=%async_computation.1 | async-start | bytes 1048576 | tf_op jit(solution)/shard_map/all_to_all | solution.py:232
  193.6 13.4 %copy-start.5 = (bf16[2,512,4,64]{1,3,2,0:T(8,128)(2,1)}, bf16[2,512,4,64]{1,3,2,0:T(8,128)(2,1)S(1)}, u32[]{:S(2)}) copy-start(bf16[2,512,4,64]{1,3,2,0:T(8,128)(2,1)S(1)} %get-tuple-element.970) | copy-start | bytes 1572868
  193.6 13.4 %copy-start.21 = (bf16[1024,4,64]{0,2,1:T(8,128)(2,1)}, bf16[1024,4,64]{0,2,1:T(8,128)(2,1)S(1)}, u32[]{:S(2)}) copy-start(bf16[1024,4,64]{0,2,1:T(8,128)(2,1)S(1)} %get-tuple-element.974) | copy-start | bytes 1572868
  193.6 50.7 %copy-start = (bf16[1024,4,64]{0,2,1:T(8,128)(2,1)}, bf16[1024,4,64]{0,2,1:T(8,128)(2,1)S(1)}, u32[]{:S(2)}) copy-start(bf16[1024,4,64]{0,2,1:T(8,128)(2,1)S(1)} %get-tuple-element.968) | copy-start | bytes 1572868
  193.6 13.4 %copy-start.80 = (bf16[512]{0:T(512)(128)(2,1)S(1)}, bf16[512]{0:T(512)(128)(2,1)}, u32[]{:S(2)}) copy-start(bf16[512]{0:T(512)(128)(2,1)} %param.31) | copy-start | bytes 3076
  193.6 13.5 %copy-start.81 = (bf16[128]{0:T(256)(128)(2,1)S(1)}, bf16[128]{0:T(256)(128)(2,1)}, u32[]{:S(2)}) copy-start(bf16[128]{0:T(256)(128)(2,1)} %param.30) | copy-start | bytes 772
  193.6 22.3 %copy-start.82 = (bf16[128]{0:T(256)(128)(2,1)S(1)}, bf16[128]{0:T(256)(128)(2,1)}, u32[]{:S(2)}) copy-start(bf16[128]{0:T(256)(128)(2,1)} %param.35) | copy-start | bytes 772
  193.6 30.0 %copy-start.83 = (bf16[128]{0:T(256)(128)(2,1)S(1)}, bf16[128]{0:T(256)(128)(2,1)}, u32[]{:S(2)}) copy-start(bf16[128]{0:T(256)(128)(2,1)} %param.36) | copy-start | bytes 772
  201.9 46.6 %all-to-all-start.3 = ((bf16[4,2,32768]{2,1,0:T(2,128)(2,1)}), bf16[4,2,32768]{2,1,0:T(2,128)(2,1)}, u32[]{:S(2)}, u32[]{:S(2)}) async-start(bf16[4,2,32768]{2,1,0:T(2,128)(2,1)} %reshape.758), calls=%async_computation.3 | async-start | bytes 1048576 | tf_op jit(solution)/shard_map/all_to_all | solution.py:232
  274.5 17.9 %slice-start = ((s8[8388608]{0:T(1024)(128)(4,1)}), s8[4194304]{0:T(1024)(128)(4,1)S(1)}, s32[]{:S(2)}) async-start(s8[8388608]{0:T(1024)(128)(4,1)} %bitcast.462), calls=%async_computation.21 | async-start | bytes 8388608
  314.2 22.3 %all-to-all-start.6 = ((bf16[4,2,32768]{2,1,0:T(2,128)(2,1)}), bf16[4,2,32768]{2,1,0:T(2,128)(2,1)}, u32[]{:S(2)}, u32[]{:S(2)}) async-start(bf16[4,2,32768]{2,1,0:T(2,128)(2,1)} %reshape.762), calls=%async_computation.6 | async-start | bytes 1048576 | tf_op jit(solution)/shard_map/all_to_all | solution.py:272
  336.5 31.8 %all-to-all-start.4 = ((bf16[4,2,32768]{2,1,0:T(2,128)(2,1)}), bf16[4,2,32768]{2,1,0:T(2,128)(2,1)}, u32[]{:S(2)}, u32[]{:S(2)}) async-start(bf16[4,2,32768]{2,1,0:T(2,128)(2,1)} %reshape.764), calls=%async_computation.4 | async-start | bytes 1048576 | tf_op jit(solution)/shard_map/all_to_all | solution.py:272
  341.6 238.9 %reduce-scatter.13.cloned.1.call-start = ((), (), s32[]{:S(2)}) async-start(), calls=%async_computation.19 | async-start | bytes 9437184
  366.3 13.8 %copy-start.3 = (bf16[1024,4,64]{0,2,1:T(8,128)(2,1)S(1)}, bf16[1024,4,64]{0,2,1:T(8,128)(2,1)}, u32[]{:S(2)}) copy-start(bf16[1024,4,64]{0,2,1:T(8,128)(2,1)} %copy-done.2) | copy-start | bytes 1572868
  366.3 13.8 %copy-start.8 = (bf16[2,512,4,64]{1,3,2,0:T(8,128)(2,1)S(1)}, bf16[2,512,4,64]{1,3,2,0:T(8,128)(2,1)}, u32[]{:S(2)}) copy-start(bf16[2,512,4,64]{1,3,2,0:T(8,128)(2,1)} %copy-done.7) | copy-start | bytes 1572868
  366.3 13.8 %copy-start.55 = (f32[2,4,512]{2,1,0:T(4,128)S(1)}, f32[2,4,512]{2,1,0:T(4,128)}, u32[]{:S(2)}) copy-start(f32[2,4,512]{2,1,0:T(4,128)} %copy-done.54) | copy-start | bytes 49156
  409.2 52.7 %all-to-all-start.5 = ((bf16[1,1024,3,256]{3,2,0,1:T(4,128)(2,1)}), bf16[1,1024,3,256]{3,2,0,1:T(4,128)(2,1)}, u32[]{:S(2)}, u32[]{:S(2)}) async-start(bf16[1,1024,3,256]{3,2,0,1:T(4,128)(2,1)} %copy.210), calls=%async_computation.5 | async-start | bytes 4194304 | tf_op jit(solution)/shard_map/all_to_all | solution.py:286
  438.8 27.6 %copy-start.35 = (bf16[1,256,4,256]{1,3,2,0:T(8,128)(2,1)S(1)}, bf16[1,256,4,256]{1,3,2,0:T(8,128)(2,1)}, u32[]{:S(2)}) copy-start(bf16[1,256,4,256]{1,3,2,0:T(8,128)(2,1)} %copy.193) | copy-start | bytes 1572868
  438.8 27.6 %copy-start.37 = (bf16[1,256,4,256]{1,3,2,0:T(8,128)(2,1)S(1)}, bf16[1,256,4,256]{1,3,2,0:T(8,128)(2,1)}, u32[]{:S(2)}) copy-start(bf16[1,256,4,256]{1,3,2,0:T(8,128)(2,1)} %copy.204) | copy-start | bytes 1572868
  438.8 27.6 %copy-start.43 = (bf16[1,256,1024]{2,1,0:T(8,128)(2,1)S(1)}, bf16[1,256,1024]{2,1,0:T(8,128)(2,1)}, u32[]{:S(2)}) copy-start(bf16[1,256,1024]{2,1,0:T(8,128)(2,1)} %get-tuple-element.601) | copy-start | bytes 1572868
  441.4 25.0 %copy-start.45 = (bf16[1,256,1024]{2,1,0:T(8,128)(2,1)S(1)}, bf16[1,256,1024]{2,1,0:T(8,128)(2,1)}, u32[]{:S(2)}) copy-start(bf16[1,256,1024]{2,1,0:T(8,128)(2,1)} %copy-done.44) | copy-start | bytes 1572868
  461.9 52.3 %all-to-all-start.7 = ((bf16[1,1024,3,256]{3,2,0,1:T(4,128)(2,1)}), bf16[1,1024,3,256]{3,2,0,1:T(4,128)(2,1)}, u32[]{:S(2)}, u32[]{:S(2)}) async-start(bf16[1,1024,3,256]{3,2,0,1:T(4,128)(2,1)} %copy.218), calls=%async_computation.7 | async-start | bytes 4194304 | tf_op jit(solution)/shard_map/all_to_all | solution.py:286
  466.3 116.9 %reduce-scatter.9.cloned.1.call-start = ((), (), s32[]{:S(2)}) async-start(), calls=%async_computation.17 | async-start | bytes 2359296 | tf_op jit(solution)/shard_map/reduce_scatter | solution.py:323
  469.0 124.0 %reduce-scatter.7.cloned.1.call-start = ((), (), s32[]{:S(2)}) async-start(), calls=%async_computation.16 | async-start | bytes 7077888 | tf_op jit(solution)/shard_map/reduce_scatter | solution.py:320
  532.8 135.2 %reduce-scatter.11.cloned.1.call-start = ((), (), s32[]{:S(2)}) async-start(), calls=%async_computation.18 | async-start | bytes 9437184 | tf_op jit(solution)/shard_map/reduce_scatter | solution.py:326
  543.0 13.1 %copy-start.75 = (bf16[4096]{0:T(1024)(128)(2,1)S(1)}, bf16[4096]{0:T(1024)(128)(2,1)}, u32[]{:S(2)}) copy-start(bf16[4096]{0:T(1024)(128)(2,1)} %get-tuple-element.640) | copy-start | bytes 24580
  543.0 13.1 %copy-start.76 = (bf16[1024]{0:T(1024)(128)(2,1)S(1)}, bf16[1024]{0:T(1024)(128)(2,1)}, u32[]{:S(2)}) copy-start(bf16[1024]{0:T(1024)(128)(2,1)} %get-tuple-element.600) | copy-start | bytes 6148
  543.0 13.1 %copy-start.77 = (bf16[1024]{0:T(1024)(128)(2,1)S(1)}, bf16[1024]{0:T(1024)(128)(2,1)}, u32[]{:S(2)}) copy-start(bf16[1024]{0:T(1024)(128)(2,1)} %get-tuple-element.621) | copy-start | bytes 6148
  543.0 13.1 %copy-start.15 = (f32[1,256,1024]{2,1,0:T(8,128)S(1)}, f32[1,256,1024]{2,1,0:T(8,128)}, u32[]{:S(2)}) copy-start(f32[1,256,1024]{2,1,0:T(8,128)} %copy-done.13) | copy-start | bytes 3145732
  543.1 249.7 %all-reduce.14.cloned.1.call-start = ((), (), s32[]{:S(2)}) async-start(), calls=%async_computation.20 | async-start | bytes 6291456 | tf_op jit(solution)/shard_map/psum | solution.py:361
  580.4 89.5 %copy-start.12 = (bf16[2,256,1024]{2,1,0:T(8,128)(2,1)S(1)}, bf16[2,256,1024]{2,1,0:T(8,128)(2,1)}, u32[]{:S(2)}) copy-start(bf16[2,256,1024]{2,1,0:T(8,128)(2,1)} %param.23) | copy-start | bytes 3145732
  580.4 89.5 %copy-start.59 = (f32[8,1,128]{2,1,0:T(1,128)S(1)}, f32[8,1,128]{2,1,0:T(1,128)}, u32[]{:S(2)}) copy-start(f32[8,1,128]{2,1,0:T(1,128)} %copy-done.58) | copy-start | bytes 12292
  580.5 89.5 %copy-start.61 = (f32[256]{0:T(256)S(1)}, f32[256]{0:T(256)}, u32[]{:S(2)}) copy-start(f32[256]{0:T(256)} %copy-done.60) | copy-start | bytes 3076
  580.5 89.5 %copy-start.63 = (f32[256]{0:T(256)S(1)}, f32[256]{0:T(256)}, u32[]{:S(2)}) copy-start(f32[256]{0:T(256)} %copy-done.62) | copy-start | bytes 3076
  580.5 89.5 %copy-start.67 = (f32[256]{0:T(256)S(1)}, f32[256]{0:T(256)}, u32[]{:S(2)}) copy-start(f32[256]{0:T(256)} %copy-done.66) | copy-start | bytes 3076
  580.5 89.5 %copy-start.69 = (f32[256]{0:T(256)S(1)}, f32[256]{0:T(256)}, u32[]{:S(2)}) copy-start(f32[256]{0:T(256)} %copy-done.68) | copy-start | bytes 3076
  670.0 48.6 %copy-start.73 = (f32[256]{0:T(256)S(1)}, f32[256]{0:T(256)}, u32[]{:S(2)}) copy-start(f32[256]{0:T(256)} %copy-done.72) | copy-start | bytes 3076
  670.0 48.6 %copy-start.71 = (f32[256]{0:T(256)S(1)}, f32[256]{0:T(256)}, u32[]{:S(2)}) copy-start(f32[256]{0:T(256)} %copy-done.70) | copy-start | bytes 3076
  (69 other events, 312.7 us)
Sparse Core Ops, SparseCore 0:
  9.9 48.1 all-gather.13
  59.9 27.7 all-gather.15
  89.6 54.2 all-gather.17
  145.7 55.8 all-gather.19
  362.5 72.0 reduce-scatter.12
  470.7 41.7 reduce-scatter.8
  532.9 60.0 reduce-scatter.6
  596.5 71.4 reduce-scatter.10
  671.2 121.5 all-reduce.13
where the time goes:
time: 818 us; the launch traced here: 808 us
  waiting for transfers between devices  279 us (34%)
  matrix products  152 us (19%)
  local copies, waits for them, and re-layouts  131 us (16%)
  blocking collectives  116 us (14%)
  other arithmetic  73.6 us (9%)
  starting transfers between devices  38.7 us (5%)
  between operations  16.9 us (2%)
    reduce_scatter x1, waiting for transfers between devices, local(): lax.psum_scatter(big[2].astype(jnp.bfloat16), 'dp', scatter_dimension=0,...  75 us
    psum x1, waiting for transfers between devices, local(): lax.psum(owned[0].astype(jnp.bfloat16), 'seq').astype(jnp.float32)  70.4 us
    all_to_all x2, waiting for transfers between devices, local(): lax.all_to_all(stacked, 'seq', split_axis=1, concat_axis=3, tiled=True)  57.1 us
    all_to_all x2, waiting for transfers between devices, local(): lax.all_to_all(projected_low, 'seq', split_axis=3, concat_axis=1, tiled=T...  56.8 us
    unnamed x197, local copies, waits for them, and re-layouts  53.9 us
    unnamed x1, blocking collectives  24.5 us
    dot_general x2, matrix products, local(): jnp.einsum('ptd,fd->ptf', grad_branch, w_down_full, preferred_element_typ...  17.9 us
    unnamed x9, other arithmetic  17.8 us
  transfers between devices with their start and end apart: 17, of which 8 were waited for; matrix products, arithmetic and copies ran while one was open for 37% of the time, Pallas kernels for 0%

commit v1 on v0

--- a/solution.py
+++ b/solution.py
@@ -1,6 +1,10 @@
+import functools
+
 import jax
 import jax.numpy as jnp
 from jax import lax
+from jax.experimental import pallas as pl
+from jax.experimental.pallas import tpu as pltpu
 from jax.sharding import PartitionSpec as P
 
 H = 16
@@ -391,6 +395,208 @@
     )
 
 
+F32=jnp.float32; BF16=jnp.bfloat16
+NT=(((1,),(1,)),((),())); TN=(((0,),(0,)),((),())); NN=(((1,),(0,)),((),()))
+def dg(a,b,dims): return lax.dot_general(a,b,dims,preferred_element_type=F32)
+
+def attn_fwd_kernel(q_ref, ka_ref, kb_ref, va_ref, vb_ref, o_ref, l_ref):
+    rows=q_ref.shape[0]
+    lane=lax.broadcasted_iota(jnp.int32,(rows,128),1)
+    q=q_ref[...]*jnp.asarray(0.125,BF16)
+    outs=[]; ls=[]
+    for h in range(2):
+        qh=jnp.where((lane<64) if h==0 else (lane>=64), q, jnp.zeros_like(q))
+        sa=dg(ka_ref[...],qh,NT); sb=dg(kb_ref[...],qh,NT)
+        m=jnp.maximum(jnp.max(sa,axis=0,keepdims=True),jnp.max(sb,axis=0,keepdims=True))
+        pa=jnp.exp(sa-m); pb=jnp.exp(sb-m)
+        tot=jnp.sum(pa,axis=0,keepdims=True)+jnp.sum(pb,axis=0,keepdims=True)
+        oT=dg(va_ref[...],pa.astype(BF16),TN)+dg(vb_ref[...],pb.astype(BF16),TN)
+        outs.append(oT[64*h:64*h+64]*(1.0/tot))
+        ls.append(m+jnp.log(tot))
+    oT=jnp.concatenate(outs,axis=0)
+    o_ref[...]=oT.T.astype(BF16)
+    l_ref[0]=jnp.concatenate(ls+[jnp.zeros((6,rows),F32)],axis=0)
+
+def attn_fwd(q,ka,kb,va,vb):
+    rows,width=q.shape
+    spec=pl.BlockSpec((rows,128),lambda i:(0,i))
+    keys=ka.shape[0]
+    ks=pl.BlockSpec((keys,128),lambda i:(0,i))
+    return pl.pallas_call(attn_fwd_kernel,grid=(width//128,),
+        in_specs=[spec,ks,ks,ks,ks],
+        out_specs=[spec,pl.BlockSpec((1,8,rows),lambda i:(i,0,0))],
+        out_shape=[jax.ShapeDtypeStruct((rows,width),BF16),jax.ShapeDtypeStruct((width//128,8,rows),F32)],
+        compiler_params=pltpu.CompilerParams(vmem_limit_bytes=48<<20),name="attn_fwd",
+        cost_estimate=pl.CostEstimate(flops=4*rows*2*keys*width,bytes_accessed=12*rows*width,transcendentals=rows*2*keys*width//64))(q,ka,kb,va,vb)
+
+def attn_bwd_kernel(q_ref, ka_ref, kb_ref, va_ref, vb_ref, o_ref, do_ref, l_ref, dq_ref, dka_ref, dkb_ref, dva_ref, dvb_ref):
+    rows=q_ref.shape[0]
+    lane=lax.broadcasted_iota(jnp.int32,(rows,128),1)
+    q=q_ref[...]*jnp.asarray(0.125,BF16)
+    do=do_ref[...]
+    t=(do.astype(F32)*o_ref[...].astype(F32)).T
+    klane=lax.broadcasted_iota(jnp.int32,(ka_ref.shape[0],128),1)
+    dq=None; dk=[None,None]; dv=[None,None]
+    add=lambda a,b: b if a is None else a+b
+    for h in range(2):
+        sel=(lane<64) if h==0 else (lane>=64)
+        ksel=(klane<64) if h==0 else (klane>=64)
+        qh=jnp.where(sel,q,jnp.zeros_like(q)); doh=jnp.where(sel,do,jnp.zeros_like(do))
+        delta=jnp.sum(t[64*h:64*h+64],axis=0,keepdims=True)
+        lse=l_ref[0,h:h+1,:]
+        for n,(k_ref,v_ref) in enumerate(((ka_ref,va_ref),(kb_ref,vb_ref))):
+            s=dg(k_ref[...],qh,NT)
+            p=jnp.exp(s-lse)
+            dp=dg(v_ref[...],doh,NT)
+            ds=(p*(dp-delta)).astype(BF16)
+            dv[n]=add(dv[n],dg(p.astype(BF16),doh,NN))
+            dk[n]=add(dk[n],dg(ds,qh,NN))
+            kh=jnp.where(ksel,k_ref[...],jnp.zeros_like(k_ref[...]))
+            dq=add(dq,dg(kh,ds,TN))
+    dq_ref[...]=(dq*0.125).T.astype(BF16)
+    dka_ref[...]=dk[0].astype(BF16); dkb_ref[...]=dk[1].astype(BF16)
+    dva_ref[...]=dv[0].astype(BF16); dvb_ref[...]=dv[1].astype(BF16)
+
+def attn_bwd(q,ka,kb,va,vb,o,do,l):
+    rows,width=q.shape; keys=ka.shape[0]
+    spec=pl.BlockSpec((rows,128),lambda i:(0,i))
+    ks=pl.BlockSpec((keys,128),lambda i:(0,i))
+    sh=jax.ShapeDtypeStruct((rows,width),BF16); kh=jax.ShapeDtypeStruct((keys,width),BF16)
+    return pl.pallas_call(attn_bwd_kernel,grid=(width//128,),
+        in_specs=[spec,ks,ks,ks,ks,spec,spec,pl.BlockSpec((1,8,rows),lambda i:(i,0,0))],
+        out_specs=[spec,ks,ks,ks,ks],
+        out_shape=[sh,kh,kh,kh,kh],
+        compiler_params=pltpu.CompilerParams(vmem_limit_bytes=48<<20),name="attn_bwd",
+        cost_estimate=pl.CostEstimate(flops=10*rows*2*keys*width,bytes_accessed=26*rows*width,transcendentals=rows*2*keys*width//64))(q,ka,kb,va,vb,o,do,l)
+
+
+def image_moves(shift):
+    pairs = []
+    for p in range(4):
+        for c in range(2):
+            for z in range(4):
+                to_core, to_z = z // 2, 2 * c + (shift ^ (z & 1))
+                pairs.append(((2 * p + c) * 4 + z, (2 * p + to_core) * 4 + to_z))
+    return pairs
+
+
+def gather_image(blocks):
+    odd = lax.axis_index("seq") % 2
+    parts = []
+    for shift in range(2):
+        mine = lax.dynamic_index_in_dim(blocks, odd ^ shift, 0, keepdims=False)
+        parts.append(lax.ppermute(mine, ("dp", "seq"), image_moves(shift)))
+    rows = parts[0].shape[0]
+    swapped = jnp.where(odd == 0, jnp.stack(parts), jnp.stack(parts[::-1]))
+    return swapped.reshape(2 * rows, parts[0].shape[1])
+
+
+def return_image(rows_all):
+    odd = lax.axis_index("seq") % 2
+    halves = rows_all.reshape(2, rows_all.shape[0] // 2, rows_all.shape[1])
+    parts = []
+    for shift in range(2):
+        mine = lax.dynamic_index_in_dim(halves, odd ^ shift, 0, keepdims=False)
+        back = [(to, start) for start, to in image_moves(shift)]
+        parts.append(lax.ppermute(mine, ("dp", "seq"), back))
+    return jnp.where(odd == 0, jnp.stack(parts), jnp.stack(parts[::-1]))
+
+
+def other_core(value):
+    return lax.ppermute(value, "dp", [(i, i ^ 1) for i in range(lax.axis_size("dp"))])
+
+
+def dot_nn(left, right):
+    return dg(left, right, NN)
+
+
+def norm_parts(value):
+    centre = jnp.mean(value, axis=-1, keepdims=True)
+    spread = jnp.mean(jnp.square(value - centre), axis=-1, keepdims=True)
+    rstd = lax.rsqrt(spread + norm_eps)
+    return ((value - centre) * rstd, rstd)
+
+
+def norm_back(xhat, rstd, grad, gain):
+    e = grad * gain
+    return rstd * (
+        e - jnp.mean(e, axis=-1, keepdims=True) - xhat * jnp.mean(e * xhat, axis=-1, keepdims=True)
+    )
+
+
+def local_fast(
+    tokens, w_qkv, w_out, w_up, w_down, b_query, b_value, b_out, b_up, b_down,
+    ln1_gain, ln1_bias, ln2_gain, ln2_bias, cotangent,
+):
+    d = tokens.shape[2]
+    small = (b_query, b_value, b_out, b_up, b_down, ln1_gain, ln1_bias, ln2_gain, ln2_bias)
+    sizes = [item.shape[0] for item in small]
+    packed = lax.all_gather(jnp.concatenate(small), "dp", axis=0, tiled=False)
+    vectors, at = [], 0
+    for size in sizes:
+        vectors.append(packed[:, at : at + size].reshape(1, -1).astype(F32))
+        at += size
+    bias_query, bias_value, bias_out, bias_up, bias_down, gain1, shift1, gain2, shift2 = vectors
+    wq = lax.all_gather(w_qkv, "dp", axis=0, tiled=True)
+    wo = lax.all_gather(w_out, "dp", axis=0, tiled=True)
+    wu = lax.all_gather(w_up, "dp", axis=0, tiled=True)
+    wd = lax.all_gather(w_down, "dp", axis=1, tiled=True)
+
+    x_low = gather_image(tokens)
+    cot_low = gather_image(cotangent)
+    x = x_low.astype(F32)
+    xhat1, rstd1 = norm_parts(x)
+    n1 = (xhat1 * gain1 + shift1).astype(BF16)
+    bias = jnp.concatenate([bias_query, jnp.zeros_like(bias_query), bias_value], axis=1)
+    projected = (dot_nn(n1, wq) + bias).astype(BF16)
+    q, k, v = (projected[:, i * d : (i + 1) * d] for i in range(3))
+    kv_other = other_core(projected[:, d:])
+    kb, vb = kv_other[:, :d], kv_other[:, d:]
+    attended, lse = attn_fwd(q, k, kb, v, vb)
+    residual = x + dot_nn(attended, wo) + bias_out
+    xhat2, rstd2 = norm_parts(residual)
+    n2 = (xhat2 * gain2 + shift2).astype(BF16)
+    upward = dot_nn(n2, wu) + bias_up
+    activated, activate_back = jax.vjp(activate, upward)
+    act = activated.astype(BF16)
+    result = return_image((residual + dot_nn(act, wd) + bias_down).astype(BF16))
+
+    (grad_up,) = activate_back(dg(cot_low, wd, NT))
+    grad_up = grad_up.astype(BF16)
+    gn2 = dg(grad_up, wu, NT)
+    grad_residual = cot_low.astype(F32) + norm_back(xhat2, rstd2, gn2, gain2)
+    grad_attn = grad_residual.astype(BF16)
+    grad_mixed = dg(grad_attn, wo, NT).astype(BF16)
+    dq, dka, dkb, dva, dvb = attn_bwd(q, k, kb, v, vb, attended, grad_mixed, lse)
+    dkv_other = other_core(jnp.concatenate([dkb, dvb], axis=1))
+    dkv = (jnp.concatenate([dka, dva], axis=1).astype(F32) + dkv_other.astype(F32)).astype(BF16)
+    gproj = jnp.concatenate([dq, dkv], axis=1)
+    gn1 = dg(gproj, wq, NT)
+    grad_input = return_image((grad_residual + norm_back(xhat1, rstd1, gn1, gain1)).astype(BF16))
+
+    total = lambda value: jnp.sum(value, axis=0, dtype=F32)
+    small_grads = (
+        total(gproj[:, :d]), total(gproj[:, 2 * d :]), total(grad_attn), total(grad_up), total(cot_low),
+        total(gn1 * xhat1), total(gn1), total(gn2 * xhat2), total(gn2),
+    )
+    packed_grads = jnp.concatenate([g.reshape(8, -1) for g in small_grads], axis=1)
+    packed_grads = lax.psum(lax.psum_scatter(packed_grads, "dp", scatter_dimension=0, tiled=True), "seq")[0]
+
+    def owned(grad, axis):
+        part = lax.psum_scatter(grad.astype(BF16), "dp", scatter_dimension=axis, tiled=True)
+        return lax.psum(part, "seq").astype(F32)
+
+    g_down = owned(dg(act, cot_low, TN), 1)
+    g_up = owned(dg(n2, grad_up, TN), 0)
+    g_out = owned(dg(attended, grad_attn, TN), 0)
+    g_qkv = owned(dg(n1, gproj, TN), 0)
+    outs, at = [], 0
+    for size in sizes:
+        outs.append(packed_grads[at : at + size])
+        at += size
+    return (result, grad_input, g_qkv, g_out, g_up, g_down, *outs)
+
+
 def solution(mesh):
     in_specs = (
         P("dp", "seq", None),
@@ -426,4 +632,5 @@
         P("dp"),
         P("dp"),
     )
-    return jax.shard_map(local, mesh=mesh, in_specs=in_specs, out_specs=out_specs, check_vma=False)
+    fn = local_fast if dict(mesh.shape) == {"dp": 8, "seq": 4} else local
+    return jax.shard_map(fn, mesh=mesh, in_specs=in_specs, out_specs=out_specs, check_vma=False)

time: 818 us -> 623 us (0.76)
  local copies, waits for them, and re-layouts: 131 us -> 32 us
  waiting for transfers between devices: 279 us -> 356 us
  blocking collectives: 116 us -> 50.6 us
  matrix products: 152 us -> 88.2 us
  other arithmetic: 73.6 us -> 19.1 us
  Pallas kernels: 0 us -> 43.1 us
  starting transfers between devices: 38.7 us -> 12.6 us
    all_to_all x8 -> x0, waiting for transfers between devices: 114 us -> none  [the longest x2 57.1 us: local(): lax.all_to_all(stacked, 'seq', split_axis=1, concat_axis=3, tiled=True)]
    all_gather x4, waiting for transfers between devices: 7.6 us -> 91.7 us  [the longest x1 37.1 us: local_fast(): wu = lax.all_gather(w_up, 'dp', axis=0, tiled=True)]
    all_gather x9 -> x1, blocking collectives: 78.9 us -> 12.2 us  [local_fast(): packed = lax.all_gather(jnp.concatenate(small), 'dp', axis=0, tiled=False)]
    dot_general x48 -> x12, matrix products: 152 us -> 88.2 us  [dg(): return lax.dot_general(a, b, dims, preferred_element_type=F32)]
    reduce_scatter x3, waiting for transfers between devices: 84.8 us -> 142 us  [owned(): lax.psum_scatter(grad.astype(BF16), 'dp', scatter_dimension=axis, tiled=T...]
    pallas_call x0 -> x2, Pallas kernels: none -> 43.1 us  [the longest x1 25.9 us: attn_bwd(): pl.pallas_call(attn_bwd_kernel, grid=(width // 128,), in_specs=[spec, ks,...]
    all_to_all x8 -> x0, starting transfers between devices: 38.4 us -> none  [the longest x2 10.2 us: local(): lax.all_to_all(grad_mixed, 'seq', split_axis=2, concat_axis=1, tiled=True)]
    unnamed x197 -> x99, local copies, waits for them, and re-layouts: 53.9 us -> 27.5 us
  transfers between devices with their start and end apart: 17 -> 19, of which waited for: 8 -> 10; matrix products, arithmetic and copies ran while one was open for 37% -> 20% of each run, Pallas kernels for 0% -> 7%
where the time goes in v1:
time: 623 us; the launch traced here: 616 us
  waiting for transfers between devices  356 us (57%)
  matrix products  88.2 us (14%)
  blocking collectives  50.6 us (8%)
  Pallas kernels  43.1 us (7%)
  local copies, waits for them, and re-layouts  32 us (5%)
  other arithmetic  19.1 us (3%)
  between operations  14.8 us (2%)
  starting transfers between devices  12.6 us (2%)
    reduce_scatter x3, waiting for transfers between devices, owned(): lax.psum_scatter(grad.astype(BF16), 'dp', scatter_dimension=axis, tiled=T...  142 us
    psum x1, waiting for transfers between devices, owned(): return lax.psum(part, 'seq').astype(F32)  95.3 us
    dot_general x12, matrix products, dg(): return lax.dot_general(a, b, dims, preferred_element_type=F32)  88.2 us
    all_gather x1, waiting for transfers between devices, local_fast(): wu = lax.all_gather(w_up, 'dp', axis=0, tiled=True)  37.1 us
    all_gather x1, waiting for transfers between devices, local_fast(): wq = lax.all_gather(w_qkv, 'dp', axis=0, tiled=True)  28.7 us
    unnamed x1, blocking collectives  28.5 us
    unnamed x99, local copies, waits for them, and re-layouts  27.5 us
    pallas_call x1, Pallas kernels, attn_bwd(): pl.pallas_call(attn_bwd_kernel, grid=(width // 128,), in_specs=[spec, ks,...  25.9 us
  transfers between devices with their start and end apart: 19, of which 10 were waited for; matrix products, arithmetic and copies ran while one was open for 20% of the time, Pallas kernels for 7%

profile of v1, /device:TPU:0, one launch (start us, length us, event | category | flops | bytes accessed | tf_op | source)
XLA Modules:
  0.0 616.5 jit_solution(8330354151666275013)
XLA Ops:
  10.9 3.1 collective-permute-start.1
  16.0 12.2 %all-gather.1 = bf16[8,1,1536]{2,1,0:T(2,128)(2,1)S(1)} all-gather(bf16[1,1,1536]{2,1,0:T(2,128)(2,1)S(1)} %reshape.266), channel_id=2, replica_groups=mesh['dp'=8,'seq'=4] {'dp'}, dimensions={0}, use_global_device_ids=true | all-gather | bytes 27648 | tf_op jit(solution)/shard_map/all_gather | solution.py:534
  29.5 28.7 %all-gather.7.cloned.1.call-done = bf16[1024,3072]{1,0:T(8,128)(2,1)} async-done(((bf16[128,3072]{1,0:T(8,128)(2,1)}), bf16[1024,3072]{1,0:T(8,128)(2,1)}) %all-gather.7.cloned.1.call-update) | async-done | bytes 6291472 | tf_op jit(solution)/shard_map/all_gather | solution.py:540
  58.2 6.4 %add_convert_fusion = bf16[512,3072]{1,0:T(8,128)(2,1)S(1)} fusion(bf16[512,1024]{1,0:T(8,128)(2,1)S(1)} %fusion.15, bf16[1024,3072]{1,0:T(8,128)(2,1)} %all-gather.7.cloned.1.call-done, f32[3072]{0:T(1024)S(1)} %bitcast.186), kind=kOutput, calls=%fused_computation.13 | convolution fusion | flops 3224371200 | bytes 10498048 | tf_op jit(solution)/shard_map/dot_general | solution.py:400
  66.8 1.5 collective-permute-start.6
  68.4 12.5 %collective-permute-done.6 = bf16[256,1024]{1,0:T(8,128)(2,1)S(1)} collective-permute-done((bf16[256,1024]{1,0:T(8,128)(2,1)S(1)}, bf16[256,1024]{1,0:T(8,128)(2,1)S(1)}, u32[]{:S(2)}, u32[]{:S(2)}) %collective-permute-start.6) | collective-permute-done | bytes 524320 | tf_op jit(solution)/shard_map/ppermute | solution.py:488
  81.7 1.4 fusion.38
  83.7 17.2 %attn_fwd.1 = (bf16[512,1024]{1,0:T(8,128)(2,1)S(1)}, f32[8,8,512]{2,1,0:T(8,128)S(1)}) custom-call(bf16[512,1024]{1,0:T(8,128)(2,1)S(1)} %get-tuple-element.51.q_ref, bf16[512,1024]{1,0:T(8,128)(2,1)S(1)} %get-tuple-element.50.ka_ref, bf16[512,1024]{1,0:T(8,128)(2,1)S(1)} %get-tuple-element.53.kb_ref, bf16[512,1024]{1,0:T(8,128)(2,1)S(1)} %get-tuple-element.49.va_ref, ...), custom_call_target="tpu_custom_call" | custom-call | flops 2147483648 | bytes 6291456 | tf_op jit(solution)/shard_map/attn_fwd/pallas_call | solution.py:425
  100.9 1.0 copy-done.3
  101.9 3.3 fusion.39
  105.3 1.3 copy-done.9
  106.9 37.1 %all-gather.11.cloned.1.call-done = bf16[1024,4096]{1,0:T(8,128)(2,1)} async-done(((bf16[128,4096]{1,0:T(8,128)(2,1)}), bf16[1024,4096]{1,0:T(8,128)(2,1)}) %all-gather.11.cloned.1.call-update) | async-done | bytes 8388624 | tf_op jit(solution)/shard_map/all_gather | solution.py:542
  144.0 7.8 %fusion.35 = f32[512,4096]{1,0:T(8,128)S(1)} fusion(bf16[1024,4096]{1,0:T(8,128)(2,1)} %all-gather.11.cloned.1.call-done, f32[512,1024]{1,0:T(8,128)} %copy-done.9, f32[1024]{0:T(1024)S(1)} %get-tuple-element.64, f32[1024]{0:T(1024)S(1)} %get-tuple-element.62, f32[512]{0:T(512)S(1)} %add_rsqrt_fusion, f32[512]{0:T(512)S(1)} %broadcast_multiply_fusion.4), kind=kOutput, calls=%fused_computation.114 | convolution fusion | flops 4297588736 | bytes 18886656 | tf_op jit(solution)/shard_map/dot_general | solution.py:400
  151.8 3.5 copy-done.35
  155.3 8.6 %convolution_convert_fusion = bf16[4096,1024]{1,0:T(8,128)(2,1)} fusion(bf16[512,1024]{1,0:T(8,128)(2,1)S(1)} %bitcast.159, f32[512,4096]{1,0:T(8,128)S(1)} %fusion.35, f32[4096]{0:T(1024)S(1)} %bitcast.181), kind=kOutput, calls=%fused_computation.11 | convolution fusion | flops 4320133120 | bytes 17842176 | tf_op jit(solution)/shard_map/dot_general | solution.py:400
  164.0 11.3 %copy.30 = bf16[4096,1024]{0,1:T(8,128)(2,1)} copy(bf16[4096,1024]{1,0:T(8,128)(2,1)} %convolution_convert_fusion) | data formatting | bytes 16777216
  175.8 25.9 %all-gather.13.cloned.1.call-done = bf16[4096,1024]{1,0:T(8,128)(2,1)} async-done(((bf16[4096,128]{1,0:T(8,128)(2,1)}), bf16[4096,1024]{1,0:T(8,128)(2,1)}) %all-gather.13.cloned.1.call-update) | async-done | bytes 8388624 | tf_op jit(solution)/shard_map/all_gather | solution.py:543
  201.7 13.1 %convert_reduce_fusion = (f32[4096]{0:T(1024)S(1)}, bf16[512,4096]{1,0:T(8,128)(2,1)S(1)}) fusion(f32[512,4096]{1,0:T(8,128)} %copy-done.35, f32[4096]{0:T(1024)S(1)} %bitcast.182, bf16[512,1024]{1,0:T(8,128)(2,1)S(1)} %bitcast.160, bf16[4096,1024]{1,0:T(8,128)(2,1)} %all-gather.13.cloned.1.call-done), kind=kOutput, calls=%fused_computation.9 | convolution fusion | flops 4343197696 | bytes 22052864 | tf_op jit(solution)/shard_map/dot_general | solution.py:400
  214.8 9.8 %multiply_reduce_fusion = (f32[1024]{0:T(1024)S(1)}, f32[512]{0:T(512)S(1)}, f32[512]{0:T(512)S(1)}, f32[1024]{0:T(1024)S(1)}, f32[512,1024]{1,0:T(8,128)S(1)}) fusion(f32[512,1024]{1,0:T(8,128)S(1)} %copy-done.10, f32[512]{0:T(512)S(1)} %add_rsqrt_fusion, f32[512]{0:T(512)S(1)} %broadcast_multiply_fusion.4, f32[1024]{0:T(1024)S(1)} %get-tuple-element.62, ...), kind=kOutput, calls=%fused_computation.38 | convolution fusion | flops 4299682816 | bytes 16797696 | tf_op jit(solution)/shard_map/dot_general | solution.py:400
  226.2 2.3 convolution_convert_fusion.4.do_ref
  228.4 25.9 %attn_bwd.1 = (bf16[512,1024]{1,0:T(8,128)(2,1)S(1)}, bf16[512,1024]{1,0:T(8,128)(2,1)S(1)}, bf16[512,1024]{1,0:T(8,128)(2,1)S(1)}, bf16[512,1024]{1,0:T(8,128)(2,1)S(1)}, bf16[512,1024]{1,0:T(8,128)(2,1)S(1)}) custom-call(bf16[512,1024]{1,0:T(8,128)(2,1)} %copy-done.2, bf16[512,1024]{1,0:T(8,128)(2,1)} %copy-done.1, bf16[512,1024]{1,0:T(8,128)(2,1)} %copy-done.3, ...), custom_call_target="tpu_custom_call" | custom-call | flops 5368709120 | bytes 13631488 | tf_op jit(solution)/shard_map/attn_bwd/pallas_call | solution.py:465
  254.3 1.6 pad_maximum_fusion.1
  256.1 2.7 convolution_convert_fusion.3
  258.9 1.5 collective-permute-done.7
  260.4 2.8 add_convert_fusion.1
  263.2 1.4 copy-done.12
  264.6 5.6 convolution_convert_fusion.2
  270.3 1.6 copy-done.11
  271.9 9.2 %convolution_convert_fusion.1 = bf16[1024,4096]{1,0:T(8,128)(2,1)} fusion(bf16[512,4096]{1,0:T(8,128)(2,1)} %copy-done.36, f32[512,1024]{1,0:T(8,128)S(1)} %copy-done.11, f32[1024]{0:T(1024)S(1)} %get-tuple-element.64, f32[1024]{0:T(1024)S(1)} %get-tuple-element.62, f32[512]{0:T(512)S(1)} %add_rsqrt_fusion, f32[512]{0:T(512)S(1)} %broadcast_multiply_fusion.4), kind=kOutput, calls=%fused_computation.12 | convolution fusion | flops 4301783040 | bytes 14692352 | tf_op jit(solution)/shard_map/dot_general | solution.py:400
  281.1 11.5 %add_convert_fusion.2 = bf16[512,1024]{1,0:T(8,128)(2,1)S(1)} fusion(f32[512,1024]{1,0:T(8,128)S(1)} %copy-done.11, bf16[4096,1024]{1,0:T(8,128)(2,1)} %all-gather.13.cloned.1.call-done, f32[1024]{0:T(1024)S(1)} %get-tuple-element.63, f32[512,4096]{1,0:T(8,128)} %copy-done.35, f32[4096]{0:T(1024)S(1)} %bitcast.183), kind=kOutput, calls=%fused_computation.45 | convolution fusion | flops 4317511680 | bytes 19943424 | tf_op jit(solution)/shard_map/dot_general | solution.py:400
  292.6 1.0 dynamic-slice_bitcast_fusion.5
  294.7 1.9 collective-permute-start.3
  297.3 9.9 %collective-permute-done.4 = bf16[256,1024]{1,0:T(8,128)(2,1)S(1)} collective-permute-done((bf16[256,1024]{1,0:T(8,128)(2,1)}, bf16[256,1024]{1,0:T(8,128)(2,1)S(1)}, u32[]{:S(2)}, u32[]{:S(2)}) %collective-permute-start.4) | collective-permute-done | bytes 524320 | tf_op jit(solution)/shard_map/ppermute | solution.py:501
  307.2 1.1 maximum_select_fusion.1
  308.3 8.0 %fusion.21 = (f32[1024]{0:T(1024)S(1)}, f32[512]{0:T(512)S(1)}, f32[512]{0:T(512)S(1)}, f32[1024]{0:T(1024)S(1)}, f32[512,1024]{1,0:T(8,128)}) fusion(bf16[2,256,1024]{2,1,0:T(8,128)(2,1)S(1)} %copy-done.7, f32[512]{0:T(512)S(1)} %bitcast.176, f32[512]{0:T(512)S(1)} %bitcast.179, f32[1024]{0:T(1024)S(1)} %get-tuple-element.69, ...), kind=kOutput, calls=%fused_computation.36 | convolution fusion | flops 3232756736 | bytes 12603392 | tf_op jit(solution)/shard_map/dot_general | solution.py:400
  316.3 2.3 copy.31
  318.6 2.2 reduce-scatter.9.cloned.1.call-done
  320.8 65.2 %reduce-scatter.7.cloned.1.call-done = bf16[128,3072]{1,0:T(8,128)(2,1)} async-done(((bf16[1024,3072]{1,0:T(8,128)(2,1)}), bf16[128,3072]{1,0:T(8,128)(2,1)}) %reduce-scatter.7.cloned.1.call-update) | async-done | bytes 786448 | tf_op jit(solution)/shard_map/reduce_scatter | solution.py:586
  386.0 75.0 %reduce-scatter.11.cloned.1.call-done = bf16[128,4096]{1,0:T(8,128)(2,1)} async-done(((bf16[1024,4096]{1,0:T(8,128)(2,1)}), bf16[128,4096]{1,0:T(8,128)(2,1)}) %reduce-scatter.11.cloned.1.call-update) | async-done | bytes 1048592 | tf_op jit(solution)/shard_map/reduce_scatter | solution.py:586
  461.0 2.9 fusion.20
  464.1 1.6 collective-permute-start.9
  466.6 28.5 %all-reduce = f32[8,1536]{1,0:T(8,128)S(1)} all-reduce(f32[8,1536]{1,0:T(8,128)S(1)} %constant_dynamic-update-slice_fusion), channel_id=7, replica_groups=mesh['dp'=8,'seq'=4] {'dp'}, use_global_device_ids=true, to_apply=%region_25.26.clone | all-reduce | flops 12288 | bytes 98304
  495.7 10.0 %psum.39 = f32[1,1536]{1,0:T(1,128)S(1)} all-reduce(f32[1,1536]{1,0:T(1,128)S(1)} %constant_dynamic-slice_fusion), channel_id=1, replica_groups=mesh['dp'=8,'seq'=4] {'seq'}, use_global_device_ids=true, to_apply=%region_26.27 | all-reduce | flops 1536 | bytes 12288 | tf_op jit(solution)/shard_map/psum | solution.py:583
  506.9 1.1 maximum_select_fusion.3
  508.0 95.3 %all-reduce.4.cloned.1.call-done = (bf16[128,3072]{1,0:T(8,128)(2,1)}, bf16[128,1024]{1,0:T(8,128)(2,1)}, bf16[128,4096]{1,0:T(8,128)(2,1)}, bf16[4096,128]{1,0:T(8,128)(2,1)}) async-done(((bf16[128,3072]{1,0:T(8,128)(2,1)}, bf16[128,1024]{1,0:T(8,128)(2,1)}, bf16[128,4096]{1,0:T(8,128)(2,1)}, bf16[4096,128]{1,0:T(8,128)(2,1)}), (bf16[128,3072]{1,0:T(8,128)(2,1)}, bf16[128,1024]{1,0:T(8,128)(2,1)}, ...) | async-done | bytes 3145744 | tf_op jit(solution)/shard_map/psum | solution.py:587
  603.3 2.5 convert_element_type.229
  606.7 1.5 convert_element_type.233
  608.2 1.5 convert_element_type.235
  (157 shorter events, 18.6 us)
Async XLA Ops:
  7.2 3.0 copy-start.21
  7.2 51.0 %all-gather.7.cloned.1.call-start = ((), (), s32[]{:S(2)}) async-start(), calls=%async_computation.4 | async-start | bytes 7077888 | tf_op jit(solution)/shard_map/all_gather | solution.py:540
  7.9 94.0 %all-gather.9.cloned.1.call-start = ((), (), s32[]{:S(2)}) async-start(), calls=%async_computation.5 | async-start | bytes 2359296 | tf_op jit(solution)/shard_map/all_gather | solution.py:541
  8.7 5.4 copy-start.25
  8.7 5.6 copy-start.26
  8.7 5.8 copy-start.27
  8.7 6.0 copy-start.24
  8.7 6.2 %copy-start.28 = (bf16[128]{0:T(256)(128)(2,1)S(1)}, bf16[128]{0:T(256)(128)(2,1)}, u32[]{:S(2)}) copy-start(bf16[128]{0:T(256)(128)(2,1)} %param.24) | copy-start | bytes 772
  8.7 6.4 %copy-start.29 = (bf16[128]{0:T(256)(128)(2,1)S(1)}, bf16[128]{0:T(256)(128)(2,1)}, u32[]{:S(2)}) copy-start(bf16[128]{0:T(256)(128)(2,1)} %param.25) | copy-start | bytes 772
  8.7 6.6 %copy-start.30 = (bf16[128]{0:T(256)(128)(2,1)S(1)}, bf16[128]{0:T(256)(128)(2,1)}, u32[]{:S(2)}) copy-start(bf16[128]{0:T(256)(128)(2,1)} %param.26) | copy-start | bytes 772
  8.7 6.8 %copy-start.31 = (bf16[128]{0:T(256)(128)(2,1)S(1)}, bf16[128]{0:T(256)(128)(2,1)}, u32[]{:S(2)}) copy-start(bf16[128]{0:T(256)(128)(2,1)} %param.27) | copy-start | bytes 772
  8.8 7.0 %copy-start.32 = (bf16[128]{0:T(256)(128)(2,1)S(1)}, bf16[128]{0:T(256)(128)(2,1)}, u32[]{:S(2)}) copy-start(bf16[128]{0:T(256)(128)(2,1)} %param.28) | copy-start | bytes 772
  8.8 135.3 %all-gather.11.cloned.1.call-start = ((), (), s32[]{:S(2)}) async-start(), calls=%async_computation.6 | async-start | bytes 9437184 | tf_op jit(solution)/shard_map/all_gather | solution.py:542
  9.5 192.2 %all-gather.13.cloned.1.call-start = ((), (), s32[]{:S(2)}) async-start(), calls=%async_computation.7 | async-start | bytes 9437184 | tf_op jit(solution)/shard_map/all_gather | solution.py:543
  10.1 306.3 %reduce-scatter.13.cloned.1.call-start = ((), (), s32[]{:S(2)}) async-start(), calls=%async_computation.11 | async-start | bytes 9437184
  10.2 17.9 %collective-permute-start = (bf16[256,1024]{1,0:T(8,128)(2,1)S(1)}, bf16[256,1024]{1,0:T(8,128)(2,1)S(1)}, u32[]{:S(2)}, u32[]{:S(2)}) collective-permute-start(bf16[256,1024]{1,0:T(8,128)(2,1)S(1)} %get-tuple-element.61), channel_id=1, source_target_pairs={{0,0},{1,1},{2,4},{3,5},{4,2},{5,3},{6,6},{7,7},{8,8},{9,9},{10,12... | collective-permute-start | bytes 1572872 | tf_op jit(solution)/shard_map/ppermute | solution.py:488
  10.9 17.2 %collective-permute-start.1 = (bf16[256,1024]{1,0:T(8,128)(2,1)S(1)}, bf16[256,1024]{1,0:T(8,128)(2,1)S(1)}, u32[]{:S(2)}, u32[]{:S(2)}) collective-permute-start(bf16[256,1024]{1,0:T(8,128)(2,1)S(1)} %get-tuple-element.60), channel_id=1, source_target_pairs={{0,1},{1,0},{2,5},{3,4},{4,3},{5,2},{6,7},{7,6},{8,9},{9,8},{10,13... | collective-permute-start | bytes 1572872 | tf_op jit(solution)/shard_map/ppermute | solution.py:488
  28.6 73.4 %copy-start.6 = (bf16[2,256,1024]{2,1,0:T(8,128)(2,1)}, bf16[2,256,1024]{2,1,0:T(8,128)(2,1)S(1)}, u32[]{:S(2)}) copy-start(bf16[2,256,1024]{2,1,0:T(8,128)(2,1)S(1)} %get-tuple-element.48) | copy-start | bytes 3145732
  29.5 35.1 %copy-start.19 = (bf16[512,1024]{1,0:T(8,128)(2,1)}, bf16[512,1024]{1,0:T(8,128)(2,1)S(1)}, u32[]{:S(2)}) copy-start(bf16[512,1024]{1,0:T(8,128)(2,1)S(1)} %fusion.15) | copy-start | bytes 3145732
  64.8 16.9 %collective-permute-start.2 = (bf16[512,2048]{1,0:T(8,128)(2,1)S(1)}, bf16[512,2048]{1,0:T(8,128)(2,1)S(1)}, u32[]{:S(2)}, u32[]{:S(2)}) collective-permute-start(bf16[512,2048]{1,0:T(8,128)(2,1)S(1)} %slice.142), channel_id=1, source_target_pairs={{0,4},{4,0},{8,12},{12,8},{16,20},{20,16},{24,28},{28,24},{1,5},{5... | collective-permute-start | bytes 6291464 | tf_op jit(solution)/shard_map/ppermute | solution.py:506
  65.9 2.5 collective-permute-start.5
  66.8 14.1 %collective-permute-start.6 = (bf16[256,1024]{1,0:T(8,128)(2,1)S(1)}, bf16[256,1024]{1,0:T(8,128)(2,1)S(1)}, u32[]{:S(2)}, u32[]{:S(2)}) collective-permute-start(bf16[256,1024]{1,0:T(8,128)(2,1)S(1)} %get-tuple-element.56), channel_id=1, source_target_pairs={{0,1},{1,0},{2,5},{3,4},{4,3},{5,2},{6,7},{7,6},{8,9},{9,8},{10,13... | collective-permute-start | bytes 1572872 | tf_op jit(solution)/shard_map/ppermute | solution.py:488
  81.2 70.6 %copy-start.15 = (bf16[2,256,1024]{2,1,0:T(8,128)(2,1)}, bf16[2,256,1024]{2,1,0:T(8,128)(2,1)S(1)}, u32[]{:S(2)}) copy-start(bf16[2,256,1024]{2,1,0:T(8,128)(2,1)S(1)} %get-tuple-element.42) | copy-start | bytes 3145732
  81.7 2.0 copy-start.2
  101.9 3.3 copy-start.4
  151.8 3.5 copy-start.35
  175.3 26.4 %copy-start.16 = (bf16[2,256,1024]{2,1,0:T(8,128)(2,1)S(1)}, bf16[2,256,1024]{2,1,0:T(8,128)(2,1)}, u32[]{:S(2)}) copy-start(bf16[2,256,1024]{2,1,0:T(8,128)(2,1)} %copy-done.15) | copy-start | bytes 3145732
  175.3 39.5 %copy-start.10 = (f32[512,1024]{1,0:T(8,128)S(1)}, f32[512,1024]{1,0:T(8,128)}, u32[]{:S(2)}) copy-start(f32[512,1024]{1,0:T(8,128)} %copy-done.9) | copy-start | bytes 6291460
  175.3 145.5 %reduce-scatter.9.cloned.1.call-start = ((), (), s32[]{:S(2)}) async-start(), calls=%async_computation.9 | async-start | bytes 2359296 | tf_op jit(solution)/shard_map/reduce_scatter | solution.py:586
  214.8 9.8 %copy-start.36 = (bf16[512,4096]{1,0:T(8,128)(2,1)}, bf16[512,4096]{1,0:T(8,128)(2,1)S(1)}, u32[]{:S(2)}) copy-start(bf16[512,4096]{1,0:T(8,128)(2,1)S(1)} %get-tuple-element.44) | copy-start | bytes 12582916
  225.4 30.7 %copy-start.8 = (f32[512,1024]{1,0:T(8,128)}, f32[512,1024]{1,0:T(8,128)S(1)}, u32[]{:S(2)}) copy-start(f32[512,1024]{1,0:T(8,128)S(1)} %get-tuple-element.46) | copy-start | bytes 6291460
  254.3 1.8 copy-start.5
  255.9 4.5 collective-permute-start.7
  258.9 127.1 %reduce-scatter.7.cloned.1.call-start = ((), (), s32[]{:S(2)}) async-start(), calls=%async_computation.8 | async-start | bytes 7077888 | tf_op jit(solution)/shard_map/reduce_scatter | solution.py:586
  260.4 4.2 copy-start.20
  270.2 190.7 %reduce-scatter.11.cloned.1.call-start = ((), (), s32[]{:S(2)}) async-start(), calls=%async_computation.10 | async-start | bytes 9437184 | tf_op jit(solution)/shard_map/reduce_scatter | solution.py:586
  281.1 322.3 %all-reduce.4.cloned.1.call-start = ((), (), s32[]{:S(2)}) async-start(), calls=%async_computation.12 | async-start | bytes 6291456 | tf_op jit(solution)/shard_map/psum | solution.py:587
  292.6 3.9 copy-start.34
  293.7 14.7 %copy-start.7 = (bf16[2,256,1024]{2,1,0:T(8,128)(2,1)S(1)}, bf16[2,256,1024]{2,1,0:T(8,128)(2,1)}, u32[]{:S(2)}) copy-start(bf16[2,256,1024]{2,1,0:T(8,128)(2,1)} %copy-done.6) | copy-start | bytes 3145732
  293.7 13.5 %collective-permute-start.4 = (bf16[256,1024]{1,0:T(8,128)(2,1)}, bf16[256,1024]{1,0:T(8,128)(2,1)S(1)}, u32[]{:S(2)}, u32[]{:S(2)}) collective-permute-start(bf16[256,1024]{1,0:T(8,128)(2,1)} %get-tuple-element.59), channel_id=1, source_target_pairs={{1,0},{0,1},{5,2},{4,3},{3,4},{2,5},{7,6},{6,7},{9,8},{8,9},{13,10... | collective-permute-start | bytes 1572872 | tf_op jit(solution)/shard_map/ppermute | solution.py:501
  294.7 12.6 %collective-permute-start.3 = (bf16[256,1024]{1,0:T(8,128)(2,1)}, bf16[256,1024]{1,0:T(8,128)(2,1)S(1)}, u32[]{:S(2)}, u32[]{:S(2)}) collective-permute-start(bf16[256,1024]{1,0:T(8,128)(2,1)} %get-tuple-element.58), channel_id=1, source_target_pairs={{0,0},{1,1},{4,2},{5,3},{2,4},{3,5},{6,6},{7,7},{8,8},{9,9},{12,10... | collective-permute-start | bytes 1572872 | tf_op jit(solution)/shard_map/ppermute | solution.py:501
  297.1 11.2 %copy-start.13 = (bf16[512,2048]{1,0:T(8,128)(2,1)S(1)}, bf16[512,2048]{1,0:T(8,128)(2,1)}, u32[]{:S(2)}) copy-start(bf16[512,2048]{1,0:T(8,128)(2,1)} %copy-done.12) | copy-start | bytes 6291460
  464.0 2.3 copy-start.14
  464.1 42.8 %collective-permute-start.9 = (bf16[256,1024]{1,0:T(8,128)(2,1)S(1)}, bf16[256,1024]{1,0:T(8,128)(2,1)S(1)}, u32[]{:S(2)}, u32[]{:S(2)}) collective-permute-start(bf16[256,1024]{1,0:T(8,128)(2,1)S(1)} %get-tuple-element.55), channel_id=1, source_target_pairs={{1,0},{0,1},{5,2},{4,3},{3,4},{2,5},{7,6},{6,7},{9,8},{8,9},{13,10... | collective-permute-start | bytes 1572872 | tf_op jit(solution)/shard_map/ppermute | solution.py:501
  465.6 41.3 %collective-permute-start.8 = (bf16[256,1024]{1,0:T(8,128)(2,1)S(1)}, bf16[256,1024]{1,0:T(8,128)(2,1)S(1)}, u32[]{:S(2)}, u32[]{:S(2)}) collective-permute-start(bf16[256,1024]{1,0:T(8,128)(2,1)S(1)} %get-tuple-element.54), channel_id=1, source_target_pairs={{0,0},{1,1},{4,2},{5,3},{2,4},{3,5},{6,6},{7,7},{8,8},{9,9},{12,10... | collective-permute-start | bytes 1572872 | tf_op jit(solution)/shard_map/ppermute | solution.py:501
  603.3 2.5 copy-start.23
  603.3 3.4 copy-start.18
  605.9 2.4 copy-start.17
  (8 other events, 11.2 us)
Sparse Core Ops, SparseCore 0:
  9.9 48.2 all-gather.6
  60.0 27.7 all-gather.8
  89.7 54.2 all-gather.10
  145.8 55.8 all-gather.12
  205.0 71.5 reduce-scatter.12
  279.7 41.0 reduce-scatter.8
  324.2 61.7 reduce-scatter.6
  389.4 71.4 reduce-scatter.10
  464.2 139.1 all-reduce.3

commit v2 on v1

--- a/solution.py
+++ b/solution.py
@@ -524,26 +524,155 @@
     )
 
 
+MESH = pl.DeviceIdType.MESH
+HBM = pltpu.MemorySpace.HBM
+
+
+def flip(value, bits):
+    return lax.ppermute(value, "dp", [(i, i ^ bits) for i in range(8)])
+
+
+def flip_z(value, bits):
+    return lax.ppermute(value, "seq", [(i, i ^ bits) for i in range(4)])
+
+
+def after(value, *earlier):
+    return lax.optimization_barrier((value,) + earlier)[0]
+
+
+def finish_kernel(a01, a2, b01, b2, out, kept, in_sem, out_sem, send_sem, recv_sem):
+    d, z = lax.axis_index("dp"), lax.axis_index("seq")
+    core, x, y = lax.rem(d, 2), lax.rem(d // 2, 2), d // 4
+    sibling = (d + 1 - 2 * core, z)
+    half = a01.shape[2]
+    barrier = pltpu.get_barrier_semaphore()
+    pl.semaphore_signal(barrier, inc=1, device_id=sibling, device_id_type=MESH)
+    pl.semaphore_wait(barrier, 1)
+    pieces = (
+        (a01.at[0], y, x, 0), (b01.at[0], y, x, 1),
+        (a01.at[1], y, 1 - x, 0), (b01.at[1], 1 - y, x, 1),
+        (a2.at[0], 1 - y, x, 0), (b2.at[0], y, 1 - x, 1),
+        (a2.at[1], 1 - y, 1 - x, 0), (b2.at[1], 1 - y, 1 - x, 1),
+    )
+    sends, loads, stores = [], [], []
+    for k, (piece, py, px, side) in enumerate(pieces):
+        row = pl.multiple_of(((py * 2 + px) * 2 + core) * 128, 128)
+        target = out.at[pl.ds(row, 128), pl.ds(side * half, half)]
+        sends.append(
+            pltpu.make_async_remote_copy(
+                src_ref=piece, dst_ref=target, send_sem=send_sem.at[k], recv_sem=recv_sem.at[k],
+                device_id=sibling, device_id_type=MESH,
+            )
+        )
+        loads.append(pltpu.make_async_copy(piece, kept.at[k], in_sem.at[k]))
+        stores.append(pltpu.make_async_copy(kept.at[k], target, out_sem.at[k]))
+    for k in range(8):
+        sends[k].start()
+        loads[k].start()
+    for k in range(8):
+        loads[k].wait()
+        stores[k].start()
+    for k in range(8):
+        stores[k].wait()
+        sends[k].wait()
+
+
+def finish(parts, ident):
+    half = parts[0].shape[2]
+    return pl.pallas_call(
+        finish_kernel,
+        in_specs=[pl.BlockSpec(memory_space=pl.ANY)] * 4,
+        out_specs=pl.BlockSpec(memory_space=HBM),
+        out_shape=jax.ShapeDtypeStruct((1024, 2 * half), BF16),
+        scratch_shapes=[pltpu.VMEM((8, 128, half), BF16)] + [pltpu.SemaphoreType.DMA((8,))] * 4,
+        compiler_params=pltpu.CompilerParams(collective_id=ident, has_side_effects=True),
+        cost_estimate=pl.CostEstimate(flops=0, bytes_accessed=8192 * half, transcendentals=0),
+        name="finish%d" % ident,
+    )(*parts)
+
+
+def first_hop(shard):
+    half = shard.shape[1] // 2
+    a, b = shard[:, :half], shard[:, half:]
+    return jnp.stack([a, flip(a, 2)]), jnp.stack([b, flip(b, 4)])
+
+
+def second_hop(first):
+    return first[0], flip(first[0], 4), first[1], flip(first[1], 2)
+
+
+def relative(value, order, me):
+    return jnp.concatenate(
+        [lax.dynamic_slice_in_dim(value, 128 * (me ^ r), 128, axis=1) for r in order], axis=1
+    )
+
+
+def to_sibling(odd, right):
+    half = right.shape[1] // 2
+    return [flip(dg(odd, right[:, i * half : (i + 1) * half], TN).astype(BF16), 1) for i in range(2)]
+
+
+def f32_add(left, right):
+    return left.astype(F32) + right.astype(F32)
+
+
+def low_add(left, right):
+    return f32_add(left, right).astype(BF16)
+
+
+def scatter(even, right, from_sibling):
+    half = right.shape[1] // 2
+    ga, gb = (
+        (dg(even, right[:, i * half : (i + 1) * half], TN) + from_sibling[i].astype(F32)).astype(BF16)
+        for i in range(2)
+    )
+    ga2 = low_add(ga[:256], flip(ga[256:], 4))
+    gb_keep = jnp.concatenate([gb[:128], gb[256:384]])
+    gb2 = low_add(gb_keep, flip(jnp.concatenate([gb[128:256], gb[384:]]), 2))
+    return low_add(ga2[:128], flip(ga2[128:], 2)), low_add(gb2[:128], flip(gb2[128:], 4))
+
+
+def sum_z(halves):
+    odd = lax.axis_index("seq") % 2 == 1
+    keep = jnp.where(odd, halves[1], halves[0])
+    give = jnp.where(odd, halves[0], halves[1])
+    kept = lax.optimization_barrier(low_add(keep, flip_z(give, 1)))
+    mine = lax.optimization_barrier(low_add(kept, flip_z(kept, 2)))
+    other = flip_z(mine, 1)
+    return jnp.concatenate([jnp.where(odd, other, mine), jnp.where(odd, mine, other)], axis=1).astype(F32)
+
+
 def local_fast(
     tokens, w_qkv, w_out, w_up, w_down, b_query, b_value, b_out, b_up, b_down,
     ln1_gain, ln1_bias, ln2_gain, ln2_bias, cotangent,
 ):
     d = tokens.shape[2]
+    me = lax.axis_index("dp")
     small = (b_query, b_value, b_out, b_up, b_down, ln1_gain, ln1_bias, ln2_gain, ln2_bias)
     sizes = [item.shape[0] for item in small]
-    packed = lax.all_gather(jnp.concatenate(small), "dp", axis=0, tiled=False)
+
+    x_low = gather_image(tokens)
+    pack = jnp.concatenate(small).reshape(1, -1)
+    for bits in (1, 2, 4):
+        pack = jnp.concatenate([pack, flip(pack, bits)])
+    packed = jnp.concatenate([lax.dynamic_slice_in_dim(pack, me ^ r, 1, axis=0) for r in range(8)])
     vectors, at = [], 0
     for size in sizes:
         vectors.append(packed[:, at : at + size].reshape(1, -1).astype(F32))
         at += size
     bias_query, bias_value, bias_out, bias_up, bias_down, gain1, shift1, gain2, shift2 = vectors
-    wq = lax.all_gather(w_qkv, "dp", axis=0, tiled=True)
-    wo = lax.all_gather(w_out, "dp", axis=0, tiled=True)
-    wu = lax.all_gather(w_up, "dp", axis=0, tiled=True)
-    wd = lax.all_gather(w_down, "dp", axis=1, tiled=True)
-
-    x_low = gather_image(tokens)
-    cot_low = gather_image(cotangent)
+
+    qkv1 = first_hop(w_qkv)
+    qkv2 = second_hop(qkv1)
+    out1 = first_hop(after(w_out, *qkv1))
+    out2 = second_hop(out1)
+    up1 = first_hop(after(w_up, *qkv2))
+    up2 = second_hop(up1)
+    down1 = first_hop(after(w_down.T, *out2))
+    down2 = second_hop(down1)
+    wq = finish(qkv2, 0)
+    cot_low = gather_image(after(cotangent, x_low))
+
     x = x_low.astype(F32)
     xhat1, rstd1 = norm_parts(x)
     n1 = (xhat1 * gain1 + shift1).astype(BF16)
@@ -553,24 +682,35 @@
     kv_other = other_core(projected[:, d:])
     kb, vb = kv_other[:, :d], kv_other[:, d:]
     attended, lse = attn_fwd(q, k, kb, v, vb)
+    wo = finish(out2, 1)
     residual = x + dot_nn(attended, wo) + bias_out
     xhat2, rstd2 = norm_parts(residual)
     n2 = (xhat2 * gain2 + shift2).astype(BF16)
+    wu = finish(up2, 2)
     upward = dot_nn(n2, wu) + bias_up
     activated, activate_back = jax.vjp(activate, upward)
     act = activated.astype(BF16)
-    result = return_image((residual + dot_nn(act, wd) + bias_down).astype(BF16))
-
-    (grad_up,) = activate_back(dg(cot_low, wd, NT))
+    down_sib = to_sibling(relative(cot_low, (1, 3, 5, 7), me), act)
+    g_down = scatter(relative(cot_low, (0, 2, 4, 6), me), act, down_sib)
+    wdt = finish(down2, 3)
+    result = return_image((residual + dg(act, wdt, NT) + bias_down).astype(BF16))
+
+    (grad_up,) = activate_back(dg(cot_low, wdt, NN))
     grad_up = grad_up.astype(BF16)
+    up_sib = to_sibling(relative(n2, (1, 3, 5, 7), me), grad_up)
+    g_up = scatter(relative(n2, (0, 2, 4, 6), me), grad_up, up_sib)
     gn2 = dg(grad_up, wu, NT)
     grad_residual = cot_low.astype(F32) + norm_back(xhat2, rstd2, gn2, gain2)
     grad_attn = grad_residual.astype(BF16)
+    out_sib = to_sibling(relative(attended, (1, 3, 5, 7), me), grad_attn)
+    g_out = scatter(relative(attended, (0, 2, 4, 6), me), grad_attn, out_sib)
     grad_mixed = dg(grad_attn, wo, NT).astype(BF16)
     dq, dka, dkb, dva, dvb = attn_bwd(q, k, kb, v, vb, attended, grad_mixed, lse)
     dkv_other = other_core(jnp.concatenate([dkb, dvb], axis=1))
     dkv = (jnp.concatenate([dka, dva], axis=1).astype(F32) + dkv_other.astype(F32)).astype(BF16)
     gproj = jnp.concatenate([dq, dkv], axis=1)
+    qkv_sib = to_sibling(relative(n1, (1, 3, 5, 7), me), gproj)
+    g_qkv = scatter(relative(n1, (0, 2, 4, 6), me), gproj, qkv_sib)
     gn1 = dg(gproj, wq, NT)
     grad_input = return_image((grad_residual + norm_back(xhat1, rstd1, gn1, gain1)).astype(BF16))
 
@@ -579,22 +719,17 @@
         total(gproj[:, :d]), total(gproj[:, 2 * d :]), total(grad_attn), total(grad_up), total(cot_low),
         total(gn1 * xhat1), total(gn1), total(gn2 * xhat2), total(gn2),
     )
-    packed_grads = jnp.concatenate([g.reshape(8, -1) for g in small_grads], axis=1)
-    packed_grads = lax.psum(lax.psum_scatter(packed_grads, "dp", scatter_dimension=0, tiled=True), "seq")[0]
-
-    def owned(grad, axis):
-        part = lax.psum_scatter(grad.astype(BF16), "dp", scatter_dimension=axis, tiled=True)
-        return lax.psum(part, "seq").astype(F32)
-
-    g_down = owned(dg(act, cot_low, TN), 1)
-    g_up = owned(dg(n2, grad_up, TN), 0)
-    g_out = owned(dg(attended, grad_attn, TN), 0)
-    g_qkv = owned(dg(n1, gproj, TN), 0)
+    sums = jnp.concatenate([g.reshape(8, -1) for g in small_grads], axis=1)
+    for bits in (1, 2, 4):
+        sums = lax.optimization_barrier(sums + flip(sums, bits))
+    for bits in (1, 2):
+        sums = lax.optimization_barrier(sums + flip_z(sums, bits))
+    mine = lax.dynamic_slice_in_dim(sums, me, 1, axis=0)[0]
     outs, at = [], 0
     for size in sizes:
-        outs.append(packed_grads[at : at + size])
+        outs.append(mine[at : at + size])
         at += size
-    return (result, grad_input, g_qkv, g_out, g_up, g_down, *outs)
+    return (result, grad_input, sum_z(g_qkv), sum_z(g_out), sum_z(g_up), sum_z(g_down).T, *outs)
 
 
 def solution(mesh):

time: 623 us -> 569 us (0.913)
  waiting for transfers between devices: 356 us -> 250 us
  starting transfers between devices: 12.6 us -> 82.2 us
  blocking collectives: 50.6 us -> 0 us
  Pallas kernels: 43.1 us -> 73.4 us
  other arithmetic: 19.1 us -> 38.6 us
  between operations: 14.8 us -> 2.79 us
  matrix products: 88.2 us -> 77.1 us
    ppermute x0 -> x60, waiting for transfers between devices: none -> 249 us  [the longest x14 132 us: flip_z(): return lax.ppermute(value, 'seq', [(i, i ^ bits) for i in range(4)])]
    reduce_scatter x3 -> x0, waiting for transfers between devices: 142 us -> none  [owned(): lax.psum_scatter(grad.astype(BF16), 'dp', scatter_dimension=axis, tiled=T...]
    psum x1 -> x0, waiting for transfers between devices: 95.3 us -> none  [owned(): return lax.psum(part, 'seq').astype(F32)]
    all_gather x4 -> x0, waiting for transfers between devices: 91.7 us -> none  [the longest x1 37.1 us: local_fast(): wu = lax.all_gather(w_up, 'dp', axis=0, tiled=True)]
    ppermute x0 -> x60, starting transfers between devices: none -> 72.4 us  [the longest x46 61.7 us: flip(): return lax.ppermute(value, 'dp', [(i, i ^ bits) for i in range(8)])]
    pallas_call x0 -> x4, Pallas kernels: none -> 29.4 us  [finish(): pl.pallas_call(finish_kernel, in_specs=[pl.BlockSpec(memory_space=pl.ANY)...]
    unnamed x1 -> x0, blocking collectives: 28.5 us -> none
    all_gather x1 -> x0, blocking collectives: 12.2 us -> none  [local_fast(): packed = lax.all_gather(jnp.concatenate(small), 'dp', axis=0, tiled=False)]
  transfers between devices with their start and end apart: 19 -> 70, of which waited for: 10 -> 32; matrix products, arithmetic and copies ran while one was open for 20% -> 16% of each run, Pallas kernels for 7% -> 5%
where the time goes in v2:
time: 569 us; the launch traced here: 560 us
  waiting for transfers between devices  250 us (44%)
  starting transfers between devices  82.2 us (14%)
  matrix products  77.1 us (14%)
  Pallas kernels  73.4 us (13%)
  other arithmetic  38.6 us (7%)
  local copies, waits for them, and re-layouts  35.8 us (6%)
    ppermute x14, waiting for transfers between devices, flip_z(): return lax.ppermute(value, 'seq', [(i, i ^ bits) for i in range(4)])  132 us
    ppermute x46, waiting for transfers between devices, flip(): return lax.ppermute(value, 'dp', [(i, i ^ bits) for i in range(8)])  117 us
    dot_general x24, matrix products, dg(): return lax.dot_general(a, b, dims, preferred_element_type=F32)  77.1 us
    ppermute x46, starting transfers between devices, flip(): return lax.ppermute(value, 'dp', [(i, i ^ bits) for i in range(8)])  61.7 us
    pallas_call x4, Pallas kernels, finish(): pl.pallas_call(finish_kernel, in_specs=[pl.BlockSpec(memory_space=pl.ANY)...  29.4 us
    pallas_call x1, Pallas kernels, attn_bwd(): pl.pallas_call(attn_bwd_kernel, grid=(width // 128,), in_specs=[spec, ks,...  26.1 us
    pallas_call x1, Pallas kernels, attn_fwd(): pl.pallas_call(attn_fwd_kernel, grid=(width // 128,), in_specs=[spec, ks,...  18 us
    unnamed x193, local copies, waits for them, and re-layouts  17.6 us
  transfers between devices with their start and end apart: 70, of which 32 were waited for; matrix products, arithmetic and copies ran while one was open for 16% of the time, Pallas kernels for 5%

profile of v2, /device:TPU:0, one launch (start us, length us, event | category | flops | bytes accessed | tf_op | source)
XLA Modules:
  0.0 559.7 jit_solution(3868271558716733625)
XLA Ops:
  9.7 2.9 collective-permute-start.3
  22.3 3.9 collective-permute-done.4
  41.8 15.3 %collective-permute-done.11.a2 = bf16[2,128,512]{2,1,0:T(8,128)(2,1)S(1)} collective-permute-done((bf16[2,128,512]{2,1,0:T(8,128)(2,1)S(1)}, bf16[2,128,512]{2,1,0:T(8,128)(2,1)S(1)}, u32[]{:S(2)}, u32[]{:S(2)}) %collective-permute-start.11) | collective-permute-done | bytes 262176 | tf_op jit(solution)/shard_map/ppermute | solution.py:532
  62.6 6.3 %finish0.1 = bf16[1024,3072]{1,0:T(8,128)(2,1)} custom-call(bf16[2,128,1536]{2,1,0:T(8,128)(2,1)} %copy-done.17, bf16[2,128,1536]{2,1,0:T(8,128)(2,1)} %copy-done.33, bf16[2,128,1536]{2,1,0:T(8,128)(2,1)} %copy-done.18, bf16[2,128,1536]{2,1,0:T(8,128)(2,1)} %collective-permute-done.8.b2), custom_call_target="tpu_custom_call" | custom-call | bytes 12582912 | tf_op jit(solution)/shard_map/finish0/pallas_call | solution.py:582
  68.9 6.4 %add_convert_fusion = bf16[512,3072]{1,0:T(8,128)(2,1)S(1)} fusion(bf16[512,1024]{1,0:T(8,128)(2,1)S(1)} %fusion.18, bf16[1024,3072]{1,0:T(8,128)(2,1)} %finish0.1, f32[3072]{0:T(1024)S(1)} %bitcast.186), kind=kOutput, calls=%fused_computation.11 | convolution fusion | flops 3224371200 | bytes 10498048 | tf_op jit(solution)/shard_map/dot_general | solution.py:400
  86.9 5.4 collective-permute-done.16
  100.8 7.5 %finish1.1 = bf16[1024,1024]{1,0:T(8,128)(2,1)} custom-call(bf16[2,128,512]{2,1,0:T(8,128)(2,1)} %copy-done.25, bf16[2,128,512]{2,1,0:T(8,128)(2,1)} %copy-done.37, bf16[2,128,512]{2,1,0:T(8,128)(2,1)} %copy-done.26, bf16[2,128,512]{2,1,0:T(8,128)(2,1)} %copy-done.38), custom_call_target="tpu_custom_call" | custom-call | bytes 4194304 | tf_op jit(solution)/shard_map/finish1/pallas_call | solution.py:582
  111.7 7.0 %collective-permute-done.21.b2 = bf16[2,128,2048]{2,1,0:T(8,128)(2,1)} collective-permute-done((bf16[2,128,2048]{2,1,0:T(8,128)(2,1)}, bf16[2,128,2048]{2,1,0:T(8,128)(2,1)}, u32[]{:S(2)}, u32[]{:S(2)}) %collective-permute-start.21) | collective-permute-done | bytes 1048608 | tf_op jit(solution)/shard_map/ppermute | solution.py:532
  120.3 7.8 %finish3.1 = bf16[1024,4096]{1,0:T(8,128)(2,1)} custom-call(bf16[2,128,2048]{2,1,0:T(8,128)(2,1)} %pad_maximum_fusion.4.a01, bf16[2,128,2048]{2,1,0:T(8,128)(2,1)} %collective-permute-done.19.a2, bf16[2,128,2048]{2,1,0:T(8,128)(2,1)} %pad_maximum_fusion.5.b01, bf16[2,128,2048]{2,1,0:T(8,128)(2,1)} %collective-permute-done.21.b2), custom_call_target="tpu_custom_call" | custom-call | bytes 16777216 | tf_op jit(solution)/shard_map/finish3/pallas_call | solution.py:582
  128.1 11.6 %collective-permute-done.17.b2 = bf16[2,128,2048]{2,1,0:T(8,128)(2,1)} collective-permute-done((bf16[2,128,2048]{2,1,0:T(8,128)(2,1)}, bf16[2,128,2048]{2,1,0:T(8,128)(2,1)}, u32[]{:S(2)}, u32[]{:S(2)}) %collective-permute-start.17) | collective-permute-done | bytes 1048608 | tf_op jit(solution)/shard_map/ppermute | solution.py:532
  139.7 2.8 collective-permute-done.15.a2
  142.5 7.8 %finish2.1 = bf16[1024,4096]{1,0:T(8,128)(2,1)} custom-call(bf16[2,128,2048]{2,1,0:T(8,128)(2,1)} %pad_maximum_fusion.2.a01, bf16[2,128,2048]{2,1,0:T(8,128)(2,1)} %collective-permute-done.15.a2, bf16[2,128,2048]{2,1,0:T(8,128)(2,1)} %pad_maximum_fusion.3.b01, bf16[2,128,2048]{2,1,0:T(8,128)(2,1)} %collective-permute-done.17.b2), custom_call_target="tpu_custom_call" | custom-call | bytes 16777216 | tf_op jit(solution)/shard_map/finish2/pallas_call | solution.py:582
  150.3 2.7 fusion.90
  153.1 18.0 %attn_fwd.1 = (bf16[512,1024]{1,0:T(8,128)(2,1)S(1)}, f32[8,8,512]{2,1,0:T(8,128)S(1)}) custom-call(bf16[512,1024]{1,0:T(8,128)(2,1)S(1)} %get-tuple-element.72.q_ref, bf16[512,1024]{1,0:T(8,128)(2,1)S(1)} %get-tuple-element.71.ka_ref, bf16[512,1024]{1,0:T(8,128)(2,1)S(1)} %get-tuple-element.82.kb_ref, bf16[512,1024]{1,0:T(8,128)(2,1)S(1)} %get-tuple-element.70.va_ref, ...), custom_call_target="tpu_custom_call" | custom-call | flops 2147483648 | bytes 6291456 | tf_op jit(solution)/shard_map/attn_fwd/pallas_call | solution.py:425
  174.9 6.9 %fusion.94 = f32[512,4096]{1,0:T(8,128)} fusion(bf16[512,1024]{1,0:T(8,128)(2,1)S(1)} %add_convert_fusion.12, bf16[1024,4096]{1,0:T(8,128)(2,1)S(1)} %copy-done.12), kind=kOutput, calls=%fused_computation.281 | convolution fusion | flops 4294967296 | bytes 17825792 | tf_op jit(solution)/shard_map/dot_general | solution.py:400
  181.8 14.5 %convert_reduce_fusion = (f32[4096]{0:T(1024)}, bf16[512,4096]{1,0:T(8,128)(2,1)}, bf16[512,4096]{1,0:T(8,128)(2,1)S(1)}) fusion(f32[512,4096]{1,0:T(8,128)} %fusion.94, f32[4096]{0:T(1024)S(1)} %bitcast.183, bf16[512,1024]{1,0:T(8,128)(2,1)S(1)} %bitcast.154, bf16[1024,4096]{1,0:T(8,128)(2,1)S(1)} %bitcast.156), kind=kOutput, calls=%fused_computation.9 | convolution fusion | flops 4347392000 | bytes 26247168 | tf_op jit(solution)/shard_map/dot_general | solution.py:400
  196.3 2.7 convolution_convert_fusion.2
  199.4 2.7 convolution_convert_fusion.3
  203.2 8.0 %multiply_reduce_fusion = (f32[1024]{0:T(1024)}, f32[512]{0:T(512)S(1)}, f32[512]{0:T(512)S(1)}, f32[1024]{0:T(1024)}, f32[512,1024]{1,0:T(8,128)S(1)}) fusion(f32[512,1024]{1,0:T(8,128)S(1)} %get-tuple-element.182, f32[512]{0:T(512)S(1)} %add_rsqrt_fusion, f32[512]{0:T(512)S(1)} %broadcast_multiply_fusion.4, f32[1024]{0:T(1024)S(1)} %get-tuple-element.165, ...), kind=kOutput, calls=%fused_computation.52 | convolution fusion | flops 4299682816 | bytes 16797696 | tf_op jit(solution)/shard_map/dot_general | solution.py:400
  211.1 2.8 convert_reduce_fusion.3
  213.9 2.3 convolution_convert_fusion.6.do_ref
  216.2 26.1 %attn_bwd.1 = (bf16[512,1024]{1,0:T(8,128)(2,1)S(1)}, bf16[512,1024]{1,0:T(8,128)(2,1)S(1)}, bf16[512,1024]{1,0:T(8,128)(2,1)S(1)}, bf16[512,1024]{1,0:T(8,128)(2,1)S(1)}, bf16[512,1024]{1,0:T(8,128)(2,1)S(1)}) custom-call(bf16[512,1024]{1,0:T(8,128)(2,1)} %copy-done.3, bf16[512,1024]{1,0:T(8,128)(2,1)} %copy-done.2, bf16[512,1024]{1,0:T(8,128)(2,1)} %copy-done.4, ...), custom_call_target="tpu_custom_call" | custom-call | flops 5368709120 | bytes 13631488 | tf_op jit(solution)/shard_map/attn_bwd/pallas_call | solution.py:465
  245.0 7.7 %add_convert_fusion.11 = bf16[512,1024]{1,0:T(8,128)(2,1)} fusion(f32[512,1024]{1,0:T(8,128)S(1)} %get-tuple-element.182, bf16[512,4096]{1,0:T(8,128)(2,1)} %copy-done.78, bf16[1024,4096]{1,0:T(8,128)(2,1)S(1)} %bitcast.158, f32[1024]{0:T(1024)S(1)} %get-tuple-element.163), kind=kOutput, calls=%fused_computation.63 | convolution fusion | flops 4296540160 | bytes 15732736 | tf_op jit(solution)/shard_map/dot_general | solution.py:400
  255.4 2.6 convolution_convert_fusion.4
  262.3 2.6 convolution_convert_fusion.5
  265.6 2.5 collective-permute-done.42
  277.9 19.3 %collective-permute-done.44 = bf16[128,512]{1,0:T(8,128)(2,1)S(1)} collective-permute-done((bf16[128,512]{1,0:T(8,128)(2,1)S(1)}, bf16[128,512]{1,0:T(8,128)(2,1)S(1)}, u32[]{:S(2)}, u32[]{:S(2)}) %collective-permute-start.44) | collective-permute-done | bytes 131104 | tf_op jit(solution)/shard_map/ppermute | solution.py:536
  297.4 8.3 %collective-permute-done.45 = bf16[128,512]{1,0:T(8,128)(2,1)S(1)} collective-permute-done((bf16[128,512]{1,0:T(8,128)(2,1)S(1)}, bf16[128,512]{1,0:T(8,128)(2,1)S(1)}, u32[]{:S(2)}, u32[]{:S(2)}) %collective-permute-start.45) | collective-permute-done | bytes 131104 | tf_op jit(solution)/shard_map/ppermute | solution.py:536
  307.4 4.4 collective-permute-done.46
  312.7 2.4 add_convert_fusion.5
  315.5 6.9 %fusion.24 = (f32[1024]{0:T(1024)S(1)}, f32[512]{0:T(512)S(1)}, f32[512]{0:T(512)S(1)}, f32[1024]{0:T(1024)S(1)}, f32[512,1024]{1,0:T(8,128)S(1)}) fusion(f32[512]{0:T(512)S(1)} %bitcast.178, f32[512]{0:T(512)S(1)} %bitcast.181, bf16[2,256,1024]{2,1,0:T(8,128)(2,1)S(1)} %copy-done.7, f32[1024]{0:T(1024)S(1)} %copy-done.63, bf16[1024,3072]{1,0:T(8,128)(2,1)} %finish0.1, ...), kind=kOutput, calls=%fused_computation.46 | convolution fusion | flops 3232756736 | bytes 12603392 | tf_op jit(solution)/shard_map/dot_general | solution.py:400
  323.1 2.9 add_convert_fusion.1
  338.0 39.4 %collective-permute-done.66 = f32[8,1536]{1,0:T(8,128)S(1)} collective-permute-done((f32[8,1536]{1,0:T(8,128)S(1)}, f32[8,1536]{1,0:T(8,128)S(1)}, u32[]{:S(2)}, u32[]{:S(2)}) %collective-permute-start.66) | collective-permute-done | bytes 49184 | tf_op jit(solution)/shard_map/ppermute | solution.py:532
  379.2 2.3 collective-permute-done.67
  383.0 2.7 collective-permute-done.68
  387.9 3.4 collective-permute-done.69
  395.7 19.9 %collective-permute-start.29 = (bf16[512,1536]{1,0:T(8,128)(2,1)S(1)}, bf16[512,1536]{1,0:T(8,128)(2,1)S(1)}, u32[]{:S(2)}, u32[]{:S(2)}) collective-permute-start(bf16[512,1536]{1,0:T(8,128)(2,1)S(1)} %convolution_convert_fusion.1), channel_id=1, source_target_pairs={{0,4},{4,0},{8,12},{12,8},{16,20},{20,16},{24,28},{28,24},{1,5},{5... | collective-permute-start | bytes 4718600 | tf_op jit(solution)/shard_map/ppermute | solution.py:532
  420.1 10.4 %collective-permute-done.58 = bf16[128,2048]{1,0:T(8,128)(2,1)S(1)} collective-permute-done((bf16[128,2048]{1,0:T(8,128)(2,1)S(1)}, bf16[128,2048]{1,0:T(8,128)(2,1)S(1)}, u32[]{:S(2)}, u32[]{:S(2)}) %collective-permute-start.58) | collective-permute-done | bytes 524320 | tf_op jit(solution)/shard_map/ppermute | solution.py:532
  430.9 9.8 %collective-permute-done.49 = bf16[128,2048]{1,0:T(8,128)(2,1)S(1)} collective-permute-done((bf16[128,2048]{1,0:T(8,128)(2,1)S(1)}, bf16[128,2048]{1,0:T(8,128)(2,1)S(1)}, u32[]{:S(2)}, u32[]{:S(2)}) %collective-permute-start.49) | collective-permute-done | bytes 524320 | tf_op jit(solution)/shard_map/ppermute | solution.py:532
  445.8 3.4 collective-permute-start.63
  449.2 11.7 %collective-permute-done.53 = bf16[128,2048]{1,0:T(8,128)(2,1)S(1)} collective-permute-done((bf16[128,2048]{1,0:T(8,128)(2,1)S(1)}, bf16[128,2048]{1,0:T(8,128)(2,1)S(1)}, u32[]{:S(2)}, u32[]{:S(2)}) %collective-permute-start.53) | collective-permute-done | bytes 524320 | tf_op jit(solution)/shard_map/ppermute | solution.py:536
  462.6 2.7 collective-permute-start.31
  465.3 19.2 %collective-permute-done.63 = bf16[128,2048]{1,0:T(8,128)(2,1)S(1)} collective-permute-done((bf16[128,2048]{1,0:T(8,128)(2,1)S(1)}, bf16[128,2048]{1,0:T(8,128)(2,1)S(1)}, u32[]{:S(2)}, u32[]{:S(2)}) %collective-permute-start.63) | collective-permute-done | bytes 524320 | tf_op jit(solution)/shard_map/ppermute | solution.py:536
  484.8 9.2 %collective-permute-done.54 = bf16[128,2048]{1,0:T(8,128)(2,1)S(1)} collective-permute-done((bf16[128,2048]{1,0:T(8,128)(2,1)S(1)}, bf16[128,2048]{1,0:T(8,128)(2,1)S(1)}, u32[]{:S(2)}, u32[]{:S(2)}) %collective-permute-start.54) | collective-permute-done | bytes 524320 | tf_op jit(solution)/shard_map/ppermute | solution.py:536
  497.2 8.0 %collective-permute-done.64 = bf16[128,2048]{1,0:T(8,128)(2,1)S(1)} collective-permute-done((bf16[128,2048]{1,0:T(8,128)(2,1)S(1)}, bf16[128,2048]{1,0:T(8,128)(2,1)S(1)}, u32[]{:S(2)}, u32[]{:S(2)}) %collective-permute-start.64) | collective-permute-done | bytes 524320 | tf_op jit(solution)/shard_map/ppermute | solution.py:536
  507.3 17.6 %collective-permute-done.35 = bf16[128,1536]{1,0:T(8,128)(2,1)} collective-permute-done((bf16[128,1536]{1,0:T(8,128)(2,1)}, bf16[128,1536]{1,0:T(8,128)(2,1)}, u32[]{:S(2)}, u32[]{:S(2)}) %collective-permute-start.35) | collective-permute-done | bytes 393248 | tf_op jit(solution)/shard_map/ppermute | solution.py:536
  528.1 18.5 %collective-permute-done.36 = bf16[128,1536]{1,0:T(8,128)(2,1)S(1)} collective-permute-done((bf16[128,1536]{1,0:T(8,128)(2,1)S(1)}, bf16[128,1536]{1,0:T(8,128)(2,1)S(1)}, u32[]{:S(2)}, u32[]{:S(2)}) %collective-permute-start.36) | collective-permute-done | bytes 393248 | tf_op jit(solution)/shard_map/ppermute | solution.py:536
  548.4 9.5 %collective-permute-done.37 = bf16[128,1536]{1,0:T(8,128)(2,1)S(1)} collective-permute-done((bf16[128,1536]{1,0:T(8,128)(2,1)S(1)}, bf16[128,1536]{1,0:T(8,128)(2,1)S(1)}, u32[]{:S(2)}, u32[]{:S(2)}) %collective-permute-start.37) | collective-permute-done | bytes 393248 | tf_op jit(solution)/shard_map/ppermute | solution.py:536
  (432 shorter events, 138.5 us)
Async XLA Ops:
  18.0 20.6 %collective-permute-start = (bf16[256,1024]{1,0:T(8,128)(2,1)}, bf16[256,1024]{1,0:T(8,128)(2,1)S(1)}, u32[]{:S(2)}, u32[]{:S(2)}) collective-permute-start(bf16[256,1024]{1,0:T(8,128)(2,1)} %get-tuple-element.138), channel_id=1, source_target_pairs={{0,0},{1,1},{2,4},{3,5},{4,2},{5,3},{6,6},{7,7},{8,8},{9,9},{10,12... | collective-permute-start | bytes 1572872 | tf_op jit(solution)/shard_map/ppermute | solution.py:488
  19.6 19.5 %collective-permute-start.1 = (bf16[256,1024]{1,0:T(8,128)(2,1)}, bf16[256,1024]{1,0:T(8,128)(2,1)}, u32[]{:S(2)}, u32[]{:S(2)}) collective-permute-start(bf16[256,1024]{1,0:T(8,128)(2,1)} %get-tuple-element.137), channel_id=1, source_target_pairs={{0,1},{1,0},{2,5},{3,4},{4,3},{5,2},{6,7},{7,6},{8,9},{9,8},{10,13... | collective-permute-start | bytes 1572872 | tf_op jit(solution)/shard_map/ppermute | solution.py:488
  32.2 29.5 %collective-permute-start.6 = (bf16[2,128,1536]{2,1,0:T(8,128)(2,1)S(1)}, bf16[2,128,1536]{2,1,0:T(8,128)(2,1)S(1)}, u32[]{:S(2)}, u32[]{:S(2)}) collective-permute-start(bf16[2,128,1536]{2,1,0:T(8,128)(2,1)S(1)} %pad_maximum_fusion.8.a01), channel_id=1, source_target_pairs={{0,16},{4,20},{8,24},{12,28},{16,0},{20,4},{24,8},{28,12},{1,17},{... | collective-permute-start | bytes 2359304 | tf_op jit(solution)/shard_map/ppermute | solution.py:532
  34.0 28.7 %collective-permute-start.8 = (bf16[2,128,1536]{2,1,0:T(8,128)(2,1)S(1)}, bf16[2,128,1536]{2,1,0:T(8,128)(2,1)}, u32[]{:S(2)}, u32[]{:S(2)}) collective-permute-start(bf16[2,128,1536]{2,1,0:T(8,128)(2,1)S(1)} %pad_maximum_fusion.9.b01), channel_id=1, source_target_pairs={{0,8},{4,12},{8,0},{12,4},{16,24},{20,28},{24,16},{28,20},{1,9},{5... | collective-permute-start | bytes 2359304 | tf_op jit(solution)/shard_map/ppermute | solution.py:532
  37.0 20.1 %collective-permute-start.11 = (bf16[2,128,512]{2,1,0:T(8,128)(2,1)S(1)}, bf16[2,128,512]{2,1,0:T(8,128)(2,1)S(1)}, u32[]{:S(2)}, u32[]{:S(2)}) collective-permute-start(bf16[2,128,512]{2,1,0:T(8,128)(2,1)S(1)} %pad_maximum_fusion.19.a01), channel_id=1, source_target_pairs={{0,16},{4,20},{8,24},{12,28},{16,0},{20,4},{24,8},{28,12},{1,17},{... | collective-permute-start | bytes 786440 | tf_op jit(solution)/shard_map/ppermute | solution.py:532
  38.6 18.8 %collective-permute-start.13 = (bf16[2,128,512]{2,1,0:T(8,128)(2,1)S(1)}, bf16[2,128,512]{2,1,0:T(8,128)(2,1)S(1)}, u32[]{:S(2)}, u32[]{:S(2)}) collective-permute-start(bf16[2,128,512]{2,1,0:T(8,128)(2,1)S(1)} %pad_maximum_fusion.20.b01), channel_id=1, source_target_pairs={{0,8},{4,12},{8,0},{12,4},{16,24},{20,28},{24,16},{28,20},{1,9},{5... | collective-permute-start | bytes 786440 | tf_op jit(solution)/shard_map/ppermute | solution.py:532
  58.7 21.0 %collective-permute-start.20 = (bf16[128,2048]{1,0:T(8,128)(2,1)}, bf16[128,2048]{1,0:T(8,128)(2,1)}, u32[]{:S(2)}, u32[]{:S(2)}) collective-permute-start(bf16[128,2048]{1,0:T(8,128)(2,1)} %get-tuple-element.131), channel_id=1, source_target_pairs={{0,16},{4,20},{8,24},{12,28},{16,0},{20,4},{24,8},{28,12},{1,17},{... | collective-permute-start | bytes 1572872 | tf_op jit(solution)/shard_map/ppermute | solution.py:532
  60.2 22.2 %collective-permute-start.18 = (bf16[128,2048]{1,0:T(8,128)(2,1)}, bf16[128,2048]{1,0:T(8,128)(2,1)S(1)}, u32[]{:S(2)}, u32[]{:S(2)}) collective-permute-start(bf16[128,2048]{1,0:T(8,128)(2,1)} %get-tuple-element.132), channel_id=1, source_target_pairs={{0,8},{4,12},{8,0},{12,4},{16,24},{20,28},{24,16},{28,20},{1,9},{5... | collective-permute-start | bytes 1572872 | tf_op jit(solution)/shard_map/ppermute | solution.py:532
  77.7 72.6 %collective-permute-start.9 = (bf16[512,2048]{1,0:T(8,128)(2,1)}, bf16[512,2048]{1,0:T(8,128)(2,1)}, u32[]{:S(2)}, u32[]{:S(2)}) collective-permute-start(bf16[512,2048]{1,0:T(8,128)(2,1)} %slice.374), channel_id=1, source_target_pairs={{0,4},{4,0},{8,12},{12,8},{16,20},{20,16},{24,28},{28,24},{1,5},{5... | collective-permute-start | bytes 6291464 | tf_op jit(solution)/shard_map/ppermute | solution.py:506
  78.1 14.3 %collective-permute-start.16 = (bf16[128,2048]{1,0:T(8,128)(2,1)S(1)}, bf16[128,2048]{1,0:T(8,128)(2,1)S(1)}, u32[]{:S(2)}, u32[]{:S(2)}) collective-permute-start(bf16[128,2048]{1,0:T(8,128)(2,1)S(1)} %get-tuple-element.135), channel_id=1, source_target_pairs={{0,16},{4,20},{8,24},{12,28},{16,0},{20,4},{24,8},{28,12},{1,17},{... | collective-permute-start | bytes 1572872 | tf_op jit(solution)/shard_map/ppermute | solution.py:532
  79.0 16.6 %collective-permute-start.24 = (bf16[256,1024]{1,0:T(8,128)(2,1)S(1)}, bf16[256,1024]{1,0:T(8,128)(2,1)S(1)}, u32[]{:S(2)}, u32[]{:S(2)}) collective-permute-start(bf16[256,1024]{1,0:T(8,128)(2,1)S(1)} %get-tuple-element.126), channel_id=1, source_target_pairs={{0,0},{1,1},{2,4},{3,5},{4,2},{5,3},{6,6},{7,7},{8,8},{9,9},{10,12... | collective-permute-start | bytes 1572872 | tf_op jit(solution)/shard_map/ppermute | solution.py:488
  79.7 14.2 %collective-permute-start.14 = (bf16[128,2048]{1,0:T(8,128)(2,1)S(1)}, bf16[128,2048]{1,0:T(8,128)(2,1)S(1)}, u32[]{:S(2)}, u32[]{:S(2)}) collective-permute-start(bf16[128,2048]{1,0:T(8,128)(2,1)S(1)} %get-tuple-element.136), channel_id=1, source_target_pairs={{0,8},{4,12},{8,0},{12,4},{16,24},{20,28},{24,16},{28,20},{1,9},{5... | collective-permute-start | bytes 1572872 | tf_op jit(solution)/shard_map/ppermute | solution.py:532
  83.2 14.6 %collective-permute-start.25 = (bf16[256,1024]{1,0:T(8,128)(2,1)S(1)}, bf16[256,1024]{1,0:T(8,128)(2,1)S(1)}, u32[]{:S(2)}, u32[]{:S(2)}) collective-permute-start(bf16[256,1024]{1,0:T(8,128)(2,1)S(1)} %get-tuple-element.125), channel_id=1, source_target_pairs={{0,1},{1,0},{2,5},{3,4},{4,3},{5,2},{6,7},{7,6},{8,9},{9,8},{10,13... | collective-permute-start | bytes 1572872 | tf_op jit(solution)/shard_map/ppermute | solution.py:488
  92.3 26.3 %collective-permute-start.21 = (bf16[2,128,2048]{2,1,0:T(8,128)(2,1)}, bf16[2,128,2048]{2,1,0:T(8,128)(2,1)}, u32[]{:S(2)}, u32[]{:S(2)}) collective-permute-start(bf16[2,128,2048]{2,1,0:T(8,128)(2,1)} %pad_maximum_fusion.5.b01), channel_id=1, source_target_pairs={{0,8},{4,12},{8,0},{12,4},{16,24},{20,28},{24,16},{28,20},{1,9},{5... | collective-permute-start | bytes 3145736 | tf_op jit(solution)/shard_map/ppermute | solution.py:532
  93.9 26.3 %collective-permute-start.19 = (bf16[2,128,2048]{2,1,0:T(8,128)(2,1)}, bf16[2,128,2048]{2,1,0:T(8,128)(2,1)}, u32[]{:S(2)}, u32[]{:S(2)}) collective-permute-start(bf16[2,128,2048]{2,1,0:T(8,128)(2,1)} %pad_maximum_fusion.4.a01), channel_id=1, source_target_pairs={{0,16},{4,20},{8,24},{12,28},{16,0},{20,4},{24,8},{28,12},{1,17},{... | collective-permute-start | bytes 3145736 | tf_op jit(solution)/shard_map/ppermute | solution.py:532
  95.6 44.1 %collective-permute-start.17 = (bf16[2,128,2048]{2,1,0:T(8,128)(2,1)}, bf16[2,128,2048]{2,1,0:T(8,128)(2,1)}, u32[]{:S(2)}, u32[]{:S(2)}) collective-permute-start(bf16[2,128,2048]{2,1,0:T(8,128)(2,1)} %pad_maximum_fusion.3.b01), channel_id=1, source_target_pairs={{0,8},{4,12},{8,0},{12,4},{16,24},{20,28},{24,16},{28,20},{1,9},{5... | collective-permute-start | bytes 3145736 | tf_op jit(solution)/shard_map/ppermute | solution.py:532
  97.8 44.7 %collective-permute-start.15 = (bf16[2,128,2048]{2,1,0:T(8,128)(2,1)}, bf16[2,128,2048]{2,1,0:T(8,128)(2,1)}, u32[]{:S(2)}, u32[]{:S(2)}) collective-permute-start(bf16[2,128,2048]{2,1,0:T(8,128)(2,1)} %pad_maximum_fusion.2.a01), channel_id=1, source_target_pairs={{0,16},{4,20},{8,24},{12,28},{16,0},{20,4},{24,8},{28,12},{1,17},{... | collective-permute-start | bytes 3145736 | tf_op jit(solution)/shard_map/ppermute | solution.py:532
  243.8 68.8 %collective-permute-start.26 = (bf16[512,2048]{1,0:T(8,128)(2,1)}, bf16[512,2048]{1,0:T(8,128)(2,1)}, u32[]{:S(2)}, u32[]{:S(2)}) collective-permute-start(bf16[512,2048]{1,0:T(8,128)(2,1)} %pad_maximum_fusion), channel_id=1, source_target_pairs={{0,4},{4,0},{8,12},{12,8},{16,20},{20,16},{24,28},{28,24},{1,5},{5... | collective-permute-start | bytes 6291464 | tf_op jit(solution)/shard_map/ppermute | solution.py:506
  244.0 79.1 %collective-permute-start.59 = (bf16[512,2048]{1,0:T(8,128)(2,1)}, bf16[512,2048]{1,0:T(8,128)(2,1)}, u32[]{:S(2)}, u32[]{:S(2)}) collective-permute-start(bf16[512,2048]{1,0:T(8,128)(2,1)} %convolution_convert_fusion.2), channel_id=1, source_target_pairs={{0,4},{4,0},{8,12},{12,8},{16,20},{20,16},{24,28},{28,24},{1,5},{5... | collective-permute-start | bytes 6291464 | tf_op jit(solution)/shard_map/ppermute | solution.py:532
  272.3 33.3 %collective-permute-start.22 = (bf16[256,1024]{1,0:T(8,128)(2,1)S(1)}, bf16[256,1024]{1,0:T(8,128)(2,1)S(1)}, u32[]{:S(2)}, u32[]{:S(2)}) collective-permute-start(bf16[256,1024]{1,0:T(8,128)(2,1)S(1)} %get-tuple-element.127), channel_id=1, source_target_pairs={{0,0},{1,1},{4,2},{5,3},{2,4},{3,5},{6,6},{7,7},{8,8},{9,9},{12,10... | collective-permute-start | bytes 1572872 | tf_op jit(solution)/shard_map/ppermute | solution.py:501
  274.3 32.0 %collective-permute-start.23 = (bf16[256,1024]{1,0:T(8,128)(2,1)S(1)}, bf16[256,1024]{1,0:T(8,128)(2,1)S(1)}, u32[]{:S(2)}, u32[]{:S(2)}) collective-permute-start(bf16[256,1024]{1,0:T(8,128)(2,1)S(1)} %get-tuple-element.128), channel_id=1, source_target_pairs={{1,0},{0,1},{5,2},{4,3},{3,4},{2,5},{7,6},{6,7},{9,8},{8,9},{13,10... | collective-permute-start | bytes 1572872 | tf_op jit(solution)/shard_map/ppermute | solution.py:501
  276.0 21.2 %collective-permute-start.44 = (bf16[128,512]{1,0:T(8,128)(2,1)S(1)}, bf16[128,512]{1,0:T(8,128)(2,1)S(1)}, u32[]{:S(2)}, u32[]{:S(2)}) collective-permute-start(bf16[128,512]{1,0:T(8,128)(2,1)S(1)} %broadcast_select_fusion.11), channel_id=1, source_target_pairs={{0,1},{1,0},{2,3},{3,2},{4,5},{5,4},{6,7},{7,6},{8,9},{9,8},{10,11... | collective-permute-start | bytes 393224 | tf_op jit(solution)/shard_map/ppermute | solution.py:536
  305.7 21.7 %collective-permute-start.56 = (bf16[512,2048]{1,0:T(8,128)(2,1)S(1)}, bf16[512,2048]{1,0:T(8,128)(2,1)S(1)}, u32[]{:S(2)}, u32[]{:S(2)}) collective-permute-start(bf16[512,2048]{1,0:T(8,128)(2,1)S(1)} %copy-done.73), channel_id=1, source_target_pairs={{0,4},{4,0},{8,12},{12,8},{16,20},{20,16},{24,28},{28,24},{1,5},{5... | collective-permute-start | bytes 6291464 | tf_op jit(solution)/shard_map/ppermute | solution.py:532
  305.7 24.3 %collective-permute-start.50 = (bf16[512,2048]{1,0:T(8,128)(2,1)S(1)}, bf16[512,2048]{1,0:T(8,128)(2,1)S(1)}, u32[]{:S(2)}, u32[]{:S(2)}) collective-permute-start(bf16[512,2048]{1,0:T(8,128)(2,1)S(1)} %copy-done.74), channel_id=1, source_target_pairs={{0,4},{4,0},{8,12},{12,8},{16,20},{20,16},{24,28},{28,24},{1,5},{5... | collective-permute-start | bytes 6291464 | tf_op jit(solution)/shard_map/ppermute | solution.py:532
  311.8 21.4 %collective-permute-start.47 = (bf16[512,2048]{1,0:T(8,128)(2,1)S(1)}, bf16[512,2048]{1,0:T(8,128)(2,1)S(1)}, u32[]{:S(2)}, u32[]{:S(2)}) collective-permute-start(bf16[512,2048]{1,0:T(8,128)(2,1)S(1)} %copy-done.75), channel_id=1, source_target_pairs={{0,4},{4,0},{8,12},{12,8},{16,20},{20,16},{24,28},{28,24},{1,5},{5... | collective-permute-start | bytes 6291464 | tf_op jit(solution)/shard_map/ppermute | solution.py:532
  326.0 66.5 %collective-permute-start.60 = (bf16[256,2048]{1,0:T(8,128)(2,1)S(1)}, bf16[256,2048]{1,0:T(8,128)(2,1)S(1)}, u32[]{:S(2)}, u32[]{:S(2)}) collective-permute-start(bf16[256,2048]{1,0:T(8,128)(2,1)S(1)} %slice.427), channel_id=1, source_target_pairs={{0,16},{4,20},{8,24},{12,28},{16,0},{20,4},{24,8},{28,12},{1,17},{... | collective-permute-start | bytes 3145736 | tf_op jit(solution)/shard_map/ppermute | solution.py:532
  328.9 65.5 %collective-permute-start.57 = (bf16[256,2048]{1,0:T(8,128)(2,1)S(1)}, bf16[256,2048]{1,0:T(8,128)(2,1)S(1)}, u32[]{:S(2)}, u32[]{:S(2)}) collective-permute-start(bf16[256,2048]{1,0:T(8,128)(2,1)S(1)} %pad_maximum_fusion.7), channel_id=1, source_target_pairs={{0,8},{4,12},{8,0},{12,4},{16,24},{20,28},{24,16},{28,20},{1,9},{5... | collective-permute-start | bytes 3145736 | tf_op jit(solution)/shard_map/ppermute | solution.py:532
  332.3 61.4 %collective-permute-start.51 = (bf16[256,2048]{1,0:T(8,128)(2,1)S(1)}, bf16[256,2048]{1,0:T(8,128)(2,1)S(1)}, u32[]{:S(2)}, u32[]{:S(2)}) collective-permute-start(bf16[256,2048]{1,0:T(8,128)(2,1)S(1)} %slice.415), channel_id=1, source_target_pairs={{0,16},{4,20},{8,24},{12,28},{16,0},{20,4},{24,8},{28,12},{1,17},{... | collective-permute-start | bytes 3145736 | tf_op jit(solution)/shard_map/ppermute | solution.py:532
  334.7 80.9 %collective-permute-start.48 = (bf16[256,2048]{1,0:T(8,128)(2,1)S(1)}, bf16[256,2048]{1,0:T(8,128)(2,1)S(1)}, u32[]{:S(2)}, u32[]{:S(2)}) collective-permute-start(bf16[256,2048]{1,0:T(8,128)(2,1)S(1)} %pad_maximum_fusion.6), channel_id=1, source_target_pairs={{0,8},{4,12},{8,0},{12,4},{16,24},{20,28},{24,16},{28,20},{1,9},{5... | collective-permute-start | bytes 3145736 | tf_op jit(solution)/shard_map/ppermute | solution.py:532
  335.8 41.6 %collective-permute-start.66 = (f32[8,1536]{1,0:T(8,128)S(1)}, f32[8,1536]{1,0:T(8,128)S(1)}, u32[]{:S(2)}, u32[]{:S(2)}) collective-permute-start(f32[8,1536]{1,0:T(8,128)S(1)} %add.370), channel_id=1, source_target_pairs={{0,8},{4,12},{8,0},{12,4},{16,24},{20,28},{24,16},{28,20},{1,9},{5... | collective-permute-start | bytes 147464 | tf_op jit(solution)/shard_map/ppermute | solution.py:532
  391.3 49.9 %collective-permute-start.32 = (bf16[512,1536]{1,0:T(8,128)(2,1)S(1)}, bf16[512,1536]{1,0:T(8,128)(2,1)S(1)}, u32[]{:S(2)}, u32[]{:S(2)}) collective-permute-start(bf16[512,1536]{1,0:T(8,128)(2,1)S(1)} %convolution_convert_fusion), channel_id=1, source_target_pairs={{0,4},{4,0},{8,12},{12,8},{16,20},{20,16},{24,28},{28,24},{1,5},{5... | collective-permute-start | bytes 4718600 | tf_op jit(solution)/shard_map/ppermute | solution.py:532
  393.7 23.0 %collective-permute-start.28 = (bf16[256,1024]{1,0:T(8,128)(2,1)S(1)}, bf16[256,1024]{1,0:T(8,128)(2,1)S(1)}, u32[]{:S(2)}, u32[]{:S(2)}) collective-permute-start(bf16[256,1024]{1,0:T(8,128)(2,1)S(1)} %get-tuple-element.124), channel_id=1, source_target_pairs={{1,0},{0,1},{5,2},{4,3},{3,4},{2,5},{7,6},{6,7},{9,8},{8,9},{13,10... | collective-permute-start | bytes 1572872 | tf_op jit(solution)/shard_map/ppermute | solution.py:501
  394.5 23.6 %collective-permute-start.61 = (bf16[128,2048]{1,0:T(8,128)(2,1)S(1)}, bf16[128,2048]{1,0:T(8,128)(2,1)S(1)}, u32[]{:S(2)}, u32[]{:S(2)}) collective-permute-start(bf16[128,2048]{1,0:T(8,128)(2,1)S(1)} %slice.429), channel_id=1, source_target_pairs={{0,8},{4,12},{8,0},{12,4},{16,24},{20,28},{24,16},{28,20},{1,9},{5... | collective-permute-start | bytes 1572872 | tf_op jit(solution)/shard_map/ppermute | solution.py:532
  395.7 47.1 %collective-permute-start.29 = (bf16[512,1536]{1,0:T(8,128)(2,1)S(1)}, bf16[512,1536]{1,0:T(8,128)(2,1)S(1)}, u32[]{:S(2)}, u32[]{:S(2)}) collective-permute-start(bf16[512,1536]{1,0:T(8,128)(2,1)S(1)} %convolution_convert_fusion.1), channel_id=1, source_target_pairs={{0,4},{4,0},{8,12},{12,8},{16,20},{20,16},{24,28},{28,24},{1,5},{5... | collective-permute-start | bytes 4718600 | tf_op jit(solution)/shard_map/ppermute | solution.py:532
  415.6 14.8 %collective-permute-start.58 = (bf16[128,2048]{1,0:T(8,128)(2,1)S(1)}, bf16[128,2048]{1,0:T(8,128)(2,1)S(1)}, u32[]{:S(2)}, u32[]{:S(2)}) collective-permute-start(bf16[128,2048]{1,0:T(8,128)(2,1)S(1)} %slice.424), channel_id=1, source_target_pairs={{0,16},{4,20},{8,24},{12,28},{16,0},{20,4},{24,8},{28,12},{1,17},{... | collective-permute-start | bytes 1572872 | tf_op jit(solution)/shard_map/ppermute | solution.py:532
  418.1 22.7 %collective-permute-start.49 = (bf16[128,2048]{1,0:T(8,128)(2,1)S(1)}, bf16[128,2048]{1,0:T(8,128)(2,1)S(1)}, u32[]{:S(2)}, u32[]{:S(2)}) collective-permute-start(bf16[128,2048]{1,0:T(8,128)(2,1)S(1)} %slice.412), channel_id=1, source_target_pairs={{0,16},{4,20},{8,24},{12,28},{16,0},{20,4},{24,8},{28,12},{1,17},{... | collective-permute-start | bytes 1572872 | tf_op jit(solution)/shard_map/ppermute | solution.py:532
  430.8 14.6 %collective-permute-start.62 = (bf16[128,2048]{1,0:T(8,128)(2,1)S(1)}, bf16[128,2048]{1,0:T(8,128)(2,1)S(1)}, u32[]{:S(2)}, u32[]{:S(2)}) collective-permute-start(bf16[128,2048]{1,0:T(8,128)(2,1)S(1)} %broadcast_select_fusion.2), channel_id=1, source_target_pairs={{0,1},{1,0},{2,3},{3,2},{4,5},{5,4},{6,7},{7,6},{8,9},{9,8},{10,11... | collective-permute-start | bytes 1572872 | tf_op jit(solution)/shard_map/ppermute | solution.py:536
  441.1 19.9 %collective-permute-start.53 = (bf16[128,2048]{1,0:T(8,128)(2,1)S(1)}, bf16[128,2048]{1,0:T(8,128)(2,1)S(1)}, u32[]{:S(2)}, u32[]{:S(2)}) collective-permute-start(bf16[128,2048]{1,0:T(8,128)(2,1)S(1)} %broadcast_select_fusion.5), channel_id=1, source_target_pairs={{0,1},{1,0},{2,3},{3,2},{4,5},{5,4},{6,7},{7,6},{8,9},{9,8},{10,11... | collective-permute-start | bytes 1572872 | tf_op jit(solution)/shard_map/ppermute | solution.py:536
  442.3 19.2 %collective-permute-start.33 = (bf16[256,1536]{1,0:T(8,128)(2,1)S(1)}, bf16[256,1536]{1,0:T(8,128)(2,1)S(1)}, u32[]{:S(2)}, u32[]{:S(2)}) collective-permute-start(bf16[256,1536]{1,0:T(8,128)(2,1)S(1)} %slice.391), channel_id=1, source_target_pairs={{0,16},{4,20},{8,24},{12,28},{16,0},{20,4},{24,8},{28,12},{1,17},{... | collective-permute-start | bytes 2359304 | tf_op jit(solution)/shard_map/ppermute | solution.py:532
  444.0 18.4 %collective-permute-start.30 = (bf16[256,1536]{1,0:T(8,128)(2,1)S(1)}, bf16[256,1536]{1,0:T(8,128)(2,1)S(1)}, u32[]{:S(2)}, u32[]{:S(2)}) collective-permute-start(bf16[256,1536]{1,0:T(8,128)(2,1)S(1)} %pad_maximum_fusion.10), channel_id=1, source_target_pairs={{0,8},{4,12},{8,0},{12,4},{16,24},{20,28},{24,16},{28,20},{1,9},{5... | collective-permute-start | bytes 2359304 | tf_op jit(solution)/shard_map/ppermute | solution.py:532
  445.8 38.7 %collective-permute-start.63 = (bf16[128,2048]{1,0:T(8,128)(2,1)S(1)}, bf16[128,2048]{1,0:T(8,128)(2,1)S(1)}, u32[]{:S(2)}, u32[]{:S(2)}) collective-permute-start(bf16[128,2048]{1,0:T(8,128)(2,1)S(1)} %add_convert_fusion.16), channel_id=1, source_target_pairs={{0,2},{1,3},{2,0},{3,1},{4,6},{5,7},{6,4},{7,5},{8,10},{9,11},{10,... | collective-permute-start | bytes 1572872 | tf_op jit(solution)/shard_map/ppermute | solution.py:536
  461.4 32.6 %collective-permute-start.54 = (bf16[128,2048]{1,0:T(8,128)(2,1)S(1)}, bf16[128,2048]{1,0:T(8,128)(2,1)S(1)}, u32[]{:S(2)}, u32[]{:S(2)}) collective-permute-start(bf16[128,2048]{1,0:T(8,128)(2,1)S(1)} %add_convert_fusion.20), channel_id=1, source_target_pairs={{0,2},{1,3},{2,0},{3,1},{4,6},{5,7},{6,4},{7,5},{8,10},{9,11},{10,... | collective-permute-start | bytes 1572872 | tf_op jit(solution)/shard_map/ppermute | solution.py:536
  461.7 32.5 %collective-permute-start.34 = (bf16[128,1536]{1,0:T(8,128)(2,1)S(1)}, bf16[128,1536]{1,0:T(8,128)(2,1)S(1)}, u32[]{:S(2)}, u32[]{:S(2)}) collective-permute-start(bf16[128,1536]{1,0:T(8,128)(2,1)S(1)} %slice.393), channel_id=1, source_target_pairs={{0,8},{4,12},{8,0},{12,4},{16,24},{20,28},{24,16},{28,20},{1,9},{5... | collective-permute-start | bytes 1179656 | tf_op jit(solution)/shard_map/ppermute | solution.py:532
  462.6 31.6 %collective-permute-start.31 = (bf16[128,1536]{1,0:T(8,128)(2,1)S(1)}, bf16[128,1536]{1,0:T(8,128)(2,1)S(1)}, u32[]{:S(2)}, u32[]{:S(2)}) collective-permute-start(bf16[128,1536]{1,0:T(8,128)(2,1)S(1)} %slice.389), channel_id=1, source_target_pairs={{0,16},{4,20},{8,24},{12,28},{16,0},{20,4},{24,8},{28,12},{1,17},{... | collective-permute-start | bytes 1179656 | tf_op jit(solution)/shard_map/ppermute | solution.py:532
  484.7 20.5 %collective-permute-start.64 = (bf16[128,2048]{1,0:T(8,128)(2,1)S(1)}, bf16[128,2048]{1,0:T(8,128)(2,1)S(1)}, u32[]{:S(2)}, u32[]{:S(2)}) collective-permute-start(bf16[128,2048]{1,0:T(8,128)(2,1)S(1)} %add_convert_fusion.15), channel_id=1, source_target_pairs={{0,1},{1,0},{2,3},{3,2},{4,5},{5,4},{6,7},{7,6},{8,9},{9,8},{10,11... | collective-permute-start | bytes 1572872 | tf_op jit(solution)/shard_map/ppermute | solution.py:536
  494.1 32.9 %collective-permute-start.55 = (bf16[128,2048]{1,0:T(8,128)(2,1)S(1)}, bf16[128,2048]{1,0:T(8,128)(2,1)}, u32[]{:S(2)}, u32[]{:S(2)}) collective-permute-start(bf16[128,2048]{1,0:T(8,128)(2,1)S(1)} %add_convert_fusion.19), channel_id=1, source_target_pairs={{0,1},{1,0},{2,3},{3,2},{4,5},{5,4},{6,7},{7,6},{8,9},{9,8},{10,11... | collective-permute-start | bytes 1572872 | tf_op jit(solution)/shard_map/ppermute | solution.py:536
  495.2 29.7 %collective-permute-start.35 = (bf16[128,1536]{1,0:T(8,128)(2,1)}, bf16[128,1536]{1,0:T(8,128)(2,1)}, u32[]{:S(2)}, u32[]{:S(2)}) collective-permute-start(bf16[128,1536]{1,0:T(8,128)(2,1)} %broadcast_select_fusion.8), channel_id=1, source_target_pairs={{0,1},{1,0},{2,3},{3,2},{4,5},{5,4},{6,7},{7,6},{8,9},{9,8},{10,11... | collective-permute-start | bytes 1179656 | tf_op jit(solution)/shard_map/ppermute | solution.py:536
  526.5 20.2 %collective-permute-start.36 = (bf16[128,1536]{1,0:T(8,128)(2,1)S(1)}, bf16[128,1536]{1,0:T(8,128)(2,1)S(1)}, u32[]{:S(2)}, u32[]{:S(2)}) collective-permute-start(bf16[128,1536]{1,0:T(8,128)(2,1)S(1)} %add_convert_fusion.26), channel_id=1, source_target_pairs={{0,2},{1,3},{2,0},{3,1},{4,6},{5,7},{6,4},{7,5},{8,10},{9,11},{10,... | collective-permute-start | bytes 1179656 | tf_op jit(solution)/shard_map/ppermute | solution.py:536
  (108 other events, 1181.6 us)

commit v3 on v2

--- a/solution.py
+++ b/solution.py
@@ -607,39 +607,352 @@
     )
 
 
-def to_sibling(odd, right):
-    half = right.shape[1] // 2
-    return [flip(dg(odd, right[:, i * half : (i + 1) * half], TN).astype(BF16), 1) for i in range(2)]
-
-
-def f32_add(left, right):
-    return left.astype(F32) + right.astype(F32)
-
-
-def low_add(left, right):
-    return f32_add(left, right).astype(BF16)
-
-
-def scatter(even, right, from_sibling):
-    half = right.shape[1] // 2
-    ga, gb = (
-        (dg(even, right[:, i * half : (i + 1) * half], TN) + from_sibling[i].astype(F32)).astype(BF16)
-        for i in range(2)
-    )
-    ga2 = low_add(ga[:256], flip(ga[256:], 4))
-    gb_keep = jnp.concatenate([gb[:128], gb[256:384]])
-    gb2 = low_add(gb_keep, flip(jnp.concatenate([gb[128:256], gb[384:]]), 2))
-    return low_add(ga2[:128], flip(ga2[128:], 2)), low_add(gb2[:128], flip(gb2[128:], 4))
-
-
-def sum_z(halves):
-    odd = lax.axis_index("seq") % 2 == 1
-    keep = jnp.where(odd, halves[1], halves[0])
-    give = jnp.where(odd, halves[0], halves[1])
-    kept = lax.optimization_barrier(low_add(keep, flip_z(give, 1)))
-    mine = lax.optimization_barrier(low_add(kept, flip_z(kept, 2)))
-    other = flip_z(mine, 1)
-    return jnp.concatenate([jnp.where(odd, other, mine), jnp.where(odd, mine, other)], axis=1).astype(F32)
+CHUNKS = 12
+
+
+def gelu_slope(u):
+    inner = 0.7978845608028654 * (u + 0.044715 * u * u * u)
+    t = jnp.tanh(inner)
+    return 0.5 * (1.0 + t) + 0.5 * u * (1.0 - t * t) * (0.7978845608028654 * (1.0 + 3 * 0.044715 * u * u))
+
+
+def bwd_kernel(
+    cot_hbm, cot_t_hbm, n2_t_hbm, act_hbm, up_hbm, wd_hbm, wu_hbm, wo_hbm, wq_hbm, att_t_hbm, n1_t_hbm,
+    q_hbm, ka_hbm, kb_hbm, va_hbm, vb_hbm, att_hbm, lse_ref, res_hbm, x_hbm, gain1_ref, gain2_ref,
+    gd_out, gu_out, go_out, gq_out, gin_out, sums_ref,
+    so, sr, g, h1a, h1b, h2a, h2b, z1, z2, z3, fin, dkv_in, cot, gres,
+    sib_s, sib_r, hop_s, hop_r, zs, zr, fin_sem, dkv_s, dkv_r, load,
+):
+    d, z = lax.axis_index("dp"), lax.axis_index("seq")
+    core, x, y = lax.rem(d, 2), lax.rem(d // 2, 2), d // 4
+    par = lax.rem(z, 2)
+    sibling = (d + 1 - 2 * core, z)
+    over_x = (d + 2 - 4 * x, z)
+    over_y = (d + 4 - 8 * y, z)
+    near_z = (d, z + 1 - 2 * par)
+    far_z = (d, z + 2 - 4 * (z // 2))
+    barrier = pltpu.get_barrier_semaphore()
+    for to in (sibling, over_x, over_y, near_z, far_z):
+        pl.semaphore_signal(barrier, inc=1, device_id=to, device_id_type=MESH)
+    pl.semaphore_wait(barrier, 5)
+
+    def remote(src, dst, send, recv, to):
+        return pltpu.make_async_remote_copy(
+            src_ref=src, dst_ref=dst, send_sem=send, recv_sem=recv, device_id=to, device_id_type=MESH
+        )
+
+    lo, hi = pl.ds(0, 512), pl.ds(512, 512)
+    keep = pl.ds(pl.multiple_of(par * 512, 512), 512)
+    give = pl.ds(pl.multiple_of((1 - par) * 512, 512), 512)
+
+    def to_sib(k):
+        return remote(so.at[lax.rem(k, 2)], sr.at[lax.rem(k, 2)], sib_s.at[k], sib_r.at[k], sibling)
+
+    def hop(k, j):
+        src, dst, to = (
+            (g.at[k, 1, :, :, lo], h1a.at[k], over_y),
+            (g.at[k, :, 1, :, hi], h1b.at[k], over_x),
+            (g.at[k, 0, 1, :, lo], h2a.at[k], over_x),
+            (g.at[k, 1, 0, :, hi], h2b.at[k], over_y),
+        )[j]
+        return remote(src, dst, hop_s.at[k, j], hop_r.at[k, j], to)
+
+    def zhop(k, j):
+        src, dst, to = (
+            (g.at[k, 0, 0, :, give], z1.at[k], near_z),
+            (g.at[k, 0, 0, :, keep], z2.at[k], far_z),
+            (g.at[k, 0, 0, :, keep], z3.at[k], near_z),
+        )[j]
+        return remote(src, dst, zs.at[k, j], zr.at[k, j], to)
+
+    def plus(a, b):
+        return (a.astype(F32) + b.astype(F32)).astype(BF16)
+
+    def out_copy(k):
+        slot = lax.rem(k, 2)
+        def with_target(run):
+            col = lambda j: pl.ds(pl.multiple_of(j * 1024, 1024), 1024)
+            sem = fin_sem.at[slot]
+            @pl.when(jnp.logical_and(k < 8, lax.rem(k, 2) == 0))
+            def _(): run(pltpu.make_async_copy(fin.at[slot], gd_out.at[:, col(k // 2)], sem))
+            @pl.when(jnp.logical_and(k < 8, lax.rem(k, 2) == 1))
+            def _(): run(pltpu.make_async_copy(fin.at[slot], gu_out.at[:, col(k // 2)], sem))
+            @pl.when(k == 8)
+            def _(): run(pltpu.make_async_copy(fin.at[slot], go_out, sem))
+            @pl.when(k > 8)
+            def _(): run(pltpu.make_async_copy(fin.at[slot], gq_out.at[:, col(k - 9)], sem))
+        return with_target
+
+    def tick(n):
+        def stage(k, body):
+            @pl.when(jnp.logical_and(k >= 0, k < CHUNKS))
+            def _(): body(k)
+
+        def c2(k):
+            hop(k, 0).wait(); hop(k, 1).wait()
+            g[k, 0, :, :, lo] = plus(g[k, 0, :, :, lo], h1a[k])
+            g[k, :, 0, :, hi] = plus(g[k, :, 0, :, hi], h1b[k])
+            hop(k, 2).start(); hop(k, 3).start()
+
+        def c3(k):
+            hop(k, 2).wait(); hop(k, 3).wait()
+            g[k, 0, 0, :, lo] = plus(g[k, 0, 0, :, lo], h2a[k])
+            g[k, 0, 0, :, hi] = plus(g[k, 0, 0, :, hi], h2b[k])
+            zhop(k, 0).start()
+
+        def c4(k):
+            zhop(k, 0).wait()
+            g[k, 0, 0, :, keep] = plus(g[k, 0, 0, :, keep], z1[k])
+            zhop(k, 1).start()
+
+        def c5(k):
+            zhop(k, 1).wait()
+            g[k, 0, 0, :, keep] = plus(g[k, 0, 0, :, keep], z2[k])
+            zhop(k, 2).start()
+
+        def c6(k):
+            zhop(k, 2).wait()
+            slot = lax.rem(k, 2)
+            @pl.when(k >= 2)
+            def _(): out_copy(k - 2)(lambda c: c.wait())
+            fin[slot, :, keep] = g[k, 0, 0, :, keep].astype(F32)
+            fin[slot, :, give] = z3[k].astype(F32)
+            out_copy(k)(lambda c: c.start())
+
+        stage(n, c2); stage(n - 1, c3); stage(n - 2, c4); stage(n - 3, c5); stage(n - 4, c6)
+
+    def tiles(count, body, size=256):
+        def step(i, carry):
+            body(pl.ds(pl.multiple_of(i * size, size), size))
+            return carry
+        lax.fori_loop(0, count, step, 0)
+
+    def send_odd(k, left, right):
+        def one(cols):
+            so[lax.rem(k, 2), :, cols] = dg(left[512:1024, :], right[:, cols], NN).astype(BF16)
+        tiles(4, one)
+        to_sib(k).start()
+
+    def add_even(k, left, right):
+        to_sib(k).wait()
+        def one(cols):
+            part = dg(left[0:512, :], right[:, cols], NN) + sr[lax.rem(k, 2), :, cols].astype(F32)
+            g[k, :, :, :, cols] = part.astype(BF16).reshape(2, 2, 128, 256)
+        tiles(4, one)
+        hop(k, 0).start(); hop(k, 1).start()
+
+    def fetch(src, dst, i):
+        return pltpu.make_async_copy(src, dst, load.at[i])
+
+    first = fetch(cot_hbm, cot, 0)
+    first.start()
+    sums_ref[...] = jnp.zeros_like(sums_ref)
+
+    def mlp(cot_t, n2_t, actb, upb, wdb, wub, gub, gn2, resb):
+        pieces = [fetch(cot_t_hbm, cot_t, 1), fetch(n2_t_hbm, n2_t, 2), fetch(res_hbm, resb, 3)]
+        for c in pieces: c.start()
+        def parts(j):
+            cols = pl.ds(pl.multiple_of(j * 1024, 1024), 1024)
+            s = lax.rem(j, 2)
+            return [
+                pltpu.make_async_copy(src.at[:, cols], dst.at[s], load.at[4 + 4 * s + i])
+                for i, (src, dst) in enumerate(((act_hbm, actb), (up_hbm, upb), (wd_hbm, wdb), (wu_hbm, wub)))
+            ]
+        for c in parts(jnp.int32(0)): c.start()
+        gn2[...] = jnp.zeros_like(gn2)
+        first.wait()
+        pieces[0].wait()
+        pieces[1].wait()
+        def block(j, carry):
+            s = lax.rem(j, 2)
+            for c in parts(j): c.wait()
+            @pl.when(j < 3)
+            def _():
+                for c in parts(j + 1): c.start()
+            kd, ku = 2 * j, 2 * j + 1
+            send_odd(kd, cot_t, actb.at[s])
+            def slope(cols):
+                back = dg(cot[...], wdb[s, :, cols], NN)
+                low = (back * gelu_slope(upb[s, :, cols])).astype(BF16)
+                gub[:, cols] = low
+                sums_ref[pl.ds(j, 1), cols] = jnp.sum(low.astype(F32), axis=0, keepdims=True)
+            tiles(4, slope)
+            add_even(kd, cot_t, actb.at[s])
+            send_odd(ku, n2_t, gub)
+            def down(cols):
+                gn2[:, cols] += dg(gub[...], wub[s, cols, :], NT)
+            tiles(4, down)
+            add_even(ku, n2_t, gub)
+            @pl.when(j > 0)
+            def _(): tick(j - 1)
+            return carry
+        lax.fori_loop(0, 4, block, 0)
+        pieces[2].wait()
+        def rows(r):
+            res = resb[r, :]
+            centre = jnp.mean(res, axis=-1, keepdims=True)
+            off = res - centre
+            rstd = lax.rsqrt(jnp.mean(off * off, axis=-1, keepdims=True) + norm_eps)
+            xhat = off * rstd
+            grad = gn2[r, :]
+            e = grad * gain2_ref[...]
+            back = rstd * (e - jnp.mean(e, axis=-1, keepdims=True) - xhat * jnp.mean(e * xhat, axis=-1, keepdims=True))
+            total = cot[r, :].astype(F32) + back
+            gres[r, :] = total
+            low = total.astype(BF16).astype(F32)
+            add = lambda i, v: sums_ref.__setitem__((slice(i, i + 1), slice(None)), sums_ref[i : i + 1, :] + jnp.sum(v, axis=0, keepdims=True))
+            add(4, low); add(5, grad * xhat); add(6, grad); add(7, cot[r, :].astype(F32))
+        tiles(8, rows, 64)
+
+    pl.run_scoped(
+        mlp, pltpu.VMEM((1024, 512), BF16), pltpu.VMEM((1024, 512), BF16), pltpu.VMEM((2, 512, 1024), BF16),
+        pltpu.VMEM((2, 512, 1024), F32), pltpu.VMEM((2, 1024, 1024), BF16), pltpu.VMEM((2, 1024, 1024), BF16),
+        pltpu.VMEM((512, 1024), BF16), pltpu.VMEM((512, 1024), F32), pltpu.VMEM((512, 1024), F32),
+    )
+
+    def rest(dqkv, n1_t, xb):
+        late = [fetch(n1_t_hbm, n1_t, 0), fetch(x_hbm, xb, 1)]
+        for c in late: c.start()
+
+        def attention(wo, att_t, ga, q, ka, kb, va, vb, att, do, dob):
+            loads = [
+                fetch(src, dst, 2 + i) for i, (src, dst) in enumerate((
+                    (wo_hbm, wo), (att_t_hbm, att_t), (q_hbm, q), (ka_hbm, ka), (kb_hbm, kb), (va_hbm, va),
+                    (vb_hbm, vb), (att_hbm, att),
+                ))
+            ]
+            for c in loads: c.start()
+            tick(jnp.int32(3))
+            ga[...] = gres[...].astype(BF16)
+            for c in loads: c.wait()
+            send_odd(jnp.int32(8), att_t, ga)
+            def mixed(cols):
+                do[:, cols] = dg(ga[...], wo[cols, :], NT).astype(BF16)
+            tiles(4, mixed)
+            add_even(jnp.int32(8), att_t, ga)
+            lane = lax.broadcasted_iota(jnp.int32, (512, 128), 1)
+            def pair(i, carry):
+                cols = pl.ds(pl.multiple_of(i * 128, 128), 128)
+                qs = q[:, cols] * jnp.asarray(0.125, BF16)
+                dos = do[:, cols]
+                t = (dos.astype(F32) * att[:, cols].astype(F32)).T
+                dq, dk, dv = None, [None, None], [None, None]
+                plus_ = lambda a, b: b if a is None else a + b
+                for h in range(2):
+                    sel = (lane < 64) if h == 0 else (lane >= 64)
+                    qh = jnp.where(sel, qs, jnp.zeros_like(qs))
+                    doh = jnp.where(sel, dos, jnp.zeros_like(dos))
+                    delta = jnp.sum(t[64 * h : 64 * h + 64], axis=0, keepdims=True)
+                    lse = lse_ref[i, h : h + 1, :]
+                    for n, (k_ref, v_ref) in enumerate(((ka, va), (kb, vb))):
+                        kk = k_ref[:, cols]
+                        s = dg(kk, qh, NT)
+                        p = jnp.exp(s - lse)
+                        dp = dg(v_ref[:, cols], doh, NT)
+                        ds = (p * (dp - delta)).astype(BF16)
+                        dv[n] = plus_(dv[n], dg(p.astype(BF16), doh, NN))
+                        dk[n] = plus_(dk[n], dg(ds, qh, NN))
+                        dq = plus_(dq, dg(jnp.where(sel, kk, jnp.zeros_like(kk)), ds, TN))
+                at = lambda base: pl.ds(pl.multiple_of(base + i * 128, 128), 128)
+                dqkv[:, at(0)] = (dq * 0.125).T.astype(BF16)
+                dqkv[:, at(1024)] = dk[0].astype(BF16)
+                dqkv[:, at(2048)] = dv[0].astype(BF16)
+                dob[:, at(0)] = dk[1].astype(BF16)
+                dob[:, at(1024)] = dv[1].astype(BF16)
+                @pl.when(lax.rem(i, 3) == 1)
+                def _(): tick(4 + i // 3)
+                return carry
+            lax.fori_loop(0, 8, pair, 0)
+            swap = remote(dob, dkv_in, dkv_s, dkv_r, sibling)
+            swap.start()
+            late[0].wait()
+            send_odd(jnp.int32(9), n1_t, dqkv.at[:, pl.ds(0, 1024)])
+            swap.wait()
+
+        pl.run_scoped(
+            attention, pltpu.VMEM((1024, 1024), BF16), pltpu.VMEM((1024, 512), BF16),
+            *[pltpu.VMEM((512, 1024), BF16)] * 8, pltpu.VMEM((512, 2048), BF16),
+        )
+
+        def last(wq, gn1):
+            def wq_part(i):
+                s = lax.rem(i, 2)
+                return pltpu.make_async_copy(wq_hbm.at[pl.ds(pl.multiple_of(i * 256, 256), 256), :], wq.at[s], load.at[2 + s])
+            wq_part(jnp.int32(0)).start()
+            def join(cols):
+                there = pl.ds(pl.multiple_of(1024 + cols.start, 256), 256)
+                dqkv[:, there] = plus(dqkv[:, there], dkv_in[:, cols])
+            tiles(8, join)
+            add_even(jnp.int32(9), n1_t, dqkv.at[:, pl.ds(0, 1024)])
+            for k in (10, 11):
+                right = dqkv.at[:, pl.ds(1024 * (k - 9), 1024)]
+                send_odd(jnp.int32(k), n1_t, right)
+                if k == 10:
+                    tick(jnp.int32(7))
+                add_even(jnp.int32(k), n1_t, right)
+            def back(i, carry):
+                wq_part(i).wait()
+                @pl.when(i < 3)
+                def _(): wq_part(i + 1).start()
+                gn1[:, pl.ds(pl.multiple_of(i * 256, 256), 256)] = dg(dqkv[...], wq[lax.rem(i, 2)], NT)
+                return carry
+            lax.fori_loop(0, 4, back, 0)
+            tick(jnp.int32(8))
+            late[1].wait()
+            def rows(r):
+                xx = xb[r, :].astype(F32)
+                centre = jnp.mean(xx, axis=-1, keepdims=True)
+                off = xx - centre
+                rstd = lax.rsqrt(jnp.mean(off * off, axis=-1, keepdims=True) + norm_eps)
+                xhat = off * rstd
+                grad = gn1[r, :]
+                e = grad * gain1_ref[...]
+                back = rstd * (e - jnp.mean(e, axis=-1, keepdims=True) - xhat * jnp.mean(e * xhat, axis=-1, keepdims=True))
+                xb[r, :] = (gres[r, :] + back).astype(BF16)
+                add = lambda i, v: sums_ref.__setitem__((slice(i, i + 1), slice(None)), sums_ref[i : i + 1, :] + jnp.sum(v, axis=0, keepdims=True))
+                add(8, grad * xhat); add(9, grad)
+                add(10, dqkv[r, 0:1024].astype(F32)); add(11, dqkv[r, 2048:3072].astype(F32))
+            tiles(8, rows, 64)
+            given = fetch(xb, gin_out, 4)
+            given.start()
+            def drain(n, carry):
+                tick(n)
+                return carry
+            lax.fori_loop(9, CHUNKS + 4, drain, 0)
+            for k in (CHUNKS - 2, CHUNKS - 1):
+                out_copy(jnp.int32(k))(lambda c: c.wait())
+            given.wait()
+
+        pl.run_scoped(last, pltpu.VMEM((2, 256, 3072), BF16), pltpu.VMEM((512, 1024), F32))
+
+    pl.run_scoped(rest, pltpu.VMEM((512, 3072), BF16), pltpu.VMEM((1024, 512), BF16), pltpu.VMEM((512, 1024), BF16))
+
+
+def backward(arrays, lse, residual, x, gain1, gain2):
+    any_ = pl.BlockSpec(memory_space=pl.ANY)
+    vmem = pl.BlockSpec(memory_space=pltpu.VMEM)
+    hbm = pl.BlockSpec(memory_space=HBM)
+    n = CHUNKS
+    dma = pltpu.SemaphoreType.DMA
+    return pl.pallas_call(
+        bwd_kernel,
+        in_specs=[any_] * len(arrays) + [vmem, any_, any_, vmem, vmem],
+        out_specs=[hbm] * 5 + [vmem],
+        out_shape=[jax.ShapeDtypeStruct((128, w), F32) for w in (4096, 4096, 1024, 3072)]
+        + [jax.ShapeDtypeStruct((512, 1024), BF16), jax.ShapeDtypeStruct((16, 1024), F32)],
+        scratch_shapes=[
+            pltpu.VMEM((2, 512, 1024), BF16), pltpu.VMEM((2, 512, 1024), BF16), pltpu.VMEM((n, 2, 2, 128, 1024), BF16),
+            pltpu.VMEM((n, 2, 128, 512), BF16), pltpu.VMEM((n, 2, 128, 512), BF16),
+            pltpu.VMEM((n, 128, 512), BF16), pltpu.VMEM((n, 128, 512), BF16),
+            pltpu.VMEM((n, 128, 512), BF16), pltpu.VMEM((n, 128, 512), BF16), pltpu.VMEM((n, 128, 512), BF16),
+            pltpu.VMEM((2, 128, 1024), F32), pltpu.VMEM((512, 2048), BF16), pltpu.VMEM((512, 1024), BF16),
+            pltpu.VMEM((512, 1024), F32),
+            dma((n,)), dma((n,)), dma((n, 4)), dma((n, 4)), dma((n, 3)), dma((n, 3)), dma((2,)), dma, dma, dma((12,)),
+        ],
+        compiler_params=pltpu.CompilerParams(collective_id=8, has_side_effects=True, vmem_limit_bytes=67043328),
+        cost_estimate=pl.CostEstimate(flops=40 * 10**9, bytes_accessed=60 << 20, transcendentals=10**7),
+        name="backward",
+    )(*arrays, lse, residual, x, gain1, gain2)
 
 
 def local_fast(
@@ -688,37 +1001,17 @@
     n2 = (xhat2 * gain2 + shift2).astype(BF16)
     wu = finish(up2, 2)
     upward = dot_nn(n2, wu) + bias_up
-    activated, activate_back = jax.vjp(activate, upward)
-    act = activated.astype(BF16)
-    down_sib = to_sibling(relative(cot_low, (1, 3, 5, 7), me), act)
-    g_down = scatter(relative(cot_low, (0, 2, 4, 6), me), act, down_sib)
+    act = activate(upward).astype(BF16)
     wdt = finish(down2, 3)
     result = return_image((residual + dg(act, wdt, NT) + bias_down).astype(BF16))
 
-    (grad_up,) = activate_back(dg(cot_low, wdt, NN))
-    grad_up = grad_up.astype(BF16)
-    up_sib = to_sibling(relative(n2, (1, 3, 5, 7), me), grad_up)
-    g_up = scatter(relative(n2, (0, 2, 4, 6), me), grad_up, up_sib)
-    gn2 = dg(grad_up, wu, NT)
-    grad_residual = cot_low.astype(F32) + norm_back(xhat2, rstd2, gn2, gain2)
-    grad_attn = grad_residual.astype(BF16)
-    out_sib = to_sibling(relative(attended, (1, 3, 5, 7), me), grad_attn)
-    g_out = scatter(relative(attended, (0, 2, 4, 6), me), grad_attn, out_sib)
-    grad_mixed = dg(grad_attn, wo, NT).astype(BF16)
-    dq, dka, dkb, dva, dvb = attn_bwd(q, k, kb, v, vb, attended, grad_mixed, lse)
-    dkv_other = other_core(jnp.concatenate([dkb, dvb], axis=1))
-    dkv = (jnp.concatenate([dka, dva], axis=1).astype(F32) + dkv_other.astype(F32)).astype(BF16)
-    gproj = jnp.concatenate([dq, dkv], axis=1)
-    qkv_sib = to_sibling(relative(n1, (1, 3, 5, 7), me), gproj)
-    g_qkv = scatter(relative(n1, (0, 2, 4, 6), me), gproj, qkv_sib)
-    gn1 = dg(gproj, wq, NT)
-    grad_input = return_image((grad_residual + norm_back(xhat1, rstd1, gn1, gain1)).astype(BF16))
-
-    total = lambda value: jnp.sum(value, axis=0, dtype=F32)
-    small_grads = (
-        total(gproj[:, :d]), total(gproj[:, 2 * d :]), total(grad_attn), total(grad_up), total(cot_low),
-        total(gn1 * xhat1), total(gn1), total(gn2 * xhat2), total(gn2),
-    )
+    order = (0, 2, 4, 6, 1, 3, 5, 7)
+    turned = lambda value: relative(value, order, me).T
+    g_down, g_up, g_out, g_qkv, gin, rows = backward(
+        (cot_low, turned(cot_low), turned(n2), act, upward, wdt, wu, wo, wq, turned(attended), turned(n1),
+         q, k, kb, v, vb, attended), lse, residual, x_low, gain1, gain2)
+    grad_input = return_image(gin)
+    small_grads = (rows[10], rows[11], rows[4], rows[:4], rows[7], rows[8], rows[9], rows[5], rows[6])
     sums = jnp.concatenate([g.reshape(8, -1) for g in small_grads], axis=1)
     for bits in (1, 2, 4):
         sums = lax.optimization_barrier(sums + flip(sums, bits))
@@ -729,7 +1022,7 @@
     for size in sizes:
         outs.append(mine[at : at + size])
         at += size
-    return (result, grad_input, sum_z(g_qkv), sum_z(g_out), sum_z(g_up), sum_z(g_down).T, *outs)
+    return (result, grad_input, g_qkv, g_out, g_up, g_down.T, *outs)
 
 
 def solution(mesh):

time: 569 us -> 451 us (0.79); the launches traced: 560 us -> 450 us
  waiting for transfers between devices: 250 us -> 81.1 us
  Pallas kernels: 73.4 us -> 220 us
  matrix products: 77.1 us -> 29.8 us
  starting transfers between devices: 82.2 us -> 42.3 us
  local copies, waits for them, and re-layouts: 35.8 us -> 56.3 us
  other arithmetic: 38.6 us -> 18.9 us
    pallas_call x1, Pallas kernels: 26.1 us -> 177 us  [backward(): pl.pallas_call(bwd_kernel, in_specs=[any_] * len(arrays) + [vmem, any_, a...]
    ppermute x14 -> x2, waiting for transfers between devices: 132 us -> 19.8 us  [flip_z(): return lax.ppermute(value, 'seq', [(i, i ^ bits) for i in range(4)])]
    ppermute x46 -> x22, waiting for transfers between devices: 117 us -> 61.3 us  [flip(): return lax.ppermute(value, 'dp', [(i, i ^ bits) for i in range(8)])]
    dot_general x24 -> x4, matrix products: 77.1 us -> 29.8 us  [dg(): return lax.dot_general(a, b, dims, preferred_element_type=F32)]
    ppermute x46 -> x22, starting transfers between devices: 61.7 us -> 22.4 us  [flip(): return lax.ppermute(value, 'dp', [(i, i ^ bits) for i in range(8)])]
    convert_element_type x21 -> x0, other arithmetic: 14.4 us -> none  [the longest x16 7.26 us: low_add(): return f32_add(left, right).astype(BF16)]
    unnamed x193 -> x140, local copies, waits for them, and re-layouts: 17.6 us -> 28.3 us
    ppermute x14 -> x2, starting transfers between devices: 10.7 us -> 1.54 us  [flip_z(): return lax.ppermute(value, 'seq', [(i, i ^ bits) for i in range(4)])]
  transfers between devices with their start and end apart: 70 -> 33, of which waited for: 32 -> 13; matrix products, arithmetic and copies ran while one was open for 16% -> 12% of each run, Pallas kernels for 5% -> 6%
where the time goes in v3:
time: 451 us; the launch traced here: 450 us
  Pallas kernels  220 us (49%)
  waiting for transfers between devices  81.1 us (18%)
  local copies, waits for them, and re-layouts  56.3 us (12%)
  starting transfers between devices  42.3 us (9%)
  matrix products  29.8 us (7%)
  other arithmetic  18.9 us (4%)
    pallas_call x1, Pallas kernels, backward(): pl.pallas_call(bwd_kernel, in_specs=[any_] * len(arrays) + [vmem, any_, a...  177 us
    ppermute x22, waiting for transfers between devices, flip(): return lax.ppermute(value, 'dp', [(i, i ^ bits) for i in range(8)])  61.3 us
    dot_general x4, matrix products, dg(): return lax.dot_general(a, b, dims, preferred_element_type=F32)  29.8 us
    unnamed x140, local copies, waits for them, and re-layouts  28.3 us
    pallas_call x4, Pallas kernels, finish(): pl.pallas_call(finish_kernel, in_specs=[pl.BlockSpec(memory_space=pl.ANY)...  25.1 us
    ppermute x22, starting transfers between devices, flip(): return lax.ppermute(value, 'dp', [(i, i ^ bits) for i in range(8)])  22.4 us
    ppermute x2, waiting for transfers between devices, flip_z(): return lax.ppermute(value, 'seq', [(i, i ^ bits) for i in range(4)])  19.8 us
    pallas_call x1, Pallas kernels, attn_fwd(): pl.pallas_call(attn_fwd_kernel, grid=(width // 128,), in_specs=[spec, ks,...  17.4 us
  transfers between devices with their start and end apart: 33, of which 13 were waited for; matrix products, arithmetic and copies ran while one was open for 12% of the time, Pallas kernels for 6%

profile of v3, /device:TPU:0, one launch (start us, length us, event | category | flops | bytes accessed | tf_op | source)
XLA Modules:
  0.0 449.7 jit_solution(17940184329396094759)
XLA Ops:
  9.7 2.9 collective-permute-start.3
  12.6 2.2 dynamic-slice_bitcast_fusion.6
  14.8 1.7 collective-permute-start
  16.5 1.6 collective-permute-start.1
  18.1 1.6 collective-permute-start.4
  23.2 8.6 %collective-permute-done.5 = bf16[128,1536]{1,0:T(8,128)(2,1)} collective-permute-done((bf16[128,1536]{1,0:T(8,128)(2,1)}, bf16[128,1536]{1,0:T(8,128)(2,1)}, u32[]{:S(2)}, u32[]{:S(2)}) %collective-permute-start.5) | collective-permute-done | bytes 393248 | tf_op jit(solution)/shard_map/ppermute | solution.py:532
  35.3 1.4 collective-permute-start.10
  36.8 1.5 collective-permute-start.12
  38.3 1.7 convert_reduce_fusion
  40.4 17.2 %collective-permute-done.10 = bf16[128,512]{1,0:T(8,128)(2,1)S(1)} collective-permute-done((bf16[128,512]{1,0:T(8,128)(2,1)S(1)}, bf16[128,512]{1,0:T(8,128)(2,1)S(1)}, u32[]{:S(2)}, u32[]{:S(2)}) %collective-permute-start.10) | collective-permute-done | bytes 131104 | tf_op jit(solution)/shard_map/ppermute | solution.py:532
  57.7 1.6 collective-permute-start.11
  61.1 5.3 %collective-permute-start.24 = (bf16[256,1024]{1,0:T(8,128)(2,1)}, bf16[256,1024]{1,0:T(8,128)(2,1)}, u32[]{:S(2)}, u32[]{:S(2)}) collective-permute-start(bf16[256,1024]{1,0:T(8,128)(2,1)} %get-tuple-element.71), channel_id=1, source_target_pairs={{0,0},{1,1},{2,4},{3,5},{4,2},{5,3},{6,6},{7,7},{8,8},{9,9},{10,12... | collective-permute-start | bytes 1572872 | tf_op jit(solution)/shard_map/ppermute | solution.py:488
  68.4 1.5 slice_bitcast_fusion.8
  71.7 1.4 slice_bitcast_fusion.10
  73.4 1.5 collective-permute-start.16
  74.9 6.3 %finish0.1.wq_hbm = bf16[1024,3072]{1,0:T(8,128)(2,1)} custom-call(bf16[2,128,1536]{2,1,0:T(8,128)(2,1)} %copy-done.13, bf16[2,128,1536]{2,1,0:T(8,128)(2,1)} %copy-done.27, bf16[2,128,1536]{2,1,0:T(8,128)(2,1)} %copy-done.14, bf16[2,128,1536]{2,1,0:T(8,128)(2,1)} %copy-done.28), custom_call_target="tpu_custom_call" | custom-call | bytes 12582912 | tf_op jit(solution)/shard_map/finish0/pallas_call | solution.py:582
  81.2 6.4 %add_convert_fusion = bf16[512,3072]{1,0:T(8,128)(2,1)S(1)} fusion(bf16[512,1024]{1,0:T(8,128)(2,1)S(1)} %fusion.11, bf16[1024,3072]{1,0:T(8,128)(2,1)} %finish0.1.wq_hbm, f32[3072]{0:T(1024)S(1)} %bitcast.162), kind=kOutput, calls=%fused_computation.9 | convolution fusion | flops 3224371200 | bytes 10498048 | tf_op jit(solution)/shard_map/dot_general | solution.py:400
  87.6 1.5 slice.206
  92.7 2.1 pad_maximum_fusion.2.a01
  96.0 2.1 pad_maximum_fusion.1.b01
  98.1 7.0 %collective-permute-done.14 = bf16[128,2048]{1,0:T(8,128)(2,1)S(1)} collective-permute-done((bf16[128,2048]{1,0:T(8,128)(2,1)}, bf16[128,2048]{1,0:T(8,128)(2,1)S(1)}, u32[]{:S(2)}, u32[]{:S(2)}) %collective-permute-start.14) | collective-permute-done | bytes 524320 | tf_op jit(solution)/shard_map/ppermute | solution.py:532
  107.5 1.4 collective-permute-start.15
  113.1 2.3 copy.42.n1_t_hbm
  115.4 3.3 finish1.1.wo_hbm
  118.7 2.4 maximum_select_fusion.2
  121.1 3.2 fusion.23
  124.3 3.4 collective-permute-done.21.b2
  127.7 3.8 collective-permute-done.19.a2
  131.5 7.8 %finish3.1.wd_hbm = bf16[1024,4096]{1,0:T(8,128)(2,1)} custom-call(bf16[2,128,2048]{2,1,0:T(8,128)(2,1)} %pad_maximum_fusion.2.a01, bf16[2,128,2048]{2,1,0:T(8,128)(2,1)} %collective-permute-done.19.a2, bf16[2,128,2048]{2,1,0:T(8,128)(2,1)} %copy-done.11, bf16[2,128,2048]{2,1,0:T(8,128)(2,1)} %collective-permute-done.21.b2), custom_call_target="tpu_custom_call" | custom-call | bytes 16777216 | tf_op jit(solution)/shard_map/finish3/pallas_call | solution.py:582
  139.3 10.3 %collective-permute-done.17.b2 = bf16[2,128,2048]{2,1,0:T(8,128)(2,1)} collective-permute-done((bf16[2,128,2048]{2,1,0:T(8,128)(2,1)}, bf16[2,128,2048]{2,1,0:T(8,128)(2,1)}, u32[]{:S(2)}, u32[]{:S(2)}) %collective-permute-start.17) | collective-permute-done | bytes 1048608 | tf_op jit(solution)/shard_map/ppermute | solution.py:532
  149.6 2.3 collective-permute-done.15.a2
  151.9 7.8 %finish2.1.wu_hbm = bf16[1024,4096]{1,0:T(8,128)(2,1)} custom-call(bf16[2,128,2048]{2,1,0:T(8,128)(2,1)} %pad_maximum_fusion.a01, bf16[2,128,2048]{2,1,0:T(8,128)(2,1)} %collective-permute-done.15.a2, bf16[2,128,2048]{2,1,0:T(8,128)(2,1)} %pad_maximum_fusion.1.b01, bf16[2,128,2048]{2,1,0:T(8,128)(2,1)} %collective-permute-done.17.b2), custom_call_target="tpu_custom_call" | custom-call | bytes 16777216 | tf_op jit(solution)/shard_map/finish2/pallas_call | solution.py:582
  159.7 2.8 fusion.24
  162.5 17.4 %attn_fwd.1 = (bf16[512,1024]{1,0:T(8,128)(2,1)S(1)}, f32[8,8,512]{2,1,0:T(8,128)S(1)}) custom-call(bf16[512,1024]{1,0:T(8,128)(2,1)S(1)} %copy-done.3, bf16[512,1024]{1,0:T(8,128)(2,1)S(1)} %get-tuple-element.57.ka_ref.ka_hbm, bf16[512,1024]{1,0:T(8,128)(2,1)S(1)} %get-tuple-element.60.kb_ref.kb_hbm, bf16[512,1024]{1,0:T(8,128)(2,1)S(1)} %get-tuple-element.56.va_ref.va_hbm, ...), custom_call_target="tpu_custom_call" | custom-call | flops 2147483648 | bytes 6291456 | tf_op jit(solution)/shard_map/attn_fwd/pallas_call | solution.py:425
  188.6 1.4 copy.41.n2_t_hbm
  194.6 12.8 %fusion.7 = (bf16[512,4096]{1,0:T(8,128)(2,1)}, f32[512,4096]{1,0:T(8,128)}) fusion(f32[4096]{0:T(1024)S(1)} %bitcast.161, bf16[512,1024]{1,0:T(8,128)(2,1)S(1)} %add_convert_fusion.2, bf16[1024,4096]{1,0:T(8,128)(2,1)} %finish2.1.wu_hbm), kind=kOutput, calls=%fused_computation.8 | convolution fusion | flops 4315938816 | bytes 22036480 | tf_op jit(solution)/shard_map/dot_general | solution.py:400
  207.4 177.3 %backward.1 = (f32[128,4096]{1,0:T(8,128)}, f32[128,4096]{1,0:T(8,128)}, f32[128,1024]{1,0:T(8,128)}, f32[128,3072]{1,0:T(8,128)}, bf16[512,1024]{1,0:T(8,128)(2,1)}, /*index=5*/f32[16,1024]{1,0:T(8,128)}) custom-call(bf16[512,1024]{1,0:T(8,128)(2,1)} %bitcast.134, bf16[1024,512]{1,0:T(8,128)(2,1)} %bitcast.159, bf16[1024,512]{1,0:T(8,128)(2,1)} %copy.41.n2_t_hbm, ...), custom_call_target="tpu_custom_call" | custom-call | flops 40000000000 | bytes 62914560 | tf_op jit(solution)/shard_map/backward/pallas_call | solution.py:937
  386.6 2.2 dynamic-slice_bitcast_fusion.1
  388.8 1.7 collective-permute-start.26
  391.0 9.2 %add_convert_fusion.1 = bf16[512,1024]{1,0:T(8,128)(2,1)S(1)} fusion(f32[512,1024]{1,0:T(8,128)S(1)} %copy-done.10, bf16[512,4096]{1,0:T(8,128)(2,1)} %get-tuple-element.131.act_hbm, bf16[1024,4096]{1,0:T(8,128)(2,1)} %finish3.1.wd_hbm, f32[1024]{0:T(1024)S(1)} %copy-done.39), kind=kOutput, calls=%fused_computation.22 | convolution fusion | flops 4296540160 | bytes 15732736 | tf_op jit(solution)/shard_map/dot_general | solution.py:400
  401.3 5.4 %collective-permute-start.22 = (bf16[256,1024]{1,0:T(8,128)(2,1)}, bf16[256,1024]{1,0:T(8,128)(2,1)}, u32[]{:S(2)}, u32[]{:S(2)}) collective-permute-start(bf16[256,1024]{1,0:T(8,128)(2,1)} %get-tuple-element.73), channel_id=1, source_target_pairs={{0,0},{1,1},{4,2},{5,3},{2,4},{3,5},{6,6},{7,7},{8,8},{9,9},{12,10... | collective-permute-start | bytes 1572872 | tf_op jit(solution)/shard_map/ppermute | solution.py:501
  406.7 1.5 collective-permute-start.23
  410.3 3.4 collective-permute-done.29
  414.5 3.4 collective-permute-done.30
  418.4 9.2 %collective-permute-done.31 = f32[8,1536]{1,0:T(8,128)S(1)} collective-permute-done((f32[8,1536]{1,0:T(8,128)S(1)}, f32[8,1536]{1,0:T(8,128)S(1)}, u32[]{:S(2)}, u32[]{:S(2)}) %collective-permute-start.31) | collective-permute-done | bytes 49184 | tf_op jit(solution)/shard_map/ppermute | solution.py:536
  428.6 1.8 copy.43
  430.4 10.6 %collective-permute-done.32 = f32[8,1536]{1,0:T(8,128)S(1)} collective-permute-done((f32[8,1536]{1,0:T(8,128)S(1)}, f32[8,1536]{1,0:T(8,128)S(1)}, u32[]{:S(2)}, u32[]{:S(2)}) %collective-permute-start.32) | collective-permute-done | bytes 49184 | tf_op jit(solution)/shard_map/ppermute | solution.py:536
  443.4 2.7 maximum_select_fusion.1
  (230 shorter events, 60.5 us)
Async XLA Ops:
  0.6 19.0 %copy-start.29 = (bf16[128,3072]{1,0:T(8,128)(2,1)S(1)}, bf16[128,3072]{1,0:T(8,128)(2,1)}, u32[]{:S(2)}) copy-start(bf16[128,3072]{1,0:T(8,128)(2,1)} %param.16) | copy-start | bytes 2359300
  8.3 1.4 collective-permute-start.2
  9.7 12.1 %copy-start.25 = (bf16[4096,128]{1,0:T(8,128)(2,1)S(1)}, bf16[4096,128]{1,0:T(8,128)(2,1)}, u32[]{:S(2)}) copy-start(bf16[4096,128]{1,0:T(8,128)(2,1)} %param.19) | copy-start | bytes 3145732
  9.7 8.4 %collective-permute-start.3 = (bf16[2,1536]{1,0:T(2,128)(2,1)S(1)}, bf16[2,1536]{1,0:T(2,128)(2,1)S(1)}, u32[]{:S(2)}, u32[]{:S(2)}) collective-permute-start(bf16[2,1536]{1,0:T(2,128)(2,1)S(1)} %pad_maximum_fusion.11), channel_id=1, source_target_pairs={{0,8},{4,12},{8,0},{12,4},{16,24},{20,28},{24,16},{28,20},{1,9},{5... | collective-permute-start | bytes 18440 | tf_op jit(solution)/shard_map/ppermute | solution.py:532
  14.8 22.0 %collective-permute-start = (bf16[256,1024]{1,0:T(8,128)(2,1)}, bf16[256,1024]{1,0:T(8,128)(2,1)S(1)}, u32[]{:S(2)}, u32[]{:S(2)}) collective-permute-start(bf16[256,1024]{1,0:T(8,128)(2,1)} %get-tuple-element.84), channel_id=1, source_target_pairs={{0,0},{1,1},{2,4},{3,5},{4,2},{5,3},{6,6},{7,7},{8,8},{9,9},{10,12... | collective-permute-start | bytes 1572872 | tf_op jit(solution)/shard_map/ppermute | solution.py:488
  16.5 21.8 %collective-permute-start.1 = (bf16[256,1024]{1,0:T(8,128)(2,1)}, bf16[256,1024]{1,0:T(8,128)(2,1)}, u32[]{:S(2)}, u32[]{:S(2)}) collective-permute-start(bf16[256,1024]{1,0:T(8,128)(2,1)} %get-tuple-element.83), channel_id=1, source_target_pairs={{0,1},{1,0},{2,5},{3,4},{4,3},{5,2},{6,7},{7,6},{8,9},{9,8},{10,13... | collective-permute-start | bytes 1572872 | tf_op jit(solution)/shard_map/ppermute | solution.py:488
  18.1 4.3 collective-permute-start.4
  20.7 11.1 %collective-permute-start.5 = (bf16[128,1536]{1,0:T(8,128)(2,1)}, bf16[128,1536]{1,0:T(8,128)(2,1)}, u32[]{:S(2)}, u32[]{:S(2)}) collective-permute-start(bf16[128,1536]{1,0:T(8,128)(2,1)} %get-tuple-element.88), channel_id=1, source_target_pairs={{0,8},{4,12},{8,0},{12,4},{16,24},{20,28},{24,16},{28,20},{1,9},{5... | collective-permute-start | bytes 1179656 | tf_op jit(solution)/shard_map/ppermute | solution.py:532
  21.2 12.2 %collective-permute-start.7 = (bf16[128,1536]{1,0:T(8,128)(2,1)}, bf16[128,1536]{1,0:T(8,128)(2,1)}, u32[]{:S(2)}, u32[]{:S(2)}) collective-permute-start(bf16[128,1536]{1,0:T(8,128)(2,1)} %get-tuple-element.87), channel_id=1, source_target_pairs={{0,16},{4,20},{8,24},{12,28},{16,0},{20,4},{24,8},{28,12},{1,17},{... | collective-permute-start | bytes 1179656 | tf_op jit(solution)/shard_map/ppermute | solution.py:532
  22.3 13.0 %copy-start.35 = (bf16[128,1024]{1,0:T(8,128)(2,1)S(1)}, bf16[128,1024]{1,0:T(8,128)(2,1)}, u32[]{:S(2)}) copy-start(bf16[128,1024]{1,0:T(8,128)(2,1)} %param.17) | copy-start | bytes 786436
  32.9 7.1 %copy-start.13 = (bf16[2,128,1536]{2,1,0:T(8,128)(2,1)}, bf16[2,128,1536]{2,1,0:T(8,128)(2,1)S(1)}, u32[]{:S(2)}) copy-start(bf16[2,128,1536]{2,1,0:T(8,128)(2,1)S(1)} %pad_maximum_fusion.4.a01) | copy-start | bytes 2359300
  32.9 38.8 %collective-permute-start.6 = (bf16[2,128,1536]{2,1,0:T(8,128)(2,1)S(1)}, bf16[2,128,1536]{2,1,0:T(8,128)(2,1)S(1)}, u32[]{:S(2)}, u32[]{:S(2)}) collective-permute-start(bf16[2,128,1536]{2,1,0:T(8,128)(2,1)S(1)} %pad_maximum_fusion.4.a01), channel_id=1, source_target_pairs={{0,16},{4,20},{8,24},{12,28},{16,0},{20,4},{24,8},{28,12},{1,17},{... | collective-permute-start | bytes 2359304 | tf_op jit(solution)/shard_map/ppermute | solution.py:532
  34.5 23.1 %copy-start.14 = (bf16[2,128,1536]{2,1,0:T(8,128)(2,1)}, bf16[2,128,1536]{2,1,0:T(8,128)(2,1)S(1)}, u32[]{:S(2)}) copy-start(bf16[2,128,1536]{2,1,0:T(8,128)(2,1)S(1)} %pad_maximum_fusion.5.b01) | copy-start | bytes 2359300
  34.6 37.1 %collective-permute-start.8 = (bf16[2,128,1536]{2,1,0:T(8,128)(2,1)S(1)}, bf16[2,128,1536]{2,1,0:T(8,128)(2,1)S(1)}, u32[]{:S(2)}, u32[]{:S(2)}) collective-permute-start(bf16[2,128,1536]{2,1,0:T(8,128)(2,1)S(1)} %pad_maximum_fusion.5.b01), channel_id=1, source_target_pairs={{0,8},{4,12},{8,0},{12,4},{16,24},{20,28},{24,16},{28,20},{1,9},{5... | collective-permute-start | bytes 2359304 | tf_op jit(solution)/shard_map/ppermute | solution.py:532
  35.3 22.3 %collective-permute-start.10 = (bf16[128,512]{1,0:T(8,128)(2,1)S(1)}, bf16[128,512]{1,0:T(8,128)(2,1)S(1)}, u32[]{:S(2)}, u32[]{:S(2)}) collective-permute-start(bf16[128,512]{1,0:T(8,128)(2,1)S(1)} %get-tuple-element.92), channel_id=1, source_target_pairs={{0,8},{4,12},{8,0},{12,4},{16,24},{20,28},{24,16},{28,20},{1,9},{5... | collective-permute-start | bytes 393224 | tf_op jit(solution)/shard_map/ppermute | solution.py:532
  36.8 22.5 %collective-permute-start.12 = (bf16[128,512]{1,0:T(8,128)(2,1)S(1)}, bf16[128,512]{1,0:T(8,128)(2,1)S(1)}, u32[]{:S(2)}, u32[]{:S(2)}) collective-permute-start(bf16[128,512]{1,0:T(8,128)(2,1)S(1)} %get-tuple-element.91), channel_id=1, source_target_pairs={{0,16},{4,20},{8,24},{12,28},{16,0},{20,4},{24,8},{28,12},{1,17},{... | collective-permute-start | bytes 393224 | tf_op jit(solution)/shard_map/ppermute | solution.py:532
  38.3 21.8 %copy-start.26 = (bf16[2,256,1024]{2,1,0:T(8,128)(2,1)S(1)}, bf16[2,256,1024]{2,1,0:T(8,128)(2,1)}, u32[]{:S(2)}) copy-start(bf16[2,256,1024]{2,1,0:T(8,128)(2,1)} %param.29) | copy-start | bytes 3145732
  40.0 26.5 %copy-start.6 = (bf16[2,256,1024]{2,1,0:T(8,128)(2,1)}, bf16[2,256,1024]{2,1,0:T(8,128)(2,1)S(1)}, u32[]{:S(2)}) copy-start(bf16[2,256,1024]{2,1,0:T(8,128)(2,1)S(1)} %get-tuple-element.55) | copy-start | bytes 3145732
  57.6 9.3 %copy-start.23 = (bf16[2,128,512]{2,1,0:T(8,128)(2,1)}, bf16[2,128,512]{2,1,0:T(8,128)(2,1)S(1)}, u32[]{:S(2)}) copy-start(bf16[2,128,512]{2,1,0:T(8,128)(2,1)S(1)} %pad_maximum_fusion.6.a01) | copy-start | bytes 786436
  57.7 10.7 %collective-permute-start.11 = (bf16[2,128,512]{2,1,0:T(8,128)(2,1)S(1)}, bf16[2,128,512]{2,1,0:T(8,128)(2,1)S(1)}, u32[]{:S(2)}, u32[]{:S(2)}) collective-permute-start(bf16[2,128,512]{2,1,0:T(8,128)(2,1)S(1)} %pad_maximum_fusion.6.a01), channel_id=1, source_target_pairs={{0,16},{4,20},{8,24},{12,28},{16,0},{20,4},{24,8},{28,12},{1,17},{... | collective-permute-start | bytes 786440 | tf_op jit(solution)/shard_map/ppermute | solution.py:532
  59.3 7.7 %copy-start.24 = (bf16[2,128,512]{2,1,0:T(8,128)(2,1)}, bf16[2,128,512]{2,1,0:T(8,128)(2,1)S(1)}, u32[]{:S(2)}) copy-start(bf16[2,128,512]{2,1,0:T(8,128)(2,1)S(1)} %pad_maximum_fusion.7.b01) | copy-start | bytes 786436
  59.3 9.1 %collective-permute-start.13 = (bf16[2,128,512]{2,1,0:T(8,128)(2,1)S(1)}, bf16[2,128,512]{2,1,0:T(8,128)(2,1)S(1)}, u32[]{:S(2)}, u32[]{:S(2)}) collective-permute-start(bf16[2,128,512]{2,1,0:T(8,128)(2,1)S(1)} %pad_maximum_fusion.7.b01), channel_id=1, source_target_pairs={{0,8},{4,12},{8,0},{12,4},{16,24},{20,28},{24,16},{28,20},{1,9},{5... | collective-permute-start | bytes 786440 | tf_op jit(solution)/shard_map/ppermute | solution.py:532
  61.1 45.6 %collective-permute-start.24 = (bf16[256,1024]{1,0:T(8,128)(2,1)}, bf16[256,1024]{1,0:T(8,128)(2,1)}, u32[]{:S(2)}, u32[]{:S(2)}) collective-permute-start(bf16[256,1024]{1,0:T(8,128)(2,1)} %get-tuple-element.71), channel_id=1, source_target_pairs={{0,0},{1,1},{2,4},{3,5},{4,2},{5,3},{6,6},{7,7},{8,8},{9,9},{10,12... | collective-permute-start | bytes 1572872 | tf_op jit(solution)/shard_map/ppermute | solution.py:488
  69.9 20.2 %collective-permute-start.20 = (bf16[128,2048]{1,0:T(8,128)(2,1)}, bf16[128,2048]{1,0:T(8,128)(2,1)S(1)}, u32[]{:S(2)}, u32[]{:S(2)}) collective-permute-start(bf16[128,2048]{1,0:T(8,128)(2,1)} %get-tuple-element.77), channel_id=1, source_target_pairs={{0,16},{4,20},{8,24},{12,28},{16,0},{20,4},{24,8},{28,12},{1,17},{... | collective-permute-start | bytes 1572872 | tf_op jit(solution)/shard_map/ppermute | solution.py:532
  70.5 21.6 %collective-permute-start.18 = (bf16[128,2048]{1,0:T(8,128)(2,1)}, bf16[128,2048]{1,0:T(8,128)(2,1)}, u32[]{:S(2)}, u32[]{:S(2)}) collective-permute-start(bf16[128,2048]{1,0:T(8,128)(2,1)} %get-tuple-element.78), channel_id=1, source_target_pairs={{0,8},{4,12},{8,0},{12,4},{16,24},{20,28},{24,16},{28,20},{1,9},{5... | collective-permute-start | bytes 1572872 | tf_op jit(solution)/shard_map/ppermute | solution.py:532
  73.4 21.4 %collective-permute-start.16 = (bf16[128,2048]{1,0:T(8,128)(2,1)}, bf16[128,2048]{1,0:T(8,128)(2,1)}, u32[]{:S(2)}, u32[]{:S(2)}) collective-permute-start(bf16[128,2048]{1,0:T(8,128)(2,1)} %get-tuple-element.81), channel_id=1, source_target_pairs={{0,16},{4,20},{8,24},{12,28},{16,0},{20,4},{24,8},{28,12},{1,17},{... | collective-permute-start | bytes 1572872 | tf_op jit(solution)/shard_map/ppermute | solution.py:532
  90.0 69.7 %collective-permute-start.9 = (bf16[512,2048]{1,0:T(8,128)(2,1)}, bf16[512,2048]{1,0:T(8,128)(2,1)}, u32[]{:S(2)}, u32[]{:S(2)}) collective-permute-start(bf16[512,2048]{1,0:T(8,128)(2,1)} %slice.206), channel_id=1, source_target_pairs={{0,4},{4,0},{8,12},{12,8},{16,20},{20,16},{24,28},{28,24},{1,5},{5... | collective-permute-start | bytes 6291464 | tf_op jit(solution)/shard_map/ppermute | solution.py:506
  90.1 15.0 %collective-permute-start.14 = (bf16[128,2048]{1,0:T(8,128)(2,1)}, bf16[128,2048]{1,0:T(8,128)(2,1)S(1)}, u32[]{:S(2)}, u32[]{:S(2)}) collective-permute-start(bf16[128,2048]{1,0:T(8,128)(2,1)} %get-tuple-element.82), channel_id=1, source_target_pairs={{0,8},{4,12},{8,0},{12,4},{16,24},{20,28},{24,16},{28,20},{1,9},{5... | collective-permute-start | bytes 1572872 | tf_op jit(solution)/shard_map/ppermute | solution.py:532
  92.1 15.4 %collective-permute-start.25 = (bf16[256,1024]{1,0:T(8,128)(2,1)S(1)}, bf16[256,1024]{1,0:T(8,128)(2,1)S(1)}, u32[]{:S(2)}, u32[]{:S(2)}) collective-permute-start(bf16[256,1024]{1,0:T(8,128)(2,1)S(1)} %copy-done.33), channel_id=1, source_target_pairs={{0,1},{1,0},{2,5},{3,4},{4,3},{5,2},{6,7},{7,6},{8,9},{9,8},{10,13... | collective-permute-start | bytes 1572872 | tf_op jit(solution)/shard_map/ppermute | solution.py:488
  94.8 32.9 %collective-permute-start.21 = (bf16[2,128,2048]{2,1,0:T(8,128)(2,1)S(1)}, bf16[2,128,2048]{2,1,0:T(8,128)(2,1)}, u32[]{:S(2)}, u32[]{:S(2)}) collective-permute-start(bf16[2,128,2048]{2,1,0:T(8,128)(2,1)S(1)} %pad_maximum_fusion.3.b01), channel_id=1, source_target_pairs={{0,8},{4,12},{8,0},{12,4},{16,24},{20,28},{24,16},{28,20},{1,9},{5... | collective-permute-start | bytes 3145736 | tf_op jit(solution)/shard_map/ppermute | solution.py:532
  105.1 26.3 %collective-permute-start.19 = (bf16[2,128,2048]{2,1,0:T(8,128)(2,1)}, bf16[2,128,2048]{2,1,0:T(8,128)(2,1)}, u32[]{:S(2)}, u32[]{:S(2)}) collective-permute-start(bf16[2,128,2048]{2,1,0:T(8,128)(2,1)} %pad_maximum_fusion.2.a01), channel_id=1, source_target_pairs={{0,16},{4,20},{8,24},{12,28},{16,0},{20,4},{24,8},{28,12},{1,17},{... | collective-permute-start | bytes 3145736 | tf_op jit(solution)/shard_map/ppermute | solution.py:532
  106.7 42.9 %collective-permute-start.17 = (bf16[2,128,2048]{2,1,0:T(8,128)(2,1)}, bf16[2,128,2048]{2,1,0:T(8,128)(2,1)}, u32[]{:S(2)}, u32[]{:S(2)}) collective-permute-start(bf16[2,128,2048]{2,1,0:T(8,128)(2,1)} %pad_maximum_fusion.1.b01), channel_id=1, source_target_pairs={{0,8},{4,12},{8,0},{12,4},{16,24},{20,28},{24,16},{28,20},{1,9},{5... | collective-permute-start | bytes 3145736 | tf_op jit(solution)/shard_map/ppermute | solution.py:532
  107.5 44.4 %collective-permute-start.15 = (bf16[2,128,2048]{2,1,0:T(8,128)(2,1)}, bf16[2,128,2048]{2,1,0:T(8,128)(2,1)}, u32[]{:S(2)}, u32[]{:S(2)}) collective-permute-start(bf16[2,128,2048]{2,1,0:T(8,128)(2,1)} %pad_maximum_fusion.a01), channel_id=1, source_target_pairs={{0,16},{4,20},{8,24},{12,28},{16,0},{20,4},{24,8},{28,12},{1,17},{... | collective-permute-start | bytes 3145736 | tf_op jit(solution)/shard_map/ppermute | solution.py:532
  124.3 38.2 %copy-start.1 = (bf16[512,1024]{1,0:T(8,128)(2,1)}, bf16[512,1024]{1,0:T(8,128)(2,1)S(1)}, u32[]{:S(2)}) copy-start(bf16[512,1024]{1,0:T(8,128)(2,1)S(1)} %get-tuple-element.56.va_ref.va_hbm) | copy-start | bytes 3145732
  124.3 38.2 %copy-start.2 = (bf16[512,1024]{1,0:T(8,128)(2,1)}, bf16[512,1024]{1,0:T(8,128)(2,1)S(1)}, u32[]{:S(2)}) copy-start(bf16[512,1024]{1,0:T(8,128)(2,1)S(1)} %get-tuple-element.57.ka_ref.ka_hbm) | copy-start | bytes 3145732
  162.5 17.4 %copy-start.4 = (bf16[512,1024]{1,0:T(8,128)(2,1)}, bf16[512,1024]{1,0:T(8,128)(2,1)S(1)}, u32[]{:S(2)}) copy-start(bf16[512,1024]{1,0:T(8,128)(2,1)S(1)} %get-tuple-element.60.kb_ref.kb_hbm) | copy-start | bytes 3145732
  384.7 6.3 %copy-start.10 = (f32[512,1024]{1,0:T(8,128)S(1)}, f32[512,1024]{1,0:T(8,128)}, u32[]{:S(2)}) copy-start(f32[512,1024]{1,0:T(8,128)} %copy-done.9) | copy-start | bytes 6291460
  384.7 6.3 %copy-start.39 = (f32[1024]{0:T(1024)S(1)}, f32[1024]{0:T(1024)}, u32[]{:S(2)}) copy-start(f32[1024]{0:T(1024)} %get-tuple-element.112) | copy-start | bytes 12292
  388.8 53.4 %collective-permute-start.26 = (bf16[256,1024]{1,0:T(8,128)(2,1)}, bf16[256,1024]{1,0:T(8,128)(2,1)S(1)}, u32[]{:S(2)}, u32[]{:S(2)}) collective-permute-start(bf16[256,1024]{1,0:T(8,128)(2,1)} %get-tuple-element.61), channel_id=1, source_target_pairs={{0,0},{1,1},{4,2},{5,3},{2,4},{3,5},{6,6},{7,7},{8,8},{9,9},{12,10... | collective-permute-start | bytes 1572872 | tf_op jit(solution)/shard_map/ppermute | solution.py:501
  390.5 51.8 %collective-permute-start.27 = (bf16[256,1024]{1,0:T(8,128)(2,1)}, bf16[256,1024]{1,0:T(8,128)(2,1)S(1)}, u32[]{:S(2)}, u32[]{:S(2)}) collective-permute-start(bf16[256,1024]{1,0:T(8,128)(2,1)} %get-tuple-element.62), channel_id=1, source_target_pairs={{1,0},{0,1},{5,2},{4,3},{3,4},{2,5},{7,6},{6,7},{9,8},{8,9},{13,10... | collective-permute-start | bytes 1572872 | tf_op jit(solution)/shard_map/ppermute | solution.py:501
  400.3 28.3 %copy-start.17 = (f32[128,4096]{1,0:T(8,128)S(1)}, f32[128,4096]{1,0:T(8,128)}, u32[]{:S(2)}) copy-start(f32[128,4096]{1,0:T(8,128)} %get-tuple-element.37) | copy-start | bytes 6291460
  401.3 42.1 %collective-permute-start.22 = (bf16[256,1024]{1,0:T(8,128)(2,1)}, bf16[256,1024]{1,0:T(8,128)(2,1)}, u32[]{:S(2)}, u32[]{:S(2)}) collective-permute-start(bf16[256,1024]{1,0:T(8,128)(2,1)} %get-tuple-element.73), channel_id=1, source_target_pairs={{0,0},{1,1},{4,2},{5,3},{2,4},{3,5},{6,6},{7,7},{8,8},{9,9},{12,10... | collective-permute-start | bytes 1572872 | tf_op jit(solution)/shard_map/ppermute | solution.py:501
  406.7 36.7 %collective-permute-start.23 = (bf16[256,1024]{1,0:T(8,128)(2,1)}, bf16[256,1024]{1,0:T(8,128)(2,1)}, u32[]{:S(2)}, u32[]{:S(2)}) collective-permute-start(bf16[256,1024]{1,0:T(8,128)(2,1)} %get-tuple-element.74), channel_id=1, source_target_pairs={{1,0},{0,1},{5,2},{4,3},{3,4},{2,5},{7,6},{6,7},{9,8},{8,9},{13,10... | collective-permute-start | bytes 1572872 | tf_op jit(solution)/shard_map/ppermute | solution.py:501
  408.2 1.3 collective-permute-start.28
  409.5 4.1 collective-permute-start.29
  413.7 4.2 collective-permute-start.30
  417.8 9.8 %collective-permute-start.31 = (f32[8,1536]{1,0:T(8,128)S(1)}, f32[8,1536]{1,0:T(8,128)S(1)}, u32[]{:S(2)}, u32[]{:S(2)}) collective-permute-start(f32[8,1536]{1,0:T(8,128)S(1)} %add.231), channel_id=1, source_target_pairs={{0,1},{1,0},{2,3},{3,2},{4,5},{5,4},{6,7},{7,6},{8,9},{9,8},{10,11... | collective-permute-start | bytes 147464 | tf_op jit(solution)/shard_map/ppermute | solution.py:536
  427.6 13.4 %collective-permute-start.32 = (f32[8,1536]{1,0:T(8,128)S(1)}, f32[8,1536]{1,0:T(8,128)S(1)}, u32[]{:S(2)}, u32[]{:S(2)}) collective-permute-start(f32[8,1536]{1,0:T(8,128)S(1)} %add.232), channel_id=1, source_target_pairs={{0,2},{1,3},{2,0},{3,1},{4,6},{5,7},{6,4},{7,5},{8,10},{9,11},{10,... | collective-permute-start | bytes 147464 | tf_op jit(solution)/shard_map/ppermute | solution.py:536
  (25 other events, 69.3 us)

commit v4 on v3

--- a/solution.py
+++ b/solution.py
@@ -399,212 +399,319 @@
 NT=(((1,),(1,)),((),())); TN=(((0,),(0,)),((),())); NN=(((1,),(0,)),((),()))
 def dg(a,b,dims): return lax.dot_general(a,b,dims,preferred_element_type=F32)
 
-def attn_fwd_kernel(q_ref, ka_ref, kb_ref, va_ref, vb_ref, o_ref, l_ref):
-    rows=q_ref.shape[0]
-    lane=lax.broadcasted_iota(jnp.int32,(rows,128),1)
-    q=q_ref[...]*jnp.asarray(0.125,BF16)
-    outs=[]; ls=[]
-    for h in range(2):
-        qh=jnp.where((lane<64) if h==0 else (lane>=64), q, jnp.zeros_like(q))
-        sa=dg(ka_ref[...],qh,NT); sb=dg(kb_ref[...],qh,NT)
-        m=jnp.maximum(jnp.max(sa,axis=0,keepdims=True),jnp.max(sb,axis=0,keepdims=True))
-        pa=jnp.exp(sa-m); pb=jnp.exp(sb-m)
-        tot=jnp.sum(pa,axis=0,keepdims=True)+jnp.sum(pb,axis=0,keepdims=True)
-        oT=dg(va_ref[...],pa.astype(BF16),TN)+dg(vb_ref[...],pb.astype(BF16),TN)
-        outs.append(oT[64*h:64*h+64]*(1.0/tot))
-        ls.append(m+jnp.log(tot))
-    oT=jnp.concatenate(outs,axis=0)
-    o_ref[...]=oT.T.astype(BF16)
-    l_ref[0]=jnp.concatenate(ls+[jnp.zeros((6,rows),F32)],axis=0)
-
-def attn_fwd(q,ka,kb,va,vb):
-    rows,width=q.shape
-    spec=pl.BlockSpec((rows,128),lambda i:(0,i))
-    keys=ka.shape[0]
-    ks=pl.BlockSpec((keys,128),lambda i:(0,i))
-    return pl.pallas_call(attn_fwd_kernel,grid=(width//128,),
-        in_specs=[spec,ks,ks,ks,ks],
-        out_specs=[spec,pl.BlockSpec((1,8,rows),lambda i:(i,0,0))],
-        out_shape=[jax.ShapeDtypeStruct((rows,width),BF16),jax.ShapeDtypeStruct((width//128,8,rows),F32)],
-        compiler_params=pltpu.CompilerParams(vmem_limit_bytes=48<<20),name="attn_fwd",
-        cost_estimate=pl.CostEstimate(flops=4*rows*2*keys*width,bytes_accessed=12*rows*width,transcendentals=rows*2*keys*width//64))(q,ka,kb,va,vb)
-
-def attn_bwd_kernel(q_ref, ka_ref, kb_ref, va_ref, vb_ref, o_ref, do_ref, l_ref, dq_ref, dka_ref, dkb_ref, dva_ref, dvb_ref):
-    rows=q_ref.shape[0]
-    lane=lax.broadcasted_iota(jnp.int32,(rows,128),1)
-    q=q_ref[...]*jnp.asarray(0.125,BF16)
-    do=do_ref[...]
-    t=(do.astype(F32)*o_ref[...].astype(F32)).T
-    klane=lax.broadcasted_iota(jnp.int32,(ka_ref.shape[0],128),1)
-    dq=None; dk=[None,None]; dv=[None,None]
-    add=lambda a,b: b if a is None else a+b
-    for h in range(2):
-        sel=(lane<64) if h==0 else (lane>=64)
-        ksel=(klane<64) if h==0 else (klane>=64)
-        qh=jnp.where(sel,q,jnp.zeros_like(q)); doh=jnp.where(sel,do,jnp.zeros_like(do))
-        delta=jnp.sum(t[64*h:64*h+64],axis=0,keepdims=True)
-        lse=l_ref[0,h:h+1,:]
-        for n,(k_ref,v_ref) in enumerate(((ka_ref,va_ref),(kb_ref,vb_ref))):
-            s=dg(k_ref[...],qh,NT)
-            p=jnp.exp(s-lse)
-            dp=dg(v_ref[...],doh,NT)
-            ds=(p*(dp-delta)).astype(BF16)
-            dv[n]=add(dv[n],dg(p.astype(BF16),doh,NN))
-            dk[n]=add(dk[n],dg(ds,qh,NN))
-            kh=jnp.where(ksel,k_ref[...],jnp.zeros_like(k_ref[...]))
-            dq=add(dq,dg(kh,ds,TN))
-    dq_ref[...]=(dq*0.125).T.astype(BF16)
-    dka_ref[...]=dk[0].astype(BF16); dkb_ref[...]=dk[1].astype(BF16)
-    dva_ref[...]=dv[0].astype(BF16); dvb_ref[...]=dv[1].astype(BF16)
-
-def attn_bwd(q,ka,kb,va,vb,o,do,l):
-    rows,width=q.shape; keys=ka.shape[0]
-    spec=pl.BlockSpec((rows,128),lambda i:(0,i))
-    ks=pl.BlockSpec((keys,128),lambda i:(0,i))
-    sh=jax.ShapeDtypeStruct((rows,width),BF16); kh=jax.ShapeDtypeStruct((keys,width),BF16)
-    return pl.pallas_call(attn_bwd_kernel,grid=(width//128,),
-        in_specs=[spec,ks,ks,ks,ks,spec,spec,pl.BlockSpec((1,8,rows),lambda i:(i,0,0))],
-        out_specs=[spec,ks,ks,ks,ks],
-        out_shape=[sh,kh,kh,kh,kh],
-        compiler_params=pltpu.CompilerParams(vmem_limit_bytes=48<<20),name="attn_bwd",
-        cost_estimate=pl.CostEstimate(flops=10*rows*2*keys*width,bytes_accessed=26*rows*width,transcendentals=rows*2*keys*width//64))(q,ka,kb,va,vb,o,do,l)
-
-
-def image_moves(shift):
-    pairs = []
-    for p in range(4):
-        for c in range(2):
-            for z in range(4):
-                to_core, to_z = z // 2, 2 * c + (shift ^ (z & 1))
-                pairs.append(((2 * p + c) * 4 + z, (2 * p + to_core) * 4 + to_z))
-    return pairs
-
-
-def gather_image(blocks):
-    odd = lax.axis_index("seq") % 2
-    parts = []
-    for shift in range(2):
-        mine = lax.dynamic_index_in_dim(blocks, odd ^ shift, 0, keepdims=False)
-        parts.append(lax.ppermute(mine, ("dp", "seq"), image_moves(shift)))
-    rows = parts[0].shape[0]
-    swapped = jnp.where(odd == 0, jnp.stack(parts), jnp.stack(parts[::-1]))
-    return swapped.reshape(2 * rows, parts[0].shape[1])
-
-
-def return_image(rows_all):
-    odd = lax.axis_index("seq") % 2
-    halves = rows_all.reshape(2, rows_all.shape[0] // 2, rows_all.shape[1])
-    parts = []
-    for shift in range(2):
-        mine = lax.dynamic_index_in_dim(halves, odd ^ shift, 0, keepdims=False)
-        back = [(to, start) for start, to in image_moves(shift)]
-        parts.append(lax.ppermute(mine, ("dp", "seq"), back))
-    return jnp.where(odd == 0, jnp.stack(parts), jnp.stack(parts[::-1]))
-
-
-def other_core(value):
-    return lax.ppermute(value, "dp", [(i, i ^ 1) for i in range(lax.axis_size("dp"))])
-
-
-def dot_nn(left, right):
-    return dg(left, right, NN)
-
-
-def norm_parts(value):
-    centre = jnp.mean(value, axis=-1, keepdims=True)
-    spread = jnp.mean(jnp.square(value - centre), axis=-1, keepdims=True)
-    rstd = lax.rsqrt(spread + norm_eps)
-    return ((value - centre) * rstd, rstd)
-
-
-def norm_back(xhat, rstd, grad, gain):
-    e = grad * gain
-    return rstd * (
-        e - jnp.mean(e, axis=-1, keepdims=True) - xhat * jnp.mean(e * xhat, axis=-1, keepdims=True)
-    )
-
-
 MESH = pl.DeviceIdType.MESH
 HBM = pltpu.MemorySpace.HBM
 
 
-def flip(value, bits):
-    return lax.ppermute(value, "dp", [(i, i ^ bits) for i in range(8)])
-
-
-def flip_z(value, bits):
-    return lax.ppermute(value, "seq", [(i, i ^ bits) for i in range(4)])
-
-
-def after(value, *earlier):
-    return lax.optimization_barrier((value,) + earlier)[0]
-
-
-def finish_kernel(a01, a2, b01, b2, out, kept, in_sem, out_sem, send_sem, recv_sem):
+def device_map():
     d, z = lax.axis_index("dp"), lax.axis_index("seq")
     core, x, y = lax.rem(d, 2), lax.rem(d // 2, 2), d // 4
-    sibling = (d + 1 - 2 * core, z)
-    half = a01.shape[2]
+    par = lax.rem(z, 2)
+    return dict(
+        d=d, z=z, core=core, x=x, y=y, par=par,
+        sibling=(d + 1 - 2 * core, z), over_x=(d + 2 - 4 * x, z), over_y=(d + 4 - 8 * y, z),
+        near_z=(d, z + 1 - 2 * par), far_z=(d, z + 2 - 4 * (z // 2)),
+        image=[(d - core + z // 2, 2 * core + b) for b in range(2)],
+        home=(z // 2) == core,
+    )
+
+
+def remote(src, dst, send, recv, to):
+    return pltpu.make_async_remote_copy(
+        src_ref=src, dst_ref=dst, send_sem=send, recv_sem=recv, device_id=to, device_id_type=MESH
+    )
+
+
+def greet(place, names):
     barrier = pltpu.get_barrier_semaphore()
-    pl.semaphore_signal(barrier, inc=1, device_id=sibling, device_id_type=MESH)
-    pl.semaphore_wait(barrier, 1)
-    pieces = (
-        (a01.at[0], y, x, 0), (b01.at[0], y, x, 1),
-        (a01.at[1], y, 1 - x, 0), (b01.at[1], 1 - y, x, 1),
-        (a2.at[0], 1 - y, x, 0), (b2.at[0], y, 1 - x, 1),
-        (a2.at[1], 1 - y, 1 - x, 0), (b2.at[1], 1 - y, 1 - x, 1),
-    )
-    sends, loads, stores = [], [], []
-    for k, (piece, py, px, side) in enumerate(pieces):
-        row = pl.multiple_of(((py * 2 + px) * 2 + core) * 128, 128)
-        target = out.at[pl.ds(row, 128), pl.ds(side * half, half)]
-        sends.append(
-            pltpu.make_async_remote_copy(
-                src_ref=piece, dst_ref=target, send_sem=send_sem.at[k], recv_sem=recv_sem.at[k],
-                device_id=sibling, device_id_type=MESH,
-            )
-        )
-        loads.append(pltpu.make_async_copy(piece, kept.at[k], in_sem.at[k]))
-        stores.append(pltpu.make_async_copy(kept.at[k], target, out_sem.at[k]))
-    for k in range(8):
-        sends[k].start()
-        loads[k].start()
-    for k in range(8):
-        loads[k].wait()
-        stores[k].start()
-    for k in range(8):
-        stores[k].wait()
-        sends[k].wait()
-
-
-def finish(parts, ident):
-    half = parts[0].shape[2]
+    for name in names:
+        pl.semaphore_signal(barrier, inc=1, device_id=place[name], device_id_type=MESH)
+    for b in range(2):
+        @pl.when(jnp.logical_not(jnp.logical_and(place["home"], place["par"] == b)))
+        def _(): pl.semaphore_signal(barrier, inc=1, device_id=place["image"][b], device_id_type=MESH)
+    pl.semaphore_wait(barrier, len(names) + 2 - place["home"].astype(jnp.int32))
+
+
+class Move:
+    def __init__(self, place, sources, target, sems):
+        self.place, self.sources, self.target, self.sems = place, sources, target, sems
+    def each(self, far, near):
+        p = self.place
+        for b in range(2):
+            stays = jnp.logical_and(p["home"], p["par"] == b)
+            target = self.target(p["par"])
+            @pl.when(jnp.logical_not(stays))
+            def _(): far(remote(self.sources[b], target, self.sems.at[0, b], self.sems.at[1, p["par"]], p["image"][b]))
+            @pl.when(stays)
+            def _(): near(pltpu.make_async_copy(self.sources[b], target, self.sems.at[2, 0]))
+    def start(self):
+        self.each(lambda c: c.start(), lambda c: c.start())
+    def wait(self):
+        p = self.place
+        self.each(lambda c: c.wait_send(), lambda c: c.wait())
+        for h in range(2):
+            @pl.when(jnp.logical_not(jnp.logical_and(p["home"], p["par"] == h)))
+            def _(): remote(self.sources[0], self.target(h), self.sems.at[0, 0], self.sems.at[1, h], p["image"][0]).wait_recv()
+
+
+def tiles(count, body, size=256):
+    def step(i, carry):
+        body(pl.ds(pl.multiple_of(i * size, size), size))
+        return carry
+    lax.fori_loop(0, count, step, 0)
+
+
+def turn(place, source, target):
+    for j in range(8):
+        jy, jx, jc = j // 4, (j // 2) % 2, j % 2
+        differ = lambda a, b: (a + b) - 2 * a * b
+        at = differ(place["core"], jc) * 4 + differ(place["y"], jy) * 2 + differ(place["x"], jx)
+        target[pl.ds(pl.multiple_of(at * 128, 128), 128), :] = source[:, 128 * j : 128 * j + 128].T
+
+
+def fwd_kernel(
+    tok_hbm, cotg_hbm, wq_s, wo_s, wu_s, wd_s, pack,
+    wq_o, wo_o, wu_o, wd_o, x_o, cot_o, cot_t_o, n1_t_o, n2_t_o, att_t_o, qkv_o, kv_o, att_o, act_o, up_o, res_o, out_o,
+    lse, vec,
+    wq, wo, wu, wd, wdn, pk, xb, cot, n1, n2, qkv, kv, att, act, upb, up_bias, res, cot_t, n1_t, n2_t, att_t,
+    ws, wr, wl, ps, pr, ms, kvs, kvr, outs, ups,
+):
+    p = device_map()
+    y, x, core, par = p["y"], p["x"], p["core"], p["par"]
+    greet(p, ("sibling", "over_x", "over_y"))
+
+    def rows(py, px):
+        return pl.ds(pl.multiple_of(((py * 2 + px) * 2 + core) * 128, 128), 128)
+
+    chunks = [(wq, wq_s, 0, 3072), (wo, wo_s, 0, 1024), (wu, wu_s, 0, 2048), (wu, wu_s, 2048, 2048),
+              (wd, None, 0, 2048), (wd, None, 2048, 2048)]
+    me, bx, by, diag = rows(y, x), rows(y, 1 - x), rows(1 - y, x), rows(1 - y, 1 - x)
+
+    def copy(n, i):
+        w, shard, at, size = chunks[n]
+        lo, hi, full = pl.ds(at, size // 2), pl.ds(at + size // 2, size // 2), pl.ds(at, size)
+        own = (lambda cols: w.at[me, cols]) if shard is None else (lambda cols: shard.at[:, cols])
+        src, dst, to = (
+            (own(lo), w.at[me, lo], "over_x"), (own(hi), w.at[me, hi], "over_y"),
+            (own(hi), w.at[me, hi], "over_x"), (own(lo), w.at[me, lo], "over_y"),
+            (own(full), w.at[me, full], "sibling"),
+            (w.at[bx, lo], w.at[bx, lo], "over_y"), (w.at[by, hi], w.at[by, hi], "over_x"),
+            (w.at[bx, full], w.at[bx, full], "sibling"), (w.at[by, full], w.at[by, full], "sibling"),
+            (w.at[diag, lo], w.at[diag, lo], "sibling"), (w.at[diag, hi], w.at[diag, hi], "sibling"),
+        )[i]
+        return remote(src, dst, ws.at[n, i], wr.at[n, i], p[to])
+
+    def start(n, *which):
+        for i in which: copy(n, i).start()
+
+    def wait(n, *which):
+        for i in which: copy(n, i).wait()
+
+    def local(n):
+        w, shard, at, size = chunks[n]
+        return pltpu.make_async_copy(shard.at[:, pl.ds(at, size)], w.at[me, pl.ds(at, size)], wl.at[n])
+
+    def own(n):
+        start(n, 0, 1, 2, 3, 4)
+        if chunks[n][1] is not None: local(n).start()
+
+    def mid(n):
+        wait(n, 0, 1)
+        start(n, 5, 6)
+        if n < 5: own(n + 1)
+
+    def late(n):
+        wait(n, 2, 3)
+        start(n, 7, 8)
+
+    def end(n):
+        wait(n, 5, 6)
+        start(n, 9, 10)
+        wait(n, 4, 7, 8, 9, 10)
+        if chunks[n][1] is not None: local(n).wait()
+
+    given, settled = [], []
+    def give(src, dst):
+        c = pltpu.make_async_copy(src, dst, outs.at[len(given)])
+        c.start()
+        given.append(c)
+        return c
+
+    def settle(c):
+        c.wait()
+        settled.append(c)
+
+    own(0)
+    pk[y, x, core] = pack[...]
+    hop1 = remote(pk.at[y, x, core], pk.at[y, x, core], ps.at[0], pr.at[0], p["over_x"])
+    hop1.start()
+    half = lambda h: pl.ds(pl.multiple_of(h * 256, 256), 256)
+    tok = Move(p, [tok_hbm.at[b] for b in range(2)], lambda h: xb.at[half(h)], ms.at[0])
+    tok.start()
+    cot_move = Move(p, [cotg_hbm.at[b] for b in range(2)], lambda h: cot.at[half(h)], ms.at[1])
+    cot_move.start()
+    down = pltpu.make_async_copy(wd_s, wdn, wl.at[5])
+    down.start()
+    hop1.wait()
+    hop2 = remote(pk.at[y, :, core], pk.at[y, :, core], ps.at[1], pr.at[1], p["over_y"])
+    hop2.start()
+    down.wait()
+    for j in range(8):
+        wd[me, 512 * j : 512 * j + 512] = wdn[512 * j : 512 * j + 512, :].T
+    hop2.wait()
+    hop3 = remote(pk.at[:, :, core], pk.at[:, :, core], ps.at[2], pr.at[2], p["sibling"])
+    hop3.start()
+    mid(0)
+    hop3.wait()
+    for j in range(8):
+        block = pk[j // 4, (j // 2) % 2, j % 2]
+        for r in range(12):
+            if 3 <= r < 7:
+                at = 512 * j + 128 * (r - 3)
+                up_bias[:, at : at + 128] = block[r : r + 1]
+            else:
+                to = {0: 4, 1: 5, 2: 6, 7: 7, 8: 8, 9: 9, 10: 10, 11: 11}[r]
+                vec[to : to + 1, 128 * j : 128 * j + 128] = block[r : r + 1]
+    vec[0:4, :] = jnp.zeros((4, 1024), F32)
+    vec[12:16, :] = jnp.zeros((4, 1024), F32)
+    tok.wait()
+
+    def stats(value):
+        off = value - jnp.mean(value, axis=-1, keepdims=True)
+        return off * lax.rsqrt(jnp.mean(off * off, axis=-1, keepdims=True) + norm_eps)
+
+    def norm_one(r):
+        n1[r, :] = (stats(xb[r, :].astype(F32)) * vec[8:9, :] + vec[9:10, :]).astype(BF16)
+    tiles(8, norm_one, 64)
+    x_given = give(xb, x_o)
+    late(0)
+    turn(p, n1, n1_t)
+    give(n1_t, n1_t_o)
+    end(0)
+    give(wq, wq_o)
+    mid(1)
+
+    def project(cols, bias):
+        part = dg(n1[...], wq[:, cols], NN)
+        qkv[:, cols] = (part if bias is None else part + bias).astype(BF16)
+    def key_cols(c): project(pl.ds(pl.multiple_of(1024 + c.start, 256), 256), None)
+    tiles(4, key_cols)
+    def value_cols(c): project(pl.ds(pl.multiple_of(2048 + c.start, 256), 256), vec[5:6, c])
+    tiles(4, value_cols)
+    swap = remote(qkv.at[:, pl.ds(1024, 2048)], kv, kvs, kvr, p["sibling"])
+    swap.start()
+    def query_cols(c): project(c, vec[4:5, c])
+    tiles(4, query_cols)
+    swap.wait()
+    give(qkv, qkv_o)
+    give(kv, kv_o)
+
+    lane = lax.broadcasted_iota(jnp.int32, (512, 128), 1)
+    def pair(i, carry):
+        at = lambda base: pl.ds(pl.multiple_of(base + i * 128, 128), 128)
+        q = qkv[:, at(0)] * jnp.asarray(0.125, BF16)
+        outs_, ls = [], []
+        for h in range(2):
+            qh = jnp.where((lane < 64) if h == 0 else (lane >= 64), q, jnp.zeros_like(q))
+            sa, sb = dg(qkv[:, at(1024)], qh, NT), dg(kv[:, at(0)], qh, NT)
+            m = jnp.maximum(jnp.max(sa, axis=0, keepdims=True), jnp.max(sb, axis=0, keepdims=True))
+            pa, pb = jnp.exp(sa - m), jnp.exp(sb - m)
+            total = jnp.sum(pa, axis=0, keepdims=True) + jnp.sum(pb, axis=0, keepdims=True)
+            o = dg(qkv[:, at(2048)], pa.astype(BF16), TN) + dg(kv[:, at(1024)], pb.astype(BF16), TN)
+            outs_.append(o[64 * h : 64 * h + 64] * (1.0 / total))
+            ls.append(m + jnp.log(total))
+        att[:, at(0)] = jnp.concatenate(outs_, axis=0).T.astype(BF16)
+        lse[i] = jnp.concatenate(ls + [jnp.zeros((6, 512), F32)], axis=0)
+        @pl.when(i == 2)
+        def _():
+            late(1)
+            end(1)
+            mid(2)
+        return carry
+    lax.fori_loop(0, 8, pair, 0)
+    give(wo, wo_o)
+    give(att, att_o)
+    late(2)
+    end(2)
+    mid(3)
+
+    def out_cols(c):
+        res[:, c] = xb[:, c].astype(F32) + dg(att[...], wo[:, c], NN) + vec[6:7, c]
+    tiles(4, out_cols)
+    res_given = give(res, res_o)
+    def norm_two(r):
+        n2[r, :] = (stats(res[r, :]) * vec[10:11, :] + vec[11:12, :]).astype(BF16)
+    tiles(8, norm_two, 64)
+
+    def up_copy(i):
+        return pltpu.make_async_copy(upb.at[lax.rem(i, 2)], up_o.at[:, pl.ds(pl.multiple_of(i * 512, 512), 512)], ups.at[lax.rem(i, 2)])
+    def up_block(i, carry):
+        @pl.when(i >= 2)
+        def _(): up_copy(i - 2).wait()
+        for t in range(2):
+            c = pl.ds(pl.multiple_of(i * 512 + 256 * t, 256), 256)
+            u = dg(n2[...], wu[:, c], NN) + up_bias[:, c]
+            upb[lax.rem(i, 2), :, 256 * t : 256 * t + 256] = u
+            act[:, c] = (0.5 * u * (1.0 + jnp.tanh(0.7978845608028654 * (u + 0.044715 * u * u * u)))).astype(BF16)
+        up_copy(i).start()
+        return carry
+    lax.fori_loop(0, 4, up_block, 0)
+    turn(p, n2, n2_t)
+    give(n2_t, n2_t_o)
+    turn(p, att, att_t)
+    give(att_t, att_t_o)
+    cot_move.wait()
+    give(cot, cot_o)
+    turn(p, cot, cot_t)
+    give(cot_t, cot_t_o)
+    late(3)
+    end(3)
+    give(wu, wu_o)
+    mid(4)
+    lax.fori_loop(4, 8, up_block, 0)
+    give(act, act_o)
+    late(4)
+    end(4)
+    settle(res_given)
+    first, second = pl.ds(0, 2048), pl.ds(2048, 2048)
+    def half_down(c):
+        res[:, c] += dg(act[:, first], wd[c, first], NT)
+    tiles(4, half_down)
+    mid(5)
+    late(5)
+    end(5)
+    give(wd, wd_o)
+    settle(x_given)
+    def finish_cols(c):
+        xb[:, c] = (res[:, c] + dg(act[:, second], wd[c, second], NT) + vec[7:8, c]).astype(BF16)
+    tiles(4, finish_cols)
+    give(xb, out_o)
+    for c in given:
+        if not any(c is s for s in settled): c.wait()
+    up_copy(jnp.int32(6)).wait()
+    up_copy(jnp.int32(7)).wait()
+
+
+def forward(tokens, cotangent, shards, pack):
+    any_, vmem, hbm = (pl.BlockSpec(memory_space=s) for s in (pl.ANY, pltpu.VMEM, HBM))
+    dma = pltpu.SemaphoreType.DMA
+    wide = [((1024, 3072), BF16), ((1024, 1024), BF16), ((1024, 4096), BF16), ((1024, 4096), BF16)]
+    rows, turned = ((512, 1024), BF16), ((1024, 512), BF16)
+    shapes = wide + [rows, rows] + [turned] * 4 + [
+        ((512, 3072), BF16), ((512, 2048), BF16), rows, ((512, 4096), BF16), ((512, 4096), F32), ((512, 1024), F32), rows]
     return pl.pallas_call(
-        finish_kernel,
-        in_specs=[pl.BlockSpec(memory_space=pl.ANY)] * 4,
-        out_specs=pl.BlockSpec(memory_space=HBM),
-        out_shape=jax.ShapeDtypeStruct((1024, 2 * half), BF16),
-        scratch_shapes=[pltpu.VMEM((8, 128, half), BF16)] + [pltpu.SemaphoreType.DMA((8,))] * 4,
-        compiler_params=pltpu.CompilerParams(collective_id=ident, has_side_effects=True),
-        cost_estimate=pl.CostEstimate(flops=0, bytes_accessed=8192 * half, transcendentals=0),
-        name="finish%d" % ident,
-    )(*parts)
-
-
-def first_hop(shard):
-    half = shard.shape[1] // 2
-    a, b = shard[:, :half], shard[:, half:]
-    return jnp.stack([a, flip(a, 2)]), jnp.stack([b, flip(b, 4)])
-
-
-def second_hop(first):
-    return first[0], flip(first[0], 4), first[1], flip(first[1], 2)
-
-
-def relative(value, order, me):
-    return jnp.concatenate(
-        [lax.dynamic_slice_in_dim(value, 128 * (me ^ r), 128, axis=1) for r in order], axis=1
-    )
+        fwd_kernel,
+        in_specs=[any_] * 6 + [vmem],
+        out_specs=[hbm] * len(shapes) + [vmem, vmem],
+        out_shape=[jax.ShapeDtypeStruct(*s) for s in shapes + [((8, 8, 512), F32), ((16, 1024), F32)]],
+        scratch_shapes=[pltpu.VMEM(*s) for s in wide + [
+            ((4096, 128), BF16), ((2, 2, 2, 12, 128), F32), rows, rows, rows, rows, ((512, 3072), BF16), ((512, 2048), BF16),
+            rows, ((512, 4096), BF16), ((2, 512, 512), F32), ((1, 4096), F32), ((512, 1024), F32)] + [turned] * 4]
+        + [dma((6, 11)), dma((6, 11)), dma((6,)), dma((3,)), dma((3,)), dma((2, 3, 2)), dma, dma, dma((20,)), dma((2,))],
+        compiler_params=pltpu.CompilerParams(collective_id=7, has_side_effects=True, vmem_limit_bytes=67043328),
+        cost_estimate=pl.CostEstimate(flops=20 * 10**9, bytes_accessed=60 << 20, transcendentals=10**7),
+        name="forward",
+    )(tokens, cotangent, *shards, pack)
 
 
 CHUNKS = 12
@@ -618,28 +725,15 @@
 
 def bwd_kernel(
     cot_hbm, cot_t_hbm, n2_t_hbm, act_hbm, up_hbm, wd_hbm, wu_hbm, wo_hbm, wq_hbm, att_t_hbm, n1_t_hbm,
-    q_hbm, ka_hbm, kb_hbm, va_hbm, vb_hbm, att_hbm, lse_ref, res_hbm, x_hbm, gain1_ref, gain2_ref,
-    gd_out, gu_out, go_out, gq_out, gin_out, sums_ref,
-    so, sr, g, h1a, h1b, h2a, h2b, z1, z2, z3, fin, dkv_in, cot, gres,
-    sib_s, sib_r, hop_s, hop_r, zs, zr, fin_sem, dkv_s, dkv_r, load,
+    qkv_hbm, kv_hbm, att_hbm, out_hbm, res_hbm, x_hbm, lse_ref, vec,
+    gd_out, gu_out, go_out, gq_out, result_out, gin_out, small_out,
+    sums_ref, sum_in, so, sr, g, h1a, h1b, h2a, h2b, z1, z2, z3, fin, dkv_in, cot, gres,
+    sib_s, sib_r, hop_s, hop_r, zs, zr, fin_sem, dkv_s, dkv_r, load, ms, ss, sm,
 ):
-    d, z = lax.axis_index("dp"), lax.axis_index("seq")
-    core, x, y = lax.rem(d, 2), lax.rem(d // 2, 2), d // 4
-    par = lax.rem(z, 2)
-    sibling = (d + 1 - 2 * core, z)
-    over_x = (d + 2 - 4 * x, z)
-    over_y = (d + 4 - 8 * y, z)
-    near_z = (d, z + 1 - 2 * par)
-    far_z = (d, z + 2 - 4 * (z // 2))
-    barrier = pltpu.get_barrier_semaphore()
-    for to in (sibling, over_x, over_y, near_z, far_z):
-        pl.semaphore_signal(barrier, inc=1, device_id=to, device_id_type=MESH)
-    pl.semaphore_wait(barrier, 5)
-
-    def remote(src, dst, send, recv, to):
-        return pltpu.make_async_remote_copy(
-            src_ref=src, dst_ref=dst, send_sem=send, recv_sem=recv, device_id=to, device_id_type=MESH
-        )
+    p = device_map()
+    x, y, core, par, z = p["x"], p["y"], p["core"], p["par"], p["z"]
+    sibling, over_x, over_y, near_z, far_z = (p[n] for n in ("sibling", "over_x", "over_y", "near_z", "far_z"))
+    greet(p, ("sibling", "over_x", "over_y", "near_z", "far_z"))
 
     lo, hi = pl.ds(0, 512), pl.ds(512, 512)
     keep = pl.ds(pl.multiple_of(par * 512, 512), 512)
@@ -721,12 +815,6 @@
 
         stage(n, c2); stage(n - 1, c3); stage(n - 2, c4); stage(n - 3, c5); stage(n - 4, c6)
 
-    def tiles(count, body, size=256):
-        def step(i, carry):
-            body(pl.ds(pl.multiple_of(i * size, size), size))
-            return carry
-        lax.fori_loop(0, count, step, 0)
-
     def send_odd(k, left, right):
         def one(cols):
             so[lax.rem(k, 2), :, cols] = dg(left[512:1024, :], right[:, cols], NN).astype(BF16)
@@ -746,6 +834,8 @@
 
     first = fetch(cot_hbm, cot, 0)
     first.start()
+    result = Move(p, [out_hbm.at[pl.ds(256 * h, 256)] for h in range(2)], lambda b: result_out.at[b], ms.at[0])
+    result.start()
     sums_ref[...] = jnp.zeros_like(sums_ref)
 
     def mlp(cot_t, n2_t, actb, upb, wdb, wub, gub, gn2, resb):
@@ -795,7 +885,7 @@
             rstd = lax.rsqrt(jnp.mean(off * off, axis=-1, keepdims=True) + norm_eps)
             xhat = off * rstd
             grad = gn2[r, :]
-            e = grad * gain2_ref[...]
+            e = grad * vec[10:11, :]
             back = rstd * (e - jnp.mean(e, axis=-1, keepdims=True) - xhat * jnp.mean(e * xhat, axis=-1, keepdims=True))
             total = cot[r, :].astype(F32) + back
             gres[r, :] = total
@@ -817,8 +907,8 @@
         def attention(wo, att_t, ga, q, ka, kb, va, vb, att, do, dob):
             loads = [
                 fetch(src, dst, 2 + i) for i, (src, dst) in enumerate((
-                    (wo_hbm, wo), (att_t_hbm, att_t), (q_hbm, q), (ka_hbm, ka), (kb_hbm, kb), (va_hbm, va),
-                    (vb_hbm, vb), (att_hbm, att),
+                    (wo_hbm, wo), (att_t_hbm, att_t), (qkv_hbm.at[:, pl.ds(0, 1024)], q), (qkv_hbm.at[:, pl.ds(1024, 1024)], ka), (kv_hbm.at[:, pl.ds(0, 1024)], kb),
+                    (qkv_hbm.at[:, pl.ds(2048, 1024)], va), (kv_hbm.at[:, pl.ds(1024, 1024)], vb), (att_hbm, att),
                 ))
             ]
             for c in loads: c.start()
@@ -906,41 +996,58 @@
                 rstd = lax.rsqrt(jnp.mean(off * off, axis=-1, keepdims=True) + norm_eps)
                 xhat = off * rstd
                 grad = gn1[r, :]
-                e = grad * gain1_ref[...]
+                e = grad * vec[8:9, :]
                 back = rstd * (e - jnp.mean(e, axis=-1, keepdims=True) - xhat * jnp.mean(e * xhat, axis=-1, keepdims=True))
                 xb[r, :] = (gres[r, :] + back).astype(BF16)
                 add = lambda i, v: sums_ref.__setitem__((slice(i, i + 1), slice(None)), sums_ref[i : i + 1, :] + jnp.sum(v, axis=0, keepdims=True))
                 add(8, grad * xhat); add(9, grad)
                 add(10, dqkv[r, 0:1024].astype(F32)); add(11, dqkv[r, 2048:3072].astype(F32))
             tiles(8, rows, 64)
-            given = fetch(xb, gin_out, 4)
+            given = Move(p, [xb.at[pl.ds(256 * h, 256)] for h in range(2)], lambda b: gin_out.at[b], ms.at[1])
             given.start()
-            def drain(n, carry):
-                tick(n)
-                return carry
-            lax.fori_loop(9, CHUNKS + 4, drain, 0)
+            steps = [
+                remote(sums_ref, sum_in.at[i], ss.at[i], sm.at[i], to)
+                for i, to in enumerate((sibling, over_x, over_y, near_z, far_z))
+            ]
+            steps[0].start()
+            for i in range(7):
+                tick(jnp.int32(9 + i))
+                if i < 5:
+                    steps[i].wait()
+                    sums_ref[...] += sum_in[i]
+                    if i < 4: steps[i + 1].start()
+            d = p["d"]
+            mine = pl.ds(pl.multiple_of(d * 128, 128), 128)
+            for to, at in ((0, 10), (1, 11), (2, 4), (7, 7), (8, 8), (9, 9), (10, 5), (11, 6)):
+                small_out[to : to + 1, :] = sums_ref[at : at + 1, mine]
+            for t in range(4):
+                lanes = pl.ds(pl.multiple_of(lax.rem(d, 2) * 512 + 128 * t, 128), 128)
+                part = sums_ref[0:1, lanes]
+                for r in range(1, 4):
+                    part = jnp.where(d // 2 == r, sums_ref[r : r + 1, lanes], part)
+                small_out[3 + t : 4 + t, :] = part
             for k in (CHUNKS - 2, CHUNKS - 1):
                 out_copy(jnp.int32(k))(lambda c: c.wait())
             given.wait()
+            result.wait()
 
         pl.run_scoped(last, pltpu.VMEM((2, 256, 3072), BF16), pltpu.VMEM((512, 1024), F32))
 
     pl.run_scoped(rest, pltpu.VMEM((512, 3072), BF16), pltpu.VMEM((1024, 512), BF16), pltpu.VMEM((512, 1024), BF16))
 
 
-def backward(arrays, lse, residual, x, gain1, gain2):
-    any_ = pl.BlockSpec(memory_space=pl.ANY)
-    vmem = pl.BlockSpec(memory_space=pltpu.VMEM)
-    hbm = pl.BlockSpec(memory_space=HBM)
+def backward(arrays, lse, vec):
+    any_, vmem, hbm = (pl.BlockSpec(memory_space=s) for s in (pl.ANY, pltpu.VMEM, HBM))
     n = CHUNKS
     dma = pltpu.SemaphoreType.DMA
     return pl.pallas_call(
         bwd_kernel,
-        in_specs=[any_] * len(arrays) + [vmem, any_, any_, vmem, vmem],
-        out_specs=[hbm] * 5 + [vmem],
+        in_specs=[any_] * len(arrays) + [vmem, vmem],
+        out_specs=[hbm] * 6 + [vmem],
         out_shape=[jax.ShapeDtypeStruct((128, w), F32) for w in (4096, 4096, 1024, 3072)]
-        + [jax.ShapeDtypeStruct((512, 1024), BF16), jax.ShapeDtypeStruct((16, 1024), F32)],
+        + [jax.ShapeDtypeStruct((2, 256, 1024), BF16)] * 2 + [jax.ShapeDtypeStruct((12, 128), F32)],
         scratch_shapes=[
+            pltpu.VMEM((16, 1024), F32), pltpu.VMEM((5, 16, 1024), F32),
             pltpu.VMEM((2, 512, 1024), BF16), pltpu.VMEM((2, 512, 1024), BF16), pltpu.VMEM((n, 2, 2, 128, 1024), BF16),
             pltpu.VMEM((n, 2, 128, 512), BF16), pltpu.VMEM((n, 2, 128, 512), BF16),
             pltpu.VMEM((n, 128, 512), BF16), pltpu.VMEM((n, 128, 512), BF16),
@@ -948,80 +1055,33 @@
             pltpu.VMEM((2, 128, 1024), F32), pltpu.VMEM((512, 2048), BF16), pltpu.VMEM((512, 1024), BF16),
             pltpu.VMEM((512, 1024), F32),
             dma((n,)), dma((n,)), dma((n, 4)), dma((n, 4)), dma((n, 3)), dma((n, 3)), dma((2,)), dma, dma, dma((12,)),
+            dma((2, 3, 2)), dma((5,)), dma((5,)),
         ],
         compiler_params=pltpu.CompilerParams(collective_id=8, has_side_effects=True, vmem_limit_bytes=67043328),
         cost_estimate=pl.CostEstimate(flops=40 * 10**9, bytes_accessed=60 << 20, transcendentals=10**7),
         name="backward",
-    )(*arrays, lse, residual, x, gain1, gain2)
+    )(*arrays, lse, vec)
 
 
 def local_fast(
     tokens, w_qkv, w_out, w_up, w_down, b_query, b_value, b_out, b_up, b_down,
     ln1_gain, ln1_bias, ln2_gain, ln2_bias, cotangent,
 ):
-    d = tokens.shape[2]
-    me = lax.axis_index("dp")
     small = (b_query, b_value, b_out, b_up, b_down, ln1_gain, ln1_bias, ln2_gain, ln2_bias)
-    sizes = [item.shape[0] for item in small]
-
-    x_low = gather_image(tokens)
-    pack = jnp.concatenate(small).reshape(1, -1)
-    for bits in (1, 2, 4):
-        pack = jnp.concatenate([pack, flip(pack, bits)])
-    packed = jnp.concatenate([lax.dynamic_slice_in_dim(pack, me ^ r, 1, axis=0) for r in range(8)])
-    vectors, at = [], 0
-    for size in sizes:
-        vectors.append(packed[:, at : at + size].reshape(1, -1).astype(F32))
-        at += size
-    bias_query, bias_value, bias_out, bias_up, bias_down, gain1, shift1, gain2, shift2 = vectors
-
-    qkv1 = first_hop(w_qkv)
-    qkv2 = second_hop(qkv1)
-    out1 = first_hop(after(w_out, *qkv1))
-    out2 = second_hop(out1)
-    up1 = first_hop(after(w_up, *qkv2))
-    up2 = second_hop(up1)
-    down1 = first_hop(after(w_down.T, *out2))
-    down2 = second_hop(down1)
-    wq = finish(qkv2, 0)
-    cot_low = gather_image(after(cotangent, x_low))
-
-    x = x_low.astype(F32)
-    xhat1, rstd1 = norm_parts(x)
-    n1 = (xhat1 * gain1 + shift1).astype(BF16)
-    bias = jnp.concatenate([bias_query, jnp.zeros_like(bias_query), bias_value], axis=1)
-    projected = (dot_nn(n1, wq) + bias).astype(BF16)
-    q, k, v = (projected[:, i * d : (i + 1) * d] for i in range(3))
-    kv_other = other_core(projected[:, d:])
-    kb, vb = kv_other[:, :d], kv_other[:, d:]
-    attended, lse = attn_fwd(q, k, kb, v, vb)
-    wo = finish(out2, 1)
-    residual = x + dot_nn(attended, wo) + bias_out
-    xhat2, rstd2 = norm_parts(residual)
-    n2 = (xhat2 * gain2 + shift2).astype(BF16)
-    wu = finish(up2, 2)
-    upward = dot_nn(n2, wu) + bias_up
-    act = activate(upward).astype(BF16)
-    wdt = finish(down2, 3)
-    result = return_image((residual + dg(act, wdt, NT) + bias_down).astype(BF16))
-
-    order = (0, 2, 4, 6, 1, 3, 5, 7)
-    turned = lambda value: relative(value, order, me).T
-    g_down, g_up, g_out, g_qkv, gin, rows = backward(
-        (cot_low, turned(cot_low), turned(n2), act, upward, wdt, wu, wo, wq, turned(attended), turned(n1),
-         q, k, kb, v, vb, attended), lse, residual, x_low, gain1, gain2)
-    grad_input = return_image(gin)
-    small_grads = (rows[10], rows[11], rows[4], rows[:4], rows[7], rows[8], rows[9], rows[5], rows[6])
-    sums = jnp.concatenate([g.reshape(8, -1) for g in small_grads], axis=1)
-    for bits in (1, 2, 4):
-        sums = lax.optimization_barrier(sums + flip(sums, bits))
-    for bits in (1, 2):
-        sums = lax.optimization_barrier(sums + flip_z(sums, bits))
-    mine = lax.dynamic_slice_in_dim(sums, me, 1, axis=0)[0]
+    pack, at = jnp.zeros((12, 128), F32), 0
+    for item in small:
+        rows = item.shape[0] // 128
+        pack = pack + jnp.pad(item.astype(F32).reshape(rows, 128), ((at, 12 - at - rows), (0, 0)))
+        at += rows
+    (wq, wo, wu, wd, x, cot, cot_t, n1_t, n2_t, att_t, qkv, kv, att, act, up, res, out, lse, vec) = forward(
+        tokens, cotangent, (w_qkv, w_out, w_up, w_down), pack)
+    g_down, g_up, g_out, g_qkv, result, grad_input, sums = backward(
+        (cot, cot_t, n2_t, act, up, wd, wu, wo, wq, att_t, n1_t, qkv, kv, att, out, res, x), lse, vec)
     outs, at = [], 0
-    for size in sizes:
-        outs.append(mine[at : at + size])
-        at += size
+    for item in small:
+        rows = item.shape[0] // 128
+        outs.append(sums[at : at + rows].reshape(-1))
+        at += rows
     return (result, grad_input, g_qkv, g_out, g_up, g_down.T, *outs)
 
 

time: 451 us -> 340 us (0.75)
  Pallas kernels: 220 us -> 326 us
  waiting for transfers between devices: 81.1 us -> 0 us
  local copies, waits for them, and re-layouts: 56.3 us -> 11.3 us
  starting transfers between devices: 42.3 us -> 0 us
  matrix products: 29.8 us -> 0 us
  other arithmetic: 18.9 us -> 1.4 us
    pallas_call x6 -> x2, Pallas kernels: 220 us -> 326 us  [the longest x1 205 us: backward(): pl.pallas_call(bwd_kernel, in_specs=[any_] * len(arrays) + [vmem, vmem],...]
    ppermute x33 -> x0, waiting for transfers between devices: 81.1 us -> none  [the longest x22 61.3 us: flip(): return lax.ppermute(value, 'dp', [(i, i ^ bits) for i in range(8)])]
    ppermute x33 -> x0, starting transfers between devices: 42.3 us -> none  [the longest x22 22.4 us: flip(): return lax.ppermute(value, 'dp', [(i, i ^ bits) for i in range(8)])]
    dot_general x4 -> x0, matrix products: 29.8 us -> none  [dg(): return lax.dot_general(a, b, dims, preferred_element_type=F32)]
    unnamed x140 -> x16, local copies, waits for them, and re-layouts: 28.3 us -> 8.63 us
    slice x7 -> x0, local copies, waits for them, and re-layouts: 10.6 us -> none  [the longest x1 3.23 us: local_fast(): q, k, v = (projected[:, i * d:(i + 1) * d] for i in range(3))]
    another operation x8 -> x0, other arithmetic: 8.69 us -> none  [first_hop(): return (jnp.stack([a, flip(a, 2)]), jnp.stack([b, flip(b, 4)]))]
    squeeze x4 -> x0, local copies, waits for them, and re-layouts: 6.56 us -> none  [the longest x2 3.28 us: return_image(): mine = lax.dynamic_index_in_dim(halves, odd ^ shift, 0, keepdims=False)]
  transfers between devices with their start and end apart: 33 -> 0, of which waited for: 13 -> 0; matrix products, arithmetic and copies ran while one was open for 12% -> 0% of each run, Pallas kernels for 6% -> 0%
where the time goes in v4:
time: 340 us
  Pallas kernels  326 us (96%)
  local copies, waits for them, and re-layouts  11.3 us (3%)
    pallas_call x1, Pallas kernels, backward(): pl.pallas_call(bwd_kernel, in_specs=[any_] * len(arrays) + [vmem, vmem],...  205 us
    pallas_call x1, Pallas kernels, forward(): pl.pallas_call(fwd_kernel, in_specs=[any_] * 6 + [vmem], out_specs=[hbm]...  121 us
    unnamed x16, local copies, waits for them, and re-layouts  8.63 us

profile of v4, /device:TPU:0, one launch (start us, length us, event | category | flops | bytes accessed | tf_op | source)
XLA Modules:
  0.0 339.8 jit_solution(10524283826915015055)
XLA Ops:
  0.6 1.4 convert_add_fusion.pack
  2.0 121.2 %forward.1 = (bf16[1024,3072]{1,0:T(8,128)(2,1)}, bf16[1024,1024]{1,0:T(8,128)(2,1)}, bf16[1024,4096]{1,0:T(8,128)(2,1)}, bf16[1024,4096]{1,0:T(8,128)(2,1)}, bf...) custom-call(bf16[2,256,1024]{2,1,0:T(8,128)(2,1)} %tok_hbm.1, ...), custom_call_target="tpu_custom_call" | custom-call | flops 20000000000 | bytes 62914560 | tf_op jit(solution)/shard_map/forward/pallas_call | solution.py:702
  123.2 205.3 %backward.1 = (f32[128,4096]{1,0:T(8,128)}, f32[128,4096]{1,0:T(8,128)}, f32[128,1024]{1,0:T(8,128)}, f32[128,3072]{1,0:T(8,128)}, bf16[2,256,1024]{2,1,0:T(8,12...) custom-call(bf16[512,1024]{1,0:T(8,128)(2,1)} %get-tuple-element.41.cot_hbm, ...), custom_call_target="tpu_custom_call" | custom-call | flops 40000000000 | bytes 62914560 | tf_op jit(solution)/shard_map/backward/pallas_call | solution.py:1043
  328.5 1.3 slice_bitcast_fusion
  329.7 1.4 slice_bitcast_fusion.1
  331.1 0.0 copy-start.3
  331.1 0.0 copy-start.2
  331.1 3.0 copy.30
  334.2 0.0 copy-done.3
  334.2 0.0 copy-start.1
  334.2 1.0 copy.36
  335.1 0.0 copy-done.2
  335.1 1.0 copy.37
  336.1 0.0 copy-done.1
  336.1 0.0 copy-start.4
  336.1 0.0 copy-start
  336.1 1.1 copy.38
  337.2 0.2 copy-done.4
  337.5 0.8 copy.39
  338.3 0.2 copy-done
  338.4 1.3 copy.40
Async XLA Ops:
  331.1 3.0 copy-start.3
  331.1 4.0 %copy-start.2 = (bf16[2,256,1024]{2,1,0:T(8,128)(2,1)S(1)}, bf16[2,256,1024]{2,1,0:T(8,128)(2,1)}, u32[]{:S(2)}) copy-start(bf16[2,256,1024]{2,1,0:T(8,128)(2,1)} %get-tuple-element.106) | copy-start | bytes 3145732
  334.2 1.9 copy-start.1
  336.1 1.4 copy-start.4
  336.1 2.3 copy-start

commit v5 on v4

--- a/solution.py
+++ b/solution.py
@@ -411,6 +411,7 @@
         d=d, z=z, core=core, x=x, y=y, par=par,
         sibling=(d + 1 - 2 * core, z), over_x=(d + 2 - 4 * x, z), over_y=(d + 4 - 8 * y, z),
         near_z=(d, z + 1 - 2 * par), far_z=(d, z + 2 - 4 * (z // 2)),
+        across=(d, 3 - z), mid=z * (3 - z) > 0,
         image=[(d - core + z // 2, 2 * core + b) for b in range(2)],
         home=(z // 2) == core,
     )
@@ -422,14 +423,18 @@
     )
 
 
-def greet(place, names):
+def greet(place, names, middle=False):
     barrier = pltpu.get_barrier_semaphore()
+    if middle:
+        @pl.when(place["mid"])
+        def _(): pl.semaphore_signal(barrier, inc=1, device_id=place["across"], device_id_type=MESH)
     for name in names:
         pl.semaphore_signal(barrier, inc=1, device_id=place[name], device_id_type=MESH)
     for b in range(2):
         @pl.when(jnp.logical_not(jnp.logical_and(place["home"], place["par"] == b)))
         def _(): pl.semaphore_signal(barrier, inc=1, device_id=place["image"][b], device_id_type=MESH)
-    pl.semaphore_wait(barrier, len(names) + 2 - place["home"].astype(jnp.int32))
+    extra = place["mid"].astype(jnp.int32) if middle else 0
+    pl.semaphore_wait(barrier, len(names) + 2 - place["home"].astype(jnp.int32) + extra)
 
 
 class Move:
@@ -715,6 +720,7 @@
 
 
 CHUNKS = 12
+SLOTS = 10
 
 
 def gelu_slope(u):
@@ -727,37 +733,35 @@
     cot_hbm, cot_t_hbm, n2_t_hbm, act_hbm, up_hbm, wd_hbm, wu_hbm, wo_hbm, wq_hbm, att_t_hbm, n1_t_hbm,
     qkv_hbm, kv_hbm, att_hbm, out_hbm, res_hbm, x_hbm, lse_ref, vec,
     gd_out, gu_out, go_out, gq_out, result_out, gin_out, small_out,
-    sums_ref, sum_in, so, sr, g, h1a, h1b, h2a, h2b, z1, z2, z3, fin, dkv_in, cot, gres,
+    sums_ref, sum_in, so, sr, g, h1a, h1b, h2a, h2b, z1, z2, fin, dkv_in, cot, gres, gub, n2_t,
     sib_s, sib_r, hop_s, hop_r, zs, zr, fin_sem, dkv_s, dkv_r, load, ms, ss, sm,
 ):
     p = device_map()
     x, y, core, par, z = p["x"], p["y"], p["core"], p["par"], p["z"]
     sibling, over_x, over_y, near_z, far_z = (p[n] for n in ("sibling", "over_x", "over_y", "near_z", "far_z"))
-    greet(p, ("sibling", "over_x", "over_y", "near_z", "far_z"))
+    greet(p, ("sibling", "over_x", "over_y", "near_z", "far_z"), True)
+    mid, across = p["mid"], p["across"]
 
     lo, hi = pl.ds(0, 512), pl.ds(512, 512)
-    keep = pl.ds(pl.multiple_of(par * 512, 512), 512)
-    give = pl.ds(pl.multiple_of((1 - par) * 512, 512), 512)
-
     def to_sib(k):
         return remote(so.at[lax.rem(k, 2)], sr.at[lax.rem(k, 2)], sib_s.at[k], sib_r.at[k], sibling)
 
     def hop(k, j):
         src, dst, to = (
-            (g.at[k, 1, :, :, lo], h1a.at[k], over_y),
-            (g.at[k, :, 1, :, hi], h1b.at[k], over_x),
-            (g.at[k, 0, 1, :, lo], h2a.at[k], over_x),
-            (g.at[k, 1, 0, :, hi], h2b.at[k], over_y),
+            (g.at[lax.rem(k, SLOTS), 1, :, :, lo], h1a.at[k], over_y),
+            (g.at[lax.rem(k, SLOTS), :, 1, :, hi], h1b.at[k], over_x),
+            (g.at[lax.rem(k, SLOTS), 0, 1, :, lo], h2a.at[k], over_x),
+            (g.at[lax.rem(k, SLOTS), 1, 0, :, hi], h2b.at[k], over_y),
         )[j]
         return remote(src, dst, hop_s.at[k, j], hop_r.at[k, j], to)
 
-    def zhop(k, j):
-        src, dst, to = (
-            (g.at[k, 0, 0, :, give], z1.at[k], near_z),
-            (g.at[k, 0, 0, :, keep], z2.at[k], far_z),
-            (g.at[k, 0, 0, :, keep], z3.at[k], near_z),
-        )[j]
-        return remote(src, dst, zs.at[k, j], zr.at[k, j], to)
+    def zhop(k, j, side):
+        cols = (lo, hi)[side]
+        dst, to = ((z1.at[k, :, cols], near_z), (z2.at[k, :, cols], across), (z2.at[k, :, cols], near_z))[j]
+        return remote(g.at[lax.rem(k, SLOTS), 0, 0, :, cols], dst, zs.at[k, 2 * j + side], zr.at[k, 2 * j + side], to)
+
+    def ends(run):
+        pl.when(jnp.logical_not(mid))(run)
 
     def plus(a, b):
         return (a.astype(F32) + b.astype(F32)).astype(BF16)
@@ -767,10 +771,10 @@
         def with_target(run):
             col = lambda j: pl.ds(pl.multiple_of(j * 1024, 1024), 1024)
             sem = fin_sem.at[slot]
-            @pl.when(jnp.logical_and(k < 8, lax.rem(k, 2) == 0))
-            def _(): run(pltpu.make_async_copy(fin.at[slot], gd_out.at[:, col(k // 2)], sem))
-            @pl.when(jnp.logical_and(k < 8, lax.rem(k, 2) == 1))
-            def _(): run(pltpu.make_async_copy(fin.at[slot], gu_out.at[:, col(k // 2)], sem))
+            @pl.when(k < 4)
+            def _(): run(pltpu.make_async_copy(fin.at[slot], gd_out.at[:, col(k)], sem))
+            @pl.when(jnp.logical_and(k >= 4, k < 8))
+            def _(): run(pltpu.make_async_copy(fin.at[slot], gu_out.at[:, col(k - 4)], sem))
             @pl.when(k == 8)
             def _(): run(pltpu.make_async_copy(fin.at[slot], go_out, sem))
             @pl.when(k > 8)
@@ -784,33 +788,51 @@
 
         def c2(k):
             hop(k, 0).wait(); hop(k, 1).wait()
-            g[k, 0, :, :, lo] = plus(g[k, 0, :, :, lo], h1a[k])
-            g[k, :, 0, :, hi] = plus(g[k, :, 0, :, hi], h1b[k])
+            g[lax.rem(k, SLOTS), 0, :, :, lo] = plus(g[lax.rem(k, SLOTS), 0, :, :, lo], h1a[k])
+            g[lax.rem(k, SLOTS), :, 0, :, hi] = plus(g[lax.rem(k, SLOTS), :, 0, :, hi], h1b[k])
             hop(k, 2).start(); hop(k, 3).start()
 
+        sides = ((0, lo), (1, hi))
+
         def c3(k):
-            hop(k, 2).wait(); hop(k, 3).wait()
-            g[k, 0, 0, :, lo] = plus(g[k, 0, 0, :, lo], h2a[k])
-            g[k, 0, 0, :, hi] = plus(g[k, 0, 0, :, hi], h2b[k])
-            zhop(k, 0).start()
+            for side, cols in sides:
+                hop(k, 2 + side).wait()
+                mine = (lax.rem(k, SLOTS), 0, 0, slice(None), cols)
+                g[mine] = plus(g[mine], (h2a, h2b)[side][k])
+                ends(lambda: zhop(k, 0, side).start())
 
         def c4(k):
-            zhop(k, 0).wait()
-            g[k, 0, 0, :, keep] = plus(g[k, 0, 0, :, keep], z1[k])
-            zhop(k, 1).start()
+            @pl.when(mid)
+            def _():
+                for side, cols in sides:
+                    zhop(k, 0, side).wait_recv()
+                    mine = (lax.rem(k, SLOTS), 0, 0, slice(None), cols)
+                    g[mine] = plus(g[mine], z1[k, :, cols])
+                    zhop(k, 1, side).start()
 
         def c5(k):
-            zhop(k, 1).wait()
-            g[k, 0, 0, :, keep] = plus(g[k, 0, 0, :, keep], z2[k])
-            zhop(k, 2).start()
+            @pl.when(mid)
+            def _():
+                for side, cols in sides:
+                    zhop(k, 1, side).wait()
+                    mine = (lax.rem(k, SLOTS), 0, 0, slice(None), cols)
+                    g[mine] = plus(g[mine], z2[k, :, cols])
+                    zhop(k, 2, side).start()
 
         def c6(k):
-            zhop(k, 2).wait()
             slot = lax.rem(k, 2)
             @pl.when(k >= 2)
             def _(): out_copy(k - 2)(lambda c: c.wait())
-            fin[slot, :, keep] = g[k, 0, 0, :, keep].astype(F32)
-            fin[slot, :, give] = z3[k].astype(F32)
+            @pl.when(mid)
+            def _():
+                fin[slot] = g[lax.rem(k, SLOTS), 0, 0].astype(F32)
+                for side in range(2): zhop(k, 2, side).wait_send()
+            def other():
+                for side, cols in sides:
+                    zhop(k, 0, side).wait_send()
+                    zhop(k, 2, side).wait_recv()
+                    fin[slot, :, cols] = z2[k, :, cols].astype(F32)
+            ends(other)
             out_copy(k)(lambda c: c.start())
 
         stage(n, c2); stage(n - 1, c3); stage(n - 2, c4); stage(n - 3, c5); stage(n - 4, c6)
@@ -818,15 +840,15 @@
     def send_odd(k, left, right):
         def one(cols):
             so[lax.rem(k, 2), :, cols] = dg(left[512:1024, :], right[:, cols], NN).astype(BF16)
-        tiles(4, one)
+        tiles(2, one, 512)
         to_sib(k).start()
 
     def add_even(k, left, right):
         to_sib(k).wait()
         def one(cols):
             part = dg(left[0:512, :], right[:, cols], NN) + sr[lax.rem(k, 2), :, cols].astype(F32)
-            g[k, :, :, :, cols] = part.astype(BF16).reshape(2, 2, 128, 256)
-        tiles(4, one)
+            g[lax.rem(k, SLOTS), :, :, :, cols] = part.astype(BF16).reshape(2, 2, 128, 512)
+        tiles(2, one, 512)
         hop(k, 0).start(); hop(k, 1).start()
 
     def fetch(src, dst, i):
@@ -838,45 +860,49 @@
     result.start()
     sums_ref[...] = jnp.zeros_like(sums_ref)
 
-    def mlp(cot_t, n2_t, actb, upb, wdb, wub, gub, gn2, resb):
+    def mlp(cot_t, actb, upb, wdb, wub, gn2, resb):
         pieces = [fetch(cot_t_hbm, cot_t, 1), fetch(n2_t_hbm, n2_t, 2), fetch(res_hbm, resb, 3)]
-        for c in pieces: c.start()
-        def parts(j):
-            cols = pl.ds(pl.multiple_of(j * 1024, 1024), 1024)
-            s = lax.rem(j, 2)
-            return [
-                pltpu.make_async_copy(src.at[:, cols], dst.at[s], load.at[4 + 4 * s + i])
-                for i, (src, dst) in enumerate(((act_hbm, actb), (up_hbm, upb), (wd_hbm, wdb), (wu_hbm, wub)))
-            ]
-        for c in parts(jnp.int32(0)): c.start()
+        def part(i, j):
+            src, dst = ((act_hbm, actb.at[lax.rem(j, 2)]), (up_hbm, upb), (wd_hbm, wdb), (wu_hbm, wub))[i]
+            sem = load.at[4 + i] if i else load.at[8 + lax.rem(j, 2)]
+            return pltpu.make_async_copy(src.at[:, pl.ds(pl.multiple_of(j * 1024, 1024), 1024)], dst, sem)
+        pieces[0].start()
+        for i in range(4): part(i, jnp.int32(0)).start()
+        for c in pieces[1:]: c.start()
         gn2[...] = jnp.zeros_like(gn2)
-        first.wait()
         pieces[0].wait()
-        pieces[1].wait()
         def block(j, carry):
-            s = lax.rem(j, 2)
-            for c in parts(j): c.wait()
-            @pl.when(j < 3)
-            def _():
-                for c in parts(j + 1): c.start()
-            kd, ku = 2 * j, 2 * j + 1
-            send_odd(kd, cot_t, actb.at[s])
+            acts = actb.at[lax.rem(j, 2)]
+            def more(*which):
+                @pl.when(j < 3)
+                def _():
+                    for i in which: part(i, j + 1).start()
+            part(0, j).wait()
+            more(0)
+            send_odd(j, cot_t, acts)
+            @pl.when(j == 0)
+            def _(): first.wait()
+            part(1, j).wait()
+            part(2, j).wait()
             def slope(cols):
-                back = dg(cot[...], wdb[s, :, cols], NN)
-                low = (back * gelu_slope(upb[s, :, cols])).astype(BF16)
-                gub[:, cols] = low
+                back = dg(cot[...], wdb[:, cols], NN)
+                low = (back * gelu_slope(upb[:, cols])).astype(BF16)
+                gub[:, pl.ds(pl.multiple_of(j * 1024 + cols.start, 256), 256)] = low
                 sums_ref[pl.ds(j, 1), cols] = jnp.sum(low.astype(F32), axis=0, keepdims=True)
             tiles(4, slope)
-            add_even(kd, cot_t, actb.at[s])
-            send_odd(ku, n2_t, gub)
+            more(1, 2)
+            add_even(j, cot_t, acts)
+            part(3, j).wait()
+            here = pl.ds(pl.multiple_of(j * 1024, 1024), 1024)
             def down(cols):
-                gn2[:, cols] += dg(gub[...], wub[s, cols, :], NT)
+                gn2[:, cols] += dg(gub[:, here], wub[cols, :], NT)
             tiles(4, down)
-            add_even(ku, n2_t, gub)
-            @pl.when(j > 0)
-            def _(): tick(j - 1)
+            more(3)
+            @pl.when(j == 2)
+            def _(): tick(jnp.int32(0))
             return carry
         lax.fori_loop(0, 4, block, 0)
+        pieces[1].wait()
         pieces[2].wait()
         def rows(r):
             res = resb[r, :]
@@ -895,73 +921,82 @@
         tiles(8, rows, 64)
 
     pl.run_scoped(
-        mlp, pltpu.VMEM((1024, 512), BF16), pltpu.VMEM((1024, 512), BF16), pltpu.VMEM((2, 512, 1024), BF16),
-        pltpu.VMEM((2, 512, 1024), F32), pltpu.VMEM((2, 1024, 1024), BF16), pltpu.VMEM((2, 1024, 1024), BF16),
-        pltpu.VMEM((512, 1024), BF16), pltpu.VMEM((512, 1024), F32), pltpu.VMEM((512, 1024), F32),
+        mlp, pltpu.VMEM((1024, 512), BF16), pltpu.VMEM((2, 512, 1024), BF16), pltpu.VMEM((512, 1024), F32),
+        pltpu.VMEM((1024, 1024), BF16), pltpu.VMEM((1024, 1024), BF16), pltpu.VMEM((512, 1024), F32),
+        pltpu.VMEM((512, 1024), F32),
     )
 
     def rest(dqkv, n1_t, xb):
         late = [fetch(n1_t_hbm, n1_t, 0), fetch(x_hbm, xb, 1)]
-        for c in late: c.start()
-
-        def attention(wo, att_t, ga, q, ka, kb, va, vb, att, do, dob):
+
+        def attention(wo, att_t, ga, kv, att, do):
             loads = [
                 fetch(src, dst, 2 + i) for i, (src, dst) in enumerate((
-                    (wo_hbm, wo), (att_t_hbm, att_t), (qkv_hbm.at[:, pl.ds(0, 1024)], q), (qkv_hbm.at[:, pl.ds(1024, 1024)], ka), (kv_hbm.at[:, pl.ds(0, 1024)], kb),
-                    (qkv_hbm.at[:, pl.ds(2048, 1024)], va), (kv_hbm.at[:, pl.ds(1024, 1024)], vb), (att_hbm, att),
+                    (wo_hbm, wo), (qkv_hbm, dqkv), (kv_hbm, kv), (att_hbm, att), (att_t_hbm, att_t),
                 ))
             ]
-            for c in loads: c.start()
-            tick(jnp.int32(3))
+            for c in loads + late: c.start()
             ga[...] = gres[...].astype(BF16)
-            for c in loads: c.wait()
-            send_odd(jnp.int32(8), att_t, ga)
+            tick(jnp.int32(1))
+            loads[0].wait()
             def mixed(cols):
                 do[:, cols] = dg(ga[...], wo[cols, :], NT).astype(BF16)
             tiles(4, mixed)
-            add_even(jnp.int32(8), att_t, ga)
+            for c in loads[1:4]: c.wait()
             lane = lax.broadcasted_iota(jnp.int32, (512, 128), 1)
+            def up_grad(m):
+                return gub.at[:, pl.ds(pl.multiple_of(m * 1024, 1024), 1024)]
             def pair(i, carry):
-                cols = pl.ds(pl.multiple_of(i * 128, 128), 128)
-                qs = q[:, cols] * jnp.asarray(0.125, BF16)
+                at = lambda base: pl.ds(pl.multiple_of(base + i * 128, 128), 128)
+                cols = at(0)
+                qs = dqkv[:, cols] * jnp.asarray(0.125, BF16)
                 dos = do[:, cols]
                 t = (dos.astype(F32) * att[:, cols].astype(F32)).T
                 dq, dk, dv = None, [None, None], [None, None]
                 plus_ = lambda a, b: b if a is None else a + b
+                sides = ((dqkv, at(1024), at(2048)), (kv, at(0), at(1024)))
                 for h in range(2):
                     sel = (lane < 64) if h == 0 else (lane >= 64)
                     qh = jnp.where(sel, qs, jnp.zeros_like(qs))
                     doh = jnp.where(sel, dos, jnp.zeros_like(dos))
                     delta = jnp.sum(t[64 * h : 64 * h + 64], axis=0, keepdims=True)
                     lse = lse_ref[i, h : h + 1, :]
-                    for n, (k_ref, v_ref) in enumerate(((ka, va), (kb, vb))):
-                        kk = k_ref[:, cols]
+                    for n, (ref, k_at, v_at) in enumerate(sides):
+                        kk = ref[:, k_at]
                         s = dg(kk, qh, NT)
-                        p = jnp.exp(s - lse)
-                        dp = dg(v_ref[:, cols], doh, NT)
-                        ds = (p * (dp - delta)).astype(BF16)
-                        dv[n] = plus_(dv[n], dg(p.astype(BF16), doh, NN))
+                        p_ = jnp.exp(s - lse)
+                        dp = dg(ref[:, v_at], doh, NT)
+                        ds = (p_ * (dp - delta)).astype(BF16)
+                        dv[n] = plus_(dv[n], dg(p_.astype(BF16), doh, NN))
                         dk[n] = plus_(dk[n], dg(ds, qh, NN))
                         dq = plus_(dq, dg(jnp.where(sel, kk, jnp.zeros_like(kk)), ds, TN))
-                at = lambda base: pl.ds(pl.multiple_of(base + i * 128, 128), 128)
-                dqkv[:, at(0)] = (dq * 0.125).T.astype(BF16)
-                dqkv[:, at(1024)] = dk[0].astype(BF16)
-                dqkv[:, at(2048)] = dv[0].astype(BF16)
-                dob[:, at(0)] = dk[1].astype(BF16)
-                dob[:, at(1024)] = dv[1].astype(BF16)
-                @pl.when(lax.rem(i, 3) == 1)
-                def _(): tick(4 + i // 3)
+                dqkv[:, cols] = (dq * 0.125).T.astype(BF16)
+                for n, (ref, k_at, v_at) in enumerate(sides):
+                    ref[:, k_at] = dk[n].astype(BF16)
+                    ref[:, v_at] = dv[n].astype(BF16)
+                m = i // 2
+                @pl.when(lax.rem(i, 2) == 1)
+                def _():
+                    send_odd(4 + m, n2_t, up_grad(m))
+                    tick(2 + m)
+                @pl.when(jnp.logical_and(lax.rem(i, 2) == 0, i > 0))
+                def _(): add_even(3 + m, n2_t, up_grad(m - 1))
                 return carry
             lax.fori_loop(0, 8, pair, 0)
-            swap = remote(dob, dkv_in, dkv_s, dkv_r, sibling)
+            swap = remote(kv, dkv_in, dkv_s, dkv_r, sibling)
             swap.start()
+            add_even(jnp.int32(7), n2_t, up_grad(jnp.int32(3)))
             late[0].wait()
+            loads[4].wait()
+            send_odd(jnp.int32(8), att_t, ga)
+            tick(jnp.int32(6))
+            add_even(jnp.int32(8), att_t, ga)
             send_odd(jnp.int32(9), n1_t, dqkv.at[:, pl.ds(0, 1024)])
             swap.wait()
 
         pl.run_scoped(
-            attention, pltpu.VMEM((1024, 1024), BF16), pltpu.VMEM((1024, 512), BF16),
-            *[pltpu.VMEM((512, 1024), BF16)] * 8, pltpu.VMEM((512, 2048), BF16),
+            attention, pltpu.VMEM((1024, 1024), BF16), pltpu.VMEM((1024, 512), BF16), pltpu.VMEM((512, 1024), BF16),
+            pltpu.VMEM((512, 2048), BF16), pltpu.VMEM((512, 1024), BF16), pltpu.VMEM((512, 1024), BF16),
         )
 
         def last(wq, gn1):
@@ -974,12 +1009,6 @@
                 dqkv[:, there] = plus(dqkv[:, there], dkv_in[:, cols])
             tiles(8, join)
             add_even(jnp.int32(9), n1_t, dqkv.at[:, pl.ds(0, 1024)])
-            for k in (10, 11):
-                right = dqkv.at[:, pl.ds(1024 * (k - 9), 1024)]
-                send_odd(jnp.int32(k), n1_t, right)
-                if k == 10:
-                    tick(jnp.int32(7))
-                add_even(jnp.int32(k), n1_t, right)
             def back(i, carry):
                 wq_part(i).wait()
                 @pl.when(i < 3)
@@ -987,7 +1016,6 @@
                 gn1[:, pl.ds(pl.multiple_of(i * 256, 256), 256)] = dg(dqkv[...], wq[lax.rem(i, 2)], NT)
                 return carry
             lax.fori_loop(0, 4, back, 0)
-            tick(jnp.int32(8))
             late[1].wait()
             def rows(r):
                 xx = xb[r, :].astype(F32)
@@ -1003,15 +1031,27 @@
                 add(8, grad * xhat); add(9, grad)
                 add(10, dqkv[r, 0:1024].astype(F32)); add(11, dqkv[r, 2048:3072].astype(F32))
             tiles(8, rows, 64)
-            given = Move(p, [xb.at[pl.ds(256 * h, 256)] for h in range(2)], lambda b: gin_out.at[b], ms.at[1])
-            given.start()
+            given = [
+                Move(p, [xb.at[pl.ds(256 * h + 64 * i, 64)] for h in range(2)],
+                     lambda b, i=i: gin_out.at[b, pl.ds(64 * i, 64)], ms.at[1 + i])
+                for i in range(4)
+            ]
             steps = [
                 remote(sums_ref, sum_in.at[i], ss.at[i], sm.at[i], to)
                 for i, to in enumerate((sibling, over_x, over_y, near_z, far_z))
             ]
             steps[0].start()
+            tick(jnp.int32(7))
+            given[0].start()
+            for k in (10, 11):
+                right = dqkv.at[:, pl.ds(1024 * (k - 9), 1024)]
+                send_odd(jnp.int32(k), n1_t, right)
+                if k == 10: tick(jnp.int32(8))
+                add_even(jnp.int32(k), n1_t, right)
+                if k == 10: given[1].start()
             for i in range(7):
                 tick(jnp.int32(9 + i))
+                if i < 2: given[2 + i].start()
                 if i < 5:
                     steps[i].wait()
                     sums_ref[...] += sum_in[i]
@@ -1028,7 +1068,7 @@
                 small_out[3 + t : 4 + t, :] = part
             for k in (CHUNKS - 2, CHUNKS - 1):
                 out_copy(jnp.int32(k))(lambda c: c.wait())
-            given.wait()
+            for move in given: move.wait()
             result.wait()
 
         pl.run_scoped(last, pltpu.VMEM((2, 256, 3072), BF16), pltpu.VMEM((512, 1024), F32))
@@ -1048,14 +1088,14 @@
         + [jax.ShapeDtypeStruct((2, 256, 1024), BF16)] * 2 + [jax.ShapeDtypeStruct((12, 128), F32)],
         scratch_shapes=[
             pltpu.VMEM((16, 1024), F32), pltpu.VMEM((5, 16, 1024), F32),
-            pltpu.VMEM((2, 512, 1024), BF16), pltpu.VMEM((2, 512, 1024), BF16), pltpu.VMEM((n, 2, 2, 128, 1024), BF16),
+            pltpu.VMEM((2, 512, 1024), BF16), pltpu.VMEM((2, 512, 1024), BF16), pltpu.VMEM((SLOTS, 2, 2, 128, 1024), BF16),
             pltpu.VMEM((n, 2, 128, 512), BF16), pltpu.VMEM((n, 2, 128, 512), BF16),
             pltpu.VMEM((n, 128, 512), BF16), pltpu.VMEM((n, 128, 512), BF16),
-            pltpu.VMEM((n, 128, 512), BF16), pltpu.VMEM((n, 128, 512), BF16), pltpu.VMEM((n, 128, 512), BF16),
+            pltpu.VMEM((n, 128, 1024), BF16), pltpu.VMEM((n, 128, 1024), BF16),
             pltpu.VMEM((2, 128, 1024), F32), pltpu.VMEM((512, 2048), BF16), pltpu.VMEM((512, 1024), BF16),
-            pltpu.VMEM((512, 1024), F32),
-            dma((n,)), dma((n,)), dma((n, 4)), dma((n, 4)), dma((n, 3)), dma((n, 3)), dma((2,)), dma, dma, dma((12,)),
-            dma((2, 3, 2)), dma((5,)), dma((5,)),
+            pltpu.VMEM((512, 1024), F32), pltpu.VMEM((512, 4096), BF16), pltpu.VMEM((1024, 512), BF16),
+            dma((n,)), dma((n,)), dma((n, 4)), dma((n, 4)), dma((n, 6)), dma((n, 6)), dma((2,)), dma, dma, dma((12,)),
+            dma((5, 3, 2)), dma((5,)), dma((5,)),
         ],
         compiler_params=pltpu.CompilerParams(collective_id=8, has_side_effects=True, vmem_limit_bytes=67043328),
         cost_estimate=pl.CostEstimate(flops=40 * 10**9, bytes_accessed=60 << 20, transcendentals=10**7),

time: 340 us -> 309 us (0.909)
  Pallas kernels: 326 us -> 296 us
    pallas_call x1, Pallas kernels: 205 us -> 174 us  [backward(): pl.pallas_call(bwd_kernel, in_specs=[any_] * len(arrays) + [vmem, vmem],...]
where the time goes in v5:
time: 309 us
  Pallas kernels  296 us (96%)
  local copies, waits for them, and re-layouts  11.3 us (4%)
    pallas_call x1, Pallas kernels, backward(): pl.pallas_call(bwd_kernel, in_specs=[any_] * len(arrays) + [vmem, vmem],...  174 us
    pallas_call x1, Pallas kernels, forward(): pl.pallas_call(fwd_kernel, in_specs=[any_] * 6 + [vmem], out_specs=[hbm]...  121 us
    unnamed x16, local copies, waits for them, and re-layouts  8.63 us

profile of v5, /device:TPU:0, one launch (start us, length us, event | category | flops | bytes accessed | tf_op | source)
XLA Modules:
  0.0 308.9 jit_solution(11817307892014158035)
XLA Ops:
  0.6 1.4 convert_add_fusion.pack
  2.0 121.2 %forward.1 = (bf16[1024,3072]{1,0:T(8,128)(2,1)}, bf16[1024,1024]{1,0:T(8,128)(2,1)}, bf16[1024,4096]{1,0:T(8,128)(2,1)}, bf16[1024,4096]{1,0:T(8,128)(2,1)}, bf...) custom-call(bf16[2,256,1024]{2,1,0:T(8,128)(2,1)} %tok_hbm.1, ...), custom_call_target="tpu_custom_call" | custom-call | flops 20000000000 | bytes 62914560 | tf_op jit(solution)/shard_map/forward/pallas_call | solution.py:707
  123.2 174.4 %backward.1 = (f32[128,4096]{1,0:T(8,128)}, f32[128,4096]{1,0:T(8,128)}, f32[128,1024]{1,0:T(8,128)}, f32[128,3072]{1,0:T(8,128)}, bf16[2,256,1024]{2,1,0:T(8,12...) custom-call(bf16[512,1024]{1,0:T(8,128)(2,1)} %get-tuple-element.41.cot_hbm, ...), custom_call_target="tpu_custom_call" | custom-call | flops 40000000000 | bytes 62914560 | tf_op jit(solution)/shard_map/backward/pallas_call | solution.py:1083
  297.6 1.3 slice_bitcast_fusion
  298.9 1.4 slice_bitcast_fusion.1
  300.2 0.0 copy-start.3
  300.2 0.0 copy-start.2
  300.3 3.0 copy.30
  303.3 0.0 copy-done.3
  303.3 0.0 copy-start.1
  303.3 1.0 copy.36
  304.3 0.0 copy-done.2
  304.3 1.0 copy.37
  305.2 0.0 copy-done.1
  305.2 0.0 copy-start.4
  305.2 0.0 copy-start
  305.2 1.1 copy.38
  306.4 0.2 copy-done.4
  306.6 0.8 copy.39
  307.4 0.2 copy-done
  307.6 1.3 copy.40
Async XLA Ops:
  300.2 3.0 copy-start.3
  300.2 4.0 %copy-start.2 = (bf16[2,256,1024]{2,1,0:T(8,128)(2,1)S(1)}, bf16[2,256,1024]{2,1,0:T(8,128)(2,1)}, u32[]{:S(2)}) copy-start(bf16[2,256,1024]{2,1,0:T(8,128)(2,1)} %get-tuple-element.106) | copy-start | bytes 3145732
  303.3 1.9 copy-start.1
  305.2 1.4 copy-start.4
  305.2 2.3 copy-start

commit v6 on v5

--- a/solution.py
+++ b/solution.py
@@ -476,14 +476,14 @@
 
 def fwd_kernel(
     tok_hbm, cotg_hbm, wq_s, wo_s, wu_s, wd_s, pack,
-    wq_o, wo_o, wu_o, wd_o, x_o, cot_o, cot_t_o, n1_t_o, n2_t_o, att_t_o, qkv_o, kv_o, att_o, act_o, up_o, res_o, out_o,
+    wq_o, wo_o, wu_o, wd_o, x_o, cot_o, n1_t_o, n2_t_o, att_t_o, qkv_o, kv_o, att_o, up_o, res_o, out_o, gd_o,
     lse, vec,
-    wq, wo, wu, wd, wdn, pk, xb, cot, n1, n2, qkv, kv, att, act, upb, up_bias, res, cot_t, n1_t, n2_t, att_t,
-    ws, wr, wl, ps, pr, ms, kvs, kvr, outs, ups,
+    wq, wo, wu, wd, wdn, pk, xb, cot, n1, n2, qkv, kv, att, act, upb, up_bias, res, cot_t, n1_t, n2_t, att_t, so, sr, gs,
+    sib_s, sib_r, ws, wr, wl, ps, pr, ms, kvs, kvr, outs, ups,
 ):
     p = device_map()
     y, x, core, par = p["y"], p["x"], p["core"], p["par"]
-    greet(p, ("sibling", "over_x", "over_y"))
+    greet(p, ("sibling", "over_x", "over_y", "near_z"))
 
     def rows(py, px):
         return pl.ds(pl.multiple_of(((py * 2 + px) * 2 + core) * 128, 128), 128)
@@ -492,18 +492,31 @@
               (wd, None, 0, 2048), (wd, None, 2048, 2048)]
     me, bx, by, diag = rows(y, x), rows(y, 1 - x), rows(1 - y, x), rows(1 - y, 1 - x)
 
+    shared = (2, 3)
+
     def copy(n, i):
         w, shard, at, size = chunks[n]
-        lo, hi, full = pl.ds(at, size // 2), pl.ds(at + size // 2, size // 2), pl.ds(at, size)
+        full = part = pl.ds(at, size)
+        lo, hi = pl.ds(at, size // 2), pl.ds(at + size // 2, size // 2)
+        rest = None
+        if n in shared:
+            start_at = lambda by: pl.multiple_of(at + by, 512)
+            part, rest = pl.ds(start_at(par * 1024), 1024), pl.ds(start_at((1 - par) * 1024), 1024)
+            lo, hi = pl.ds(start_at(par * 1024), 512), pl.ds(start_at(par * 1024 + 512), 512)
         own = (lambda cols: w.at[me, cols]) if shard is None else (lambda cols: shard.at[:, cols])
         src, dst, to = (
             (own(lo), w.at[me, lo], "over_x"), (own(hi), w.at[me, hi], "over_y"),
             (own(hi), w.at[me, hi], "over_x"), (own(lo), w.at[me, lo], "over_y"),
             (own(full), w.at[me, full], "sibling"),
             (w.at[bx, lo], w.at[bx, lo], "over_y"), (w.at[by, hi], w.at[by, hi], "over_x"),
-            (w.at[bx, full], w.at[bx, full], "sibling"), (w.at[by, full], w.at[by, full], "sibling"),
+            (w.at[bx, part], w.at[bx, part], "sibling"), (w.at[by, part], w.at[by, part], "sibling"),
             (w.at[diag, lo], w.at[diag, lo], "sibling"), (w.at[diag, hi], w.at[diag, hi], "sibling"),
-        )[i]
+        )[i] if i < 11 else (
+            (w.at[bx, part], w.at[bx, part], "near_z"), (w.at[by, part], w.at[by, part], "near_z"),
+            (w.at[diag, part], w.at[diag, part], "near_z"),
+            (w.at[bx, rest], w.at[bx, rest], "sibling"), (w.at[by, rest], w.at[by, rest], "sibling"),
+            (w.at[diag, rest], w.at[diag, rest], "sibling"),
+        )[i - 11]
         return remote(src, dst, ws.at[n, i], wr.at[n, i], p[to])
 
     def start(n, *which):
@@ -528,10 +541,19 @@
     def late(n):
         wait(n, 2, 3)
         start(n, 7, 8)
+        if n in shared: start(n, 11, 12)
 
     def end(n):
         wait(n, 5, 6)
         start(n, 9, 10)
+        if n in shared: start(n, 13)
+        else: settle_chunk(n)
+
+    def settle_chunk(n):
+        if n in shared:
+            wait(n, 11, 12, 13)
+            start(n, 14, 15, 16)
+            wait(n, 14, 15, 16)
         wait(n, 4, 7, 8, 9, 10)
         if chunks[n][1] is not None: local(n).wait()
 
@@ -627,19 +649,25 @@
             ls.append(m + jnp.log(total))
         att[:, at(0)] = jnp.concatenate(outs_, axis=0).T.astype(BF16)
         lse[i] = jnp.concatenate(ls + [jnp.zeros((6, 512), F32)], axis=0)
-        @pl.when(i == 2)
+        @pl.when(i == 1)
         def _():
             late(1)
             end(1)
-            mid(2)
+            late(2)
+        @pl.when(i == 3)
+        def _():
+            end(2)
+            mid(3)
+        @pl.when(i == 6)
+        def _():
+            late(3)
+            end(3)
         return carry
+    mid(2)
     lax.fori_loop(0, 8, pair, 0)
+    mid(4)
     give(wo, wo_o)
     give(att, att_o)
-    late(2)
-    end(2)
-    mid(3)
-
     def out_cols(c):
         res[:, c] = xb[:, c].astype(F32) + dg(att[...], wo[:, c], NN) + vec[6:7, c]
     tiles(4, out_cols)
@@ -660,37 +688,59 @@
             act[:, c] = (0.5 * u * (1.0 + jnp.tanh(0.7978845608028654 * (u + 0.044715 * u * u * u)))).astype(BF16)
         up_copy(i).start()
         return carry
-    lax.fori_loop(0, 4, up_block, 0)
+    def to_sib(k):
+        return remote(so.at[k % 2], sr.at[k % 2], sib_s.at[k], sib_r.at[k], p["sibling"])
+
+    def down_odd(k):
+        def one(cols):
+            so[k % 2, :, cols] = dg(cot_t[512:1024, :], act[:, pl.ds(pl.multiple_of(1024 * k + cols.start, 512), 512)], NN).astype(BF16)
+        tiles(2, one, 512)
+        to_sib(k).start()
+
+    def down_even(k):
+        to_sib(k).wait()
+        def one(cols):
+            part = dg(cot_t[0:512, :], act[:, pl.ds(pl.multiple_of(1024 * k + cols.start, 512), 512)], NN)
+            gs[k, :, :, :, cols] = (part + sr[k % 2, :, cols].astype(F32)).astype(BF16).reshape(2, 2, 128, 512)
+        tiles(2, one, 512)
+        give(gs.at[k], gd_o.at[k])
+
     turn(p, n2, n2_t)
     give(n2_t, n2_t_o)
-    turn(p, att, att_t)
-    give(att_t, att_t_o)
+    settle_chunk(2)
+    lax.fori_loop(0, 4, up_block, 0)
     cot_move.wait()
+    turn(p, cot, cot_t)
     give(cot, cot_o)
-    turn(p, cot, cot_t)
-    give(cot_t, cot_t_o)
-    late(3)
-    end(3)
-    give(wu, wu_o)
-    mid(4)
-    lax.fori_loop(4, 8, up_block, 0)
-    give(act, act_o)
     late(4)
+    down_odd(0)
     end(4)
+    down_even(0)
+    down_odd(1)
     settle(res_given)
     first, second = pl.ds(0, 2048), pl.ds(2048, 2048)
     def half_down(c):
         res[:, c] += dg(act[:, first], wd[c, first], NT)
     tiles(4, half_down)
     mid(5)
+    down_even(1)
+    turn(p, att, att_t)
+    give(att_t, att_t_o)
+    settle_chunk(3)
+    give(wu, wu_o)
+    lax.fori_loop(4, 8, up_block, 0)
     late(5)
+    down_odd(2)
     end(5)
     give(wd, wd_o)
     settle(x_given)
+    down_even(2)
+    down_odd(3)
     def finish_cols(c):
         xb[:, c] = (res[:, c] + dg(act[:, second], wd[c, second], NT) + vec[7:8, c]).astype(BF16)
     tiles(4, finish_cols)
     give(xb, out_o)
+    down_even(3)
     for c in given:
         if not any(c is s for s in settled): c.wait()
     up_copy(jnp.int32(6)).wait()
@@ -702,8 +752,8 @@
     dma = pltpu.SemaphoreType.DMA
     wide = [((1024, 3072), BF16), ((1024, 1024), BF16), ((1024, 4096), BF16), ((1024, 4096), BF16)]
     rows, turned = ((512, 1024), BF16), ((1024, 512), BF16)
-    shapes = wide + [rows, rows] + [turned] * 4 + [
-        ((512, 3072), BF16), ((512, 2048), BF16), rows, ((512, 4096), BF16), ((512, 4096), F32), ((512, 1024), F32), rows]
+    shapes = wide + [rows, rows] + [turned] * 3 + [
+        ((512, 3072), BF16), ((512, 2048), BF16), rows, ((512, 4096), F32), ((512, 1024), F32), rows, ((4, 2, 2, 128, 1024), BF16)]
     return pl.pallas_call(
         fwd_kernel,
         in_specs=[any_] * 6 + [vmem],
@@ -711,8 +761,9 @@
         out_shape=[jax.ShapeDtypeStruct(*s) for s in shapes + [((8, 8, 512), F32), ((16, 1024), F32)]],
         scratch_shapes=[pltpu.VMEM(*s) for s in wide + [
             ((4096, 128), BF16), ((2, 2, 2, 12, 128), F32), rows, rows, rows, rows, ((512, 3072), BF16), ((512, 2048), BF16),
-            rows, ((512, 4096), BF16), ((2, 512, 512), F32), ((1, 4096), F32), ((512, 1024), F32)] + [turned] * 4]
-        + [dma((6, 11)), dma((6, 11)), dma((6,)), dma((3,)), dma((3,)), dma((2, 3, 2)), dma, dma, dma((20,)), dma((2,))],
+            rows, ((512, 4096), BF16), ((2, 512, 512), F32), ((1, 4096), F32), ((512, 1024), F32)] + [turned] * 4 + [
+            ((2, 512, 1024), BF16), ((2, 512, 1024), BF16), ((4, 2, 2, 128, 1024), BF16)]]
+        + [dma((4,)), dma((4,)), dma((6, 17)), dma((6, 17)), dma((6,)), dma((3,)), dma((3,)), dma((2, 3, 2)), dma, dma, dma((20,)), dma((2,))],
         compiler_params=pltpu.CompilerParams(collective_id=7, has_side_effects=True, vmem_limit_bytes=67043328),
         cost_estimate=pl.CostEstimate(flops=20 * 10**9, bytes_accessed=60 << 20, transcendentals=10**7),
         name="forward",
@@ -730,7 +781,7 @@
 
 
 def bwd_kernel(
-    cot_hbm, cot_t_hbm, n2_t_hbm, act_hbm, up_hbm, wd_hbm, wu_hbm, wo_hbm, wq_hbm, att_t_hbm, n1_t_hbm,
+    cot_hbm, gd_hbm, n2_t_hbm, up_hbm, wd_hbm, wu_hbm, wo_hbm, wq_hbm, att_t_hbm, n1_t_hbm,
     qkv_hbm, kv_hbm, att_hbm, out_hbm, res_hbm, x_hbm, lse_ref, vec,
     gd_out, gu_out, go_out, gq_out, result_out, gin_out, small_out,
     sums_ref, sum_in, so, sr, g, h1a, h1b, h2a, h2b, z1, z2, fin, dkv_in, cot, gres, gub, n2_t,
@@ -791,6 +842,9 @@
             g[lax.rem(k, SLOTS), 0, :, :, lo] = plus(g[lax.rem(k, SLOTS), 0, :, :, lo], h1a[k])
             g[lax.rem(k, SLOTS), :, 0, :, hi] = plus(g[lax.rem(k, SLOTS), :, 0, :, hi], h1b[k])
             hop(k, 2).start(); hop(k, 3).start()
+            @pl.when(k == 0)
+            def _():
+                hop(k + 3, 0).start(); hop(k + 3, 1).start()
 
         sides = ((0, lo), (1, hi))
 
@@ -860,50 +914,46 @@
     result.start()
     sums_ref[...] = jnp.zeros_like(sums_ref)
 
-    def mlp(cot_t, actb, upb, wdb, wub, gn2, resb):
-        pieces = [fetch(cot_t_hbm, cot_t, 1), fetch(n2_t_hbm, n2_t, 2), fetch(res_hbm, resb, 3)]
+    def mlp(upb, wdb, wub, gn2, resb):
+        sums4 = fetch(gd_hbm, g.at[pl.ds(0, 4)], 1)
+        pieces = [fetch(n2_t_hbm, n2_t, 2), fetch(res_hbm, resb, 3)]
         def part(i, j):
-            src, dst = ((act_hbm, actb.at[lax.rem(j, 2)]), (up_hbm, upb), (wd_hbm, wdb), (wu_hbm, wub))[i]
-            sem = load.at[4 + i] if i else load.at[8 + lax.rem(j, 2)]
-            return pltpu.make_async_copy(src.at[:, pl.ds(pl.multiple_of(j * 1024, 1024), 1024)], dst, sem)
-        pieces[0].start()
-        for i in range(4): part(i, jnp.int32(0)).start()
-        for c in pieces[1:]: c.start()
+            src, dst = ((up_hbm, upb), (wd_hbm, wdb), (wu_hbm, wub))[i]
+            return pltpu.make_async_copy(src.at[:, pl.ds(pl.multiple_of(j * 1024, 1024), 1024)], dst, load.at[4 + i])
+        sums4.start()
+        for i in range(3): part(i, jnp.int32(0)).start()
+        for c in pieces: c.start()
+        sums4.wait()
+        for k in range(3):
+            hop(jnp.int32(k), 0).start()
+            hop(jnp.int32(k), 1).start()
         gn2[...] = jnp.zeros_like(gn2)
-        pieces[0].wait()
+        first.wait()
         def block(j, carry):
-            acts = actb.at[lax.rem(j, 2)]
             def more(*which):
                 @pl.when(j < 3)
                 def _():
                     for i in which: part(i, j + 1).start()
             part(0, j).wait()
-            more(0)
-            send_odd(j, cot_t, acts)
-            @pl.when(j == 0)
-            def _(): first.wait()
             part(1, j).wait()
-            part(2, j).wait()
             def slope(cols):
                 back = dg(cot[...], wdb[:, cols], NN)
                 low = (back * gelu_slope(upb[:, cols])).astype(BF16)
                 gub[:, pl.ds(pl.multiple_of(j * 1024 + cols.start, 256), 256)] = low
                 sums_ref[pl.ds(j, 1), cols] = jnp.sum(low.astype(F32), axis=0, keepdims=True)
             tiles(4, slope)
-            more(1, 2)
-            add_even(j, cot_t, acts)
-            part(3, j).wait()
+            more(0, 1)
+            part(2, j).wait()
             here = pl.ds(pl.multiple_of(j * 1024, 1024), 1024)
             def down(cols):
                 gn2[:, cols] += dg(gub[:, here], wub[cols, :], NT)
             tiles(4, down)
-            more(3)
+            more(2)
             @pl.when(j == 2)
             def _(): tick(jnp.int32(0))
             return carry
         lax.fori_loop(0, 4, block, 0)
-        pieces[1].wait()
-        pieces[2].wait()
+        for c in pieces: c.wait()
         def rows(r):
             res = resb[r, :]
             centre = jnp.mean(res, axis=-1, keepdims=True)
@@ -921,7 +971,7 @@
         tiles(8, rows, 64)
 
     pl.run_scoped(
-        mlp, pltpu.VMEM((1024, 512), BF16), pltpu.VMEM((2, 512, 1024), BF16), pltpu.VMEM((512, 1024), F32),
+        mlp, pltpu.VMEM((512, 1024), F32),
         pltpu.VMEM((1024, 1024), BF16), pltpu.VMEM((1024, 1024), BF16), pltpu.VMEM((512, 1024), F32),
         pltpu.VMEM((512, 1024), F32),
     )
@@ -1113,10 +1163,10 @@
         rows = item.shape[0] // 128
         pack = pack + jnp.pad(item.astype(F32).reshape(rows, 128), ((at, 12 - at - rows), (0, 0)))
         at += rows
-    (wq, wo, wu, wd, x, cot, cot_t, n1_t, n2_t, att_t, qkv, kv, att, act, up, res, out, lse, vec) = forward(
+    (wq, wo, wu, wd, x, cot, n1_t, n2_t, att_t, qkv, kv, att, up, res, out, gd, lse, vec) = forward(
         tokens, cotangent, (w_qkv, w_out, w_up, w_down), pack)
     g_down, g_up, g_out, g_qkv, result, grad_input, sums = backward(
-        (cot, cot_t, n2_t, act, up, wd, wu, wo, wq, att_t, n1_t, qkv, kv, att, out, res, x), lse, vec)
+        (cot, gd, n2_t, up, wd, wu, wo, wq, att_t, n1_t, qkv, kv, att, out, res, x), lse, vec)
     outs, at = [], 0
     for item in small:
         rows = item.shape[0] // 128

time: 309 us -> 295 us (0.955)
  Pallas kernels: 296 us -> 281 us
    pallas_call x1, Pallas kernels: 174 us -> 161 us  [backward(): pl.pallas_call(bwd_kernel, in_specs=[any_] * len(arrays) + [vmem, vmem],...]
where the time goes in v6:
time: 295 us
  Pallas kernels  281 us (95%)
  local copies, waits for them, and re-layouts  11.3 us (4%)
    pallas_call x1, Pallas kernels, backward(): pl.pallas_call(bwd_kernel, in_specs=[any_] * len(arrays) + [vmem, vmem],...  161 us
    pallas_call x1, Pallas kernels, forward(): pl.pallas_call(fwd_kernel, in_specs=[any_] * 6 + [vmem], out_specs=[hbm]...  120 us
    unnamed x16, local copies, waits for them, and re-layouts  8.63 us

profile of v6, /device:TPU:0, one launch (start us, length us, event | category | flops | bytes accessed | tf_op | source)
XLA Modules:
  0.0 294.8 jit_solution(4429024111610514392)
XLA Ops:
  0.6 1.4 convert_add_fusion.pack
  2.0 120.1 %forward.1 = (bf16[1024,3072]{1,0:T(8,128)(2,1)}, bf16[1024,1024]{1,0:T(8,128)(2,1)}, bf16[1024,4096]{1,0:T(8,128)(2,1)}, bf16[1024,4096]{1,0:T(8,128)(2,1)}, bf...) custom-call(bf16[2,256,1024]{2,1,0:T(8,128)(2,1)} %tok_hbm.1, ...), custom_call_target="tpu_custom_call" | custom-call | flops 20000000000 | bytes 62914560 | tf_op jit(solution)/shard_map/forward/pallas_call | solution.py:757
  122.1 161.4 %backward.1 = (f32[128,4096]{1,0:T(8,128)}, f32[128,4096]{1,0:T(8,128)}, f32[128,1024]{1,0:T(8,128)}, f32[128,3072]{1,0:T(8,128)}, bf16[2,256,1024]{2,1,0:T(8,12...) custom-call(bf16[512,1024]{1,0:T(8,128)(2,1)} %get-tuple-element.40.cot_hbm, ...), custom_call_target="tpu_custom_call" | custom-call | flops 40000000000 | bytes 62914560 | tf_op jit(solution)/shard_map/backward/pallas_call | solution.py:1133
  283.5 1.3 slice_bitcast_fusion
  284.8 1.4 slice_bitcast_fusion.1
  286.1 0.0 copy-start.3
  286.1 0.0 copy-start.2
  286.2 3.0 %copy.30 = f32[4096,128]{1,0:T(8,128)} copy(f32[4096,128]{0,1:T(8,128)} %bitcast.28) | data formatting | bytes 4194304
  289.2 0.0 copy-done.3
  289.2 0.0 copy-start.1
  289.2 1.0 copy.36
  290.2 0.0 copy-done.2
  290.2 1.0 copy.37
  291.1 0.0 copy-done.1
  291.1 0.0 copy-start.4
  291.1 0.0 copy-start
  291.1 1.1 copy.38
  292.3 0.2 copy-done.4
  292.5 0.8 copy.39
  293.3 0.2 copy-done
  293.5 1.3 copy.40
Async XLA Ops:
  286.1 3.0 %copy-start.3 = (bf16[2,256,1024]{2,1,0:T(8,128)(2,1)S(1)}, bf16[2,256,1024]{2,1,0:T(8,128)(2,1)}, u32[]{:S(2)}) copy-start(bf16[2,256,1024]{2,1,0:T(8,128)(2,1)} %get-tuple-element.103) | copy-start | bytes 3145732
  286.1 4.0 %copy-start.2 = (bf16[2,256,1024]{2,1,0:T(8,128)(2,1)S(1)}, bf16[2,256,1024]{2,1,0:T(8,128)(2,1)}, u32[]{:S(2)}) copy-start(bf16[2,256,1024]{2,1,0:T(8,128)(2,1)} %get-tuple-element.104) | copy-start | bytes 3145732
  289.2 1.9 copy-start.1
  291.1 1.4 copy-start.4
  291.1 2.3 copy-start

commit v7 on v6

--- a/solution.py
+++ b/solution.py
@@ -842,9 +842,9 @@
             g[lax.rem(k, SLOTS), 0, :, :, lo] = plus(g[lax.rem(k, SLOTS), 0, :, :, lo], h1a[k])
             g[lax.rem(k, SLOTS), :, 0, :, hi] = plus(g[lax.rem(k, SLOTS), :, 0, :, hi], h1b[k])
             hop(k, 2).start(); hop(k, 3).start()
-            @pl.when(k == 0)
+            @pl.when(k < 7)
             def _():
-                hop(k + 3, 0).start(); hop(k + 3, 1).start()
+                hop(k + 2, 0).start(); hop(k + 2, 1).start()
 
         sides = ((0, lo), (1, hi))
 
@@ -889,7 +889,7 @@
             ends(other)
             out_copy(k)(lambda c: c.start())
 
-        stage(n, c2); stage(n - 1, c3); stage(n - 2, c4); stage(n - 3, c5); stage(n - 4, c6)
+        stage(n - 3, c5); stage(n - 2, c4); stage(n - 1, c3); stage(n, c2); stage(n - 4, c6)
 
     def send_odd(k, left, right):
         def one(cols):
@@ -903,7 +903,9 @@
             part = dg(left[0:512, :], right[:, cols], NN) + sr[lax.rem(k, 2), :, cols].astype(F32)
             g[lax.rem(k, SLOTS), :, :, :, cols] = part.astype(BF16).reshape(2, 2, 128, 512)
         tiles(2, one, 512)
-        hop(k, 0).start(); hop(k, 1).start()
+        @pl.when(k > 8)
+        def _():
+            hop(k, 0).start(); hop(k, 1).start()
 
     def fetch(src, dst, i):
         return pltpu.make_async_copy(src, dst, load.at[i])
@@ -913,6 +915,9 @@
     result = Move(p, [out_hbm.at[pl.ds(256 * h, 256)] for h in range(2)], lambda b: result_out.at[b], ms.at[0])
     result.start()
     sums_ref[...] = jnp.zeros_like(sums_ref)
+
+    def up_grad(m):
+        return gub.at[:, pl.ds(pl.multiple_of(m * 1024, 1024), 1024)]
 
     def mlp(upb, wdb, wub, gn2, resb):
         sums4 = fetch(gd_hbm, g.at[pl.ds(0, 4)], 1)
@@ -924,7 +929,7 @@
         for i in range(3): part(i, jnp.int32(0)).start()
         for c in pieces: c.start()
         sums4.wait()
-        for k in range(3):
+        for k in range(2):
             hop(jnp.int32(k), 0).start()
             hop(jnp.int32(k), 1).start()
         gn2[...] = jnp.zeros_like(gn2)
@@ -949,11 +954,12 @@
                 gn2[:, cols] += dg(gub[:, here], wub[cols, :], NT)
             tiles(4, down)
             more(2)
-            @pl.when(j == 2)
-            def _(): tick(jnp.int32(0))
+            @pl.when(lax.rem(j, 2) == 1)
+            def _(): tick(j // 2)
             return carry
         lax.fori_loop(0, 4, block, 0)
         for c in pieces: c.wait()
+        send_odd(jnp.int32(4), n2_t, up_grad(0))
         def rows(r):
             res = resb[r, :]
             centre = jnp.mean(res, axis=-1, keepdims=True)
@@ -987,15 +993,16 @@
             ]
             for c in loads + late: c.start()
             ga[...] = gres[...].astype(BF16)
-            tick(jnp.int32(1))
+            add_even(jnp.int32(4), n2_t, up_grad(0))
+            send_odd(jnp.int32(5), n2_t, up_grad(1))
+            tick(jnp.int32(2))
             loads[0].wait()
             def mixed(cols):
                 do[:, cols] = dg(ga[...], wo[cols, :], NT).astype(BF16)
             tiles(4, mixed)
-            for c in loads[1:4]: c.wait()
+            add_even(jnp.int32(5), n2_t, up_grad(1))
+            for c in loads[1:]: c.wait()
             lane = lax.broadcasted_iota(jnp.int32, (512, 128), 1)
-            def up_grad(m):
-                return gub.at[:, pl.ds(pl.multiple_of(m * 1024, 1024), 1024)]
             def pair(i, carry):
                 at = lambda base: pl.ds(pl.multiple_of(base + i * 128, 128), 128)
                 cols = at(0)
@@ -1027,20 +1034,23 @@
                 m = i // 2
                 @pl.when(lax.rem(i, 2) == 1)
                 def _():
-                    send_odd(4 + m, n2_t, up_grad(m))
-                    tick(2 + m)
+                    @pl.when(m < 2)
+                    def _(): send_odd(6 + m, n2_t, up_grad(2 + m))
+                    @pl.when(m == 2)
+                    def _(): send_odd(jnp.int32(8), att_t, ga)
+                    tick(3 + m)
                 @pl.when(jnp.logical_and(lax.rem(i, 2) == 0, i > 0))
-                def _(): add_even(3 + m, n2_t, up_grad(m - 1))
+                def _():
+                    @pl.when(m < 3)
+                    def _(): add_even(5 + m, n2_t, up_grad(1 + m))
+                    @pl.when(m == 3)
+                    def _(): add_even(jnp.int32(8), att_t, ga)
                 return carry
             lax.fori_loop(0, 8, pair, 0)
             swap = remote(kv, dkv_in, dkv_s, dkv_r, sibling)
             swap.start()
-            add_even(jnp.int32(7), n2_t, up_grad(jnp.int32(3)))
             late[0].wait()
-            loads[4].wait()
-            send_odd(jnp.int32(8), att_t, ga)
-            tick(jnp.int32(6))
-            add_even(jnp.int32(8), att_t, ga)
+            tick(jnp.int32(7))
             send_odd(jnp.int32(9), n1_t, dqkv.at[:, pl.ds(0, 1024)])
             swap.wait()
 
@@ -1066,6 +1076,7 @@
                 gn1[:, pl.ds(pl.multiple_of(i * 256, 256), 256)] = dg(dqkv[...], wq[lax.rem(i, 2)], NT)
                 return carry
             lax.fori_loop(0, 4, back, 0)
+            tick(jnp.int32(8))
             late[1].wait()
             def rows(r):
                 xx = xb[r, :].astype(F32)
@@ -1082,26 +1093,25 @@
                 add(10, dqkv[r, 0:1024].astype(F32)); add(11, dqkv[r, 2048:3072].astype(F32))
             tiles(8, rows, 64)
             given = [
-                Move(p, [xb.at[pl.ds(256 * h + 64 * i, 64)] for h in range(2)],
-                     lambda b, i=i: gin_out.at[b, pl.ds(64 * i, 64)], ms.at[1 + i])
-                for i in range(4)
+                Move(p, [xb.at[pl.ds(256 * h + 32 * i, 32)] for h in range(2)],
+                     lambda b, i=i: gin_out.at[b, pl.ds(32 * i, 32)], ms.at[1 + i])
+                for i in range(8)
             ]
             steps = [
                 remote(sums_ref, sum_in.at[i], ss.at[i], sm.at[i], to)
                 for i, to in enumerate((sibling, over_x, over_y, near_z, far_z))
             ]
             steps[0].start()
-            tick(jnp.int32(7))
             given[0].start()
             for k in (10, 11):
                 right = dqkv.at[:, pl.ds(1024 * (k - 9), 1024)]
                 send_odd(jnp.int32(k), n1_t, right)
-                if k == 10: tick(jnp.int32(8))
+                if k == 10: tick(jnp.int32(9))
                 add_even(jnp.int32(k), n1_t, right)
-                if k == 10: given[1].start()
-            for i in range(7):
-                tick(jnp.int32(9 + i))
-                if i < 2: given[2 + i].start()
+                for m_ in ((given[1], given[2]) if k == 10 else (given[3],)): m_.start()
+            for i in range(6):
+                tick(jnp.int32(10 + i))
+                if i < 4: given[4 + i].start()
                 if i < 5:
                     steps[i].wait()
                     sums_ref[...] += sum_in[i]
@@ -1145,7 +1155,7 @@
             pltpu.VMEM((2, 128, 1024), F32), pltpu.VMEM((512, 2048), BF16), pltpu.VMEM((512, 1024), BF16),
             pltpu.VMEM((512, 1024), F32), pltpu.VMEM((512, 4096), BF16), pltpu.VMEM((1024, 512), BF16),
             dma((n,)), dma((n,)), dma((n, 4)), dma((n, 4)), dma((n, 6)), dma((n, 6)), dma((2,)), dma, dma, dma((12,)),
-            dma((5, 3, 2)), dma((5,)), dma((5,)),
+            dma((9, 3, 2)), dma((5,)), dma((5,)),
         ],
         compiler_params=pltpu.CompilerParams(collective_id=8, has_side_effects=True, vmem_limit_bytes=67043328),
         cost_estimate=pl.CostEstimate(flops=40 * 10**9, bytes_accessed=60 << 20, transcendentals=10**7),

time: 295 us -> 287 us (0.973)
  Pallas kernels: 281 us -> 273 us
    pallas_call x1, Pallas kernels: 161 us -> 153 us  [backward(): pl.pallas_call(bwd_kernel, in_specs=[any_] * len(arrays) + [vmem, vmem],...]
where the time goes in v7:
time: 287 us
  Pallas kernels  273 us (95%)
  local copies, waits for them, and re-layouts  11.3 us (4%)
    pallas_call x1, Pallas kernels, backward(): pl.pallas_call(bwd_kernel, in_specs=[any_] * len(arrays) + [vmem, vmem],...  153 us
    pallas_call x1, Pallas kernels, forward(): pl.pallas_call(fwd_kernel, in_specs=[any_] * 6 + [vmem], out_specs=[hbm]...  120 us
    unnamed x16, local copies, waits for them, and re-layouts  8.63 us

profile of v7, /device:TPU:0, one launch (start us, length us, event | category | flops | bytes accessed | tf_op | source)
XLA Modules:
  0.0 286.8 jit_solution(4322181205981120043)
XLA Ops:
  0.6 1.4 convert_add_fusion.pack
  2.0 120.1 %forward.1 = (bf16[1024,3072]{1,0:T(8,128)(2,1)}, bf16[1024,1024]{1,0:T(8,128)(2,1)}, bf16[1024,4096]{1,0:T(8,128)(2,1)}, bf16[1024,4096]{1,0:T(8,128)(2,1)}, bf...) custom-call(bf16[2,256,1024]{2,1,0:T(8,128)(2,1)} %tok_hbm.1, ...), custom_call_target="tpu_custom_call" | custom-call | flops 20000000000 | bytes 62914560 | tf_op jit(solution)/shard_map/forward/pallas_call | solution.py:757
  122.1 153.4 %backward.1 = (f32[128,4096]{1,0:T(8,128)}, f32[128,4096]{1,0:T(8,128)}, f32[128,1024]{1,0:T(8,128)}, f32[128,3072]{1,0:T(8,128)}, bf16[2,256,1024]{2,1,0:T(8,12...) custom-call(bf16[512,1024]{1,0:T(8,128)(2,1)} %get-tuple-element.40.cot_hbm, ...), custom_call_target="tpu_custom_call" | custom-call | flops 40000000000 | bytes 62914560 | tf_op jit(solution)/shard_map/backward/pallas_call | solution.py:1143
  275.5 1.3 slice_bitcast_fusion
  276.8 1.4 slice_bitcast_fusion.1
  278.2 0.0 copy-start.3
  278.2 0.0 copy-start.2
  278.2 3.0 %copy.30 = f32[4096,128]{1,0:T(8,128)} copy(f32[4096,128]{0,1:T(8,128)} %bitcast.28) | data formatting | bytes 4194304
  281.2 0.0 copy-done.3
  281.2 0.0 copy-start.1
  281.2 1.0 copy.36
  282.2 0.0 copy-done.2
  282.2 1.0 copy.37
  283.1 0.0 copy-done.1
  283.1 0.0 copy-start.4
  283.1 0.0 copy-start
  283.1 1.1 copy.38
  284.3 0.2 copy-done.4
  284.5 0.8 copy.39
  285.3 0.2 copy-done
  285.5 1.3 copy.40
Async XLA Ops:
  278.2 3.0 %copy-start.3 = (bf16[2,256,1024]{2,1,0:T(8,128)(2,1)S(1)}, bf16[2,256,1024]{2,1,0:T(8,128)(2,1)}, u32[]{:S(2)}) copy-start(bf16[2,256,1024]{2,1,0:T(8,128)(2,1)} %get-tuple-element.103) | copy-start | bytes 3145732
  278.2 4.0 %copy-start.2 = (bf16[2,256,1024]{2,1,0:T(8,128)(2,1)S(1)}, bf16[2,256,1024]{2,1,0:T(8,128)(2,1)}, u32[]{:S(2)}) copy-start(bf16[2,256,1024]{2,1,0:T(8,128)(2,1)} %get-tuple-element.104) | copy-start | bytes 3145732
  281.2 1.9 copy-start.1
  283.1 1.4 copy-start.4
  283.1 2.3 copy-start

commit v8 on v7

--- a/solution.py
+++ b/solution.py
@@ -1038,13 +1038,16 @@
                     def _(): send_odd(6 + m, n2_t, up_grad(2 + m))
                     @pl.when(m == 2)
                     def _(): send_odd(jnp.int32(8), att_t, ga)
-                    tick(3 + m)
+                    pass
+                @pl.when(i == 0)
+                def _(): tick(jnp.int32(3))
                 @pl.when(jnp.logical_and(lax.rem(i, 2) == 0, i > 0))
                 def _():
                     @pl.when(m < 3)
                     def _(): add_even(5 + m, n2_t, up_grad(1 + m))
                     @pl.when(m == 3)
                     def _(): add_even(jnp.int32(8), att_t, ga)
+                    tick(3 + m)
                 return carry
             lax.fori_loop(0, 8, pair, 0)
             swap = remote(kv, dkv_in, dkv_s, dkv_r, sibling)

time: 287 us -> 286 us (level)
  no operation moved by 1% of the time
where the time goes in v8:
time: 286 us
  Pallas kernels  273 us (95%)
  local copies, waits for them, and re-layouts  11.3 us (4%)
    pallas_call x1, Pallas kernels, backward(): pl.pallas_call(bwd_kernel, in_specs=[any_] * len(arrays) + [vmem, vmem],...  153 us
    pallas_call x1, Pallas kernels, forward(): pl.pallas_call(fwd_kernel, in_specs=[any_] * 6 + [vmem], out_specs=[hbm]...  120 us
    unnamed x16, local copies, waits for them, and re-layouts  8.63 us

profile of v8, /device:TPU:0, one launch (start us, length us, event | category | flops | bytes accessed | tf_op | source)
XLA Modules:
  0.0 286.0 jit_solution(5379421207389088603)
XLA Ops:
  0.6 1.4 convert_add_fusion.pack
  2.0 120.1 %forward.1 = (bf16[1024,3072]{1,0:T(8,128)(2,1)}, bf16[1024,1024]{1,0:T(8,128)(2,1)}, bf16[1024,4096]{1,0:T(8,128)(2,1)}, bf16[1024,4096]{1,0:T(8,128)(2,1)}, bf...) custom-call(bf16[2,256,1024]{2,1,0:T(8,128)(2,1)} %tok_hbm.1, ...), custom_call_target="tpu_custom_call" | custom-call | flops 20000000000 | bytes 62914560 | tf_op jit(solution)/shard_map/forward/pallas_call | solution.py:757
  122.1 152.5 %backward.1 = (f32[128,4096]{1,0:T(8,128)}, f32[128,4096]{1,0:T(8,128)}, f32[128,1024]{1,0:T(8,128)}, f32[128,3072]{1,0:T(8,128)}, bf16[2,256,1024]{2,1,0:T(8,12...) custom-call(bf16[512,1024]{1,0:T(8,128)(2,1)} %get-tuple-element.40.cot_hbm, ...), custom_call_target="tpu_custom_call" | custom-call | flops 40000000000 | bytes 62914560 | tf_op jit(solution)/shard_map/backward/pallas_call | solution.py:1146
  274.7 1.3 slice_bitcast_fusion
  275.9 1.4 slice_bitcast_fusion.1
  277.3 0.0 copy-start.3
  277.3 0.0 copy-start.2
  277.3 3.0 %copy.30 = f32[4096,128]{1,0:T(8,128)} copy(f32[4096,128]{0,1:T(8,128)} %bitcast.28) | data formatting | bytes 4194304
  280.3 0.0 copy-done.3
  280.3 0.0 copy-start.1
  280.3 1.0 copy.36
  281.3 0.0 copy-done.2
  281.3 1.0 copy.37
  282.3 0.0 copy-done.1
  282.3 0.0 copy-start.4
  282.3 0.0 copy-start
  282.3 1.1 copy.38
  283.4 0.2 copy-done.4
  283.7 0.8 copy.39
  284.5 0.2 copy-done
  284.6 1.3 copy.40
Async XLA Ops:
  277.3 3.0 %copy-start.3 = (bf16[2,256,1024]{2,1,0:T(8,128)(2,1)S(1)}, bf16[2,256,1024]{2,1,0:T(8,128)(2,1)}, u32[]{:S(2)}) copy-start(bf16[2,256,1024]{2,1,0:T(8,128)(2,1)} %get-tuple-element.103) | copy-start | bytes 3145732
  277.3 4.0 %copy-start.2 = (bf16[2,256,1024]{2,1,0:T(8,128)(2,1)S(1)}, bf16[2,256,1024]{2,1,0:T(8,128)(2,1)}, u32[]{:S(2)}) copy-start(bf16[2,256,1024]{2,1,0:T(8,128)(2,1)} %get-tuple-element.104) | copy-start | bytes 3145732
  280.3 1.9 copy-start.1
  282.3 1.4 copy-start.4
  282.3 2.3 copy-start
